TPU v7x, 128 devices: a whole 4x4x4 slice. The times are simulated.
128 devices in a mesh: view: 4 (over z), seg: 32 (over x, y, core).
Axes of the slice: x: 4, y: 4, z: 4, core: 2. Of those that a mesh axis runs over, the one named last changes fastest.
Arguments:
- features: bfloat16 [128, 1369, 1024], P(('view', 'seg')), may hold values from -6 to 6
- block_ids: int32 [128, 32, 2], P(('view', 'seg')), may hold values from 0 to 32, as said below
- patch_rows: int32 [128, 32, 2, 32], P(('view', 'seg')), may hold values from 0 to 1368
- lift_weights: bfloat16 [128, 32, 2, 64, 32], P(('view', 'seg')), may hold values from 0 to 0.5
- coords: int32 [4, 32, 3, 512], P('view', 'seg'), may hold values from 0 to 127, as said below
- w_in: float32 [1024, 768], replicated, may hold values from -0.1875 to 0.1875
- w_query: bfloat16 [768, 768], replicated, may hold values from -1 to 1
- w_key: bfloat16 [768, 768], replicated, may hold values from -1 to 1
- w_value: bfloat16 [768, 768], replicated, may hold values from -0.21875 to 0.21875
- w_out: bfloat16 [768, 768], replicated, may hold values from -0.21875 to 0.21875
- w_up: bfloat16 [768, 3072], replicated, may hold values from -0.21875 to 0.21875
- w_down: bfloat16 [3072, 768], replicated, may hold values from -0.109375 to 0.109375
Outputs:
- encoded: bfloat16 [4, 32, 512, 768], P('view', 'seg')
Inputs may be any that keep to these rules, and one draw needn't show every extreme that they name: In each row block_ids[j, s] the live entries (below 32) come first, are distinct and number 1 to 2; the others equal 32. All rows of one destination segment are full. The value 4 * 8 - 1 never occurs. `coords`: the three coordinates of distinct voxels of a 128-cube; their Morton codes rise strictly with the voxel index.
All inputs are finite; a program needn't handle non-finite values.
Results may differ from a plain program's by a relative error of at most 0.007.
Values may be sent and summed in bfloat16 or wider, within the bound.
No kernel may reach another device: no remote copies, remote signals or barrier semaphores. Data moves between devices by JAX's collectives and lax.ppermute only.
A program may use at most 128 MiB of HBM per device.

v0:
```python
import math

import jax
import jax.numpy as jnp
from jax import lax
from jax.sharding import PartitionSpec as P

HEAD_DIM = 64


def padded(shard, sides, width):
    for axis, dim in sides:
        count, length = (lax.axis_size(axis), shard.shape[dim])
        up = [(i, (i + 1) % count) for i in range(count)]
        down = [(j, i) for i, j in up]
        last = lax.slice_in_dim(shard, length - width, length, axis=dim)
        leading = lax.slice_in_dim(shard, 0, width, axis=dim)
        before = lax.ppermute(last, axis, up)
        after = lax.ppermute(leading, axis, down)
        shard = jnp.concatenate([before, shard, after], axis=dim)
    return shard


def normalize(values):
    average = jnp.mean(values, axis=-1, keepdims=True)
    centred = values - average
    spread = jnp.mean(centred * centred, axis=-1, keepdims=True)
    return (centred * lax.rsqrt(spread + 1e-05)).astype(jnp.bfloat16)


def position_code(places, model_width):
    freq_count = model_width // 6
    frequency = jnp.exp(-math.log(10000.0) * jnp.arange(freq_count, dtype=jnp.float32) / freq_count)
    angles = places.astype(jnp.float32)[:, :, None] * frequency
    pieces = jnp.concatenate([jnp.sin(angles), jnp.cos(angles)], axis=-1)
    return jnp.transpose(pieces, (1, 0, 2)).reshape(places.shape[1], model_width)


def lift_blocks(weights, patches):
    return jnp.einsum(
        "sabk,sakc->sabc", weights, patches, preferred_element_type=jnp.float32
    ).astype(jnp.bfloat16)


def shards(
    features,
    block_ids,
    patch_rows,
    lift_weights,
    coords,
    w_in,
    w_query,
    w_key,
    w_value,
    w_out,
    w_up,
    w_down,
):
    view_table = features[0]
    rows_here = coords.shape[-1]
    block_size = lift_weights.shape[-2]
    model_width = w_in.shape[1]
    channel_count = view_table.shape[1]
    quarter_blocks = rows_here // block_size
    segment_blocks = lax.axis_size("view") * quarter_blocks
    patch_picks = patch_rows[0]
    patches = jnp.take(view_table, patch_picks.reshape(-1), axis=0).reshape(
        patch_picks.shape + (channel_count,)
    )
    weights = lift_weights[0]
    block_marks = block_ids[0].astype(jnp.bfloat16)
    lifted, received_ids = (
        lax.all_to_all(
            lift_blocks(weights, patches), "seg", split_axis=0, concat_axis=0, tiled=True
        ),
        lax.all_to_all(block_marks, "seg", split_axis=0, concat_axis=0, tiled=True),
    )
    slot_count = lifted.shape[0] * lifted.shape[1]
    chosen = received_ids.reshape(slot_count).astype(jnp.float32)
    onehot = jnp.arange(segment_blocks, dtype=jnp.float32)[:, None] == chosen[None, :]
    counts = jnp.sum(onehot.astype(jnp.float32), axis=1)
    dense_rows = jnp.einsum(
        "bm,mrc->brc",
        onehot.astype(jnp.bfloat16),
        lifted.reshape(slot_count, block_size, channel_count),
        preferred_element_type=jnp.float32,
    )
    dense_rows = dense_rows.reshape(segment_blocks * block_size, channel_count)
    own_sums, totals = (
        lax.psum_scatter(dense_rows, "view", scatter_dimension=0, tiled=True),
        lax.psum_scatter(counts, "view", scatter_dimension=0, tiled=True),
    )
    summed = jnp.dot(
        own_sums, w_in, precision=lax.Precision.HIGHEST, preferred_element_type=jnp.float32
    )
    averaged = (
        summed.reshape(quarter_blocks, block_size, model_width)
        / jnp.maximum(totals, 1.0)[:, None, None]
    )
    stream = averaged.reshape(rows_here, model_width) + position_code(coords[0, 0], model_width)
    normed = normalize(stream)
    query = jnp.dot(normed, w_query, preferred_element_type=jnp.float32).astype(jnp.bfloat16)
    keys = jnp.dot(normed, w_key, preferred_element_type=jnp.float32).astype(jnp.bfloat16)
    values = jnp.dot(normed, w_value, preferred_element_type=jnp.float32).astype(jnp.bfloat16)
    key_value = jnp.concatenate([keys, values], axis=1)
    half = block_size // 2
    extended = padded(key_value, ((("view", "seg"), 0),), half)
    head_count = model_width // HEAD_DIM
    window_count = (rows_here + block_size) // block_size
    padded_query = jnp.pad(query, ((half, half), (0, 0)))
    query_win = padded_query.reshape(window_count, block_size, head_count, HEAD_DIM)
    key_win = extended[:, :model_width].reshape(window_count, block_size, head_count, HEAD_DIM)
    value_win = extended[:, model_width:].reshape(window_count, block_size, head_count, HEAD_DIM)
    scores = jnp.einsum(
        "wqhd,wkhd->whqk", query_win, key_win, preferred_element_type=jnp.float32
    ) / math.sqrt(HEAD_DIM)
    scores = scores - jnp.max(scores, axis=-1, keepdims=True)
    weights_exp = jnp.exp(scores)
    probs = (weights_exp / jnp.sum(weights_exp, axis=-1, keepdims=True)).astype(jnp.bfloat16)
    mixed = jnp.einsum(
        "whqk,wkhd->wqhd", probs, value_win, preferred_element_type=jnp.float32
    ).astype(jnp.bfloat16)
    mixed = mixed.reshape(rows_here + block_size, model_width)[half : half + rows_here]
    attended = stream + jnp.dot(mixed, w_out, preferred_element_type=jnp.float32)
    normed_two = normalize(attended)
    hidden = jax.nn.gelu(
        jnp.dot(normed_two, w_up, preferred_element_type=jnp.float32), approximate=True
    ).astype(jnp.bfloat16)
    encoded = attended + jnp.dot(hidden, w_down, preferred_element_type=jnp.float32)
    return encoded.astype(jnp.bfloat16).reshape(1, 1, rows_here, model_width)


def solution(mesh):
    in_specs = (
        P(("view", "seg"), None, None),
        P(("view", "seg"), None, None),
        P(("view", "seg"), None, None, None),
        P(("view", "seg"), None, None, None, None),
        P("view", "seg", None, None),
        P(),
        P(),
        P(),
        P(),
        P(),
        P(),
        P(),
    )
    out_specs = P("view", "seg", None, None)
    return jax.shard_map(shards, mesh=mesh, in_specs=in_specs, out_specs=out_specs, check_vma=False)
```

profile of v0, /device:TPU:0, one launch (start us, length us, event | category | flops | bytes accessed | tf_op | source)
XLA Modules:
  0.0 342.0 jit_solution(6856836436526939963)
XLA Ops:
  6.5 0.8 convert_bitcast_fusion.2
  7.4 0.7 copy.29
  8.1 7.4 %all-to-all-start = ((bf16[32,1,2]{2,1,0:T(2,128)(2,1)}), bf16[32,1,2]{2,1,0:T(2,128)(2,1)S(1)}, u32[]{:S(2)}, u32[]{:S(2)}) async-start(bf16[32,1,2]{2,1,0:T(2,128)(2,1)} %copy.29), calls=%async_computation | async-start | bytes 32768 | tf_op jit(solution)/shard_map/all_to_all | solution.py:76
  15.5 0.9 reshape_squeeze.6
  16.4 0.8 compare_and_fusion
  17.2 13.2 %gather_fusion = bf16[2048,1024]{1,0:T(8,128)(2,1)} fusion(bf16[1369,1024]{1,0:T(8,128)(2,1)} %bitcast.39, s32[2048]{0:T(1024)S(1)} %broadcast_clamp_fusion), kind=kCustom, calls=%fused_computation | custom fusion | bytes 8396800 | tf_op jit(solution)/shard_map/jit(_take)/gather | solution.py:67
  30.4 7.9 %convert_bitcast_fusion = bf16[32,2,64,1024]{3,2,1,0:T(8,128)(2,1)} fusion(bf16[32,2,32,1024]{3,2,1,0:T(8,128)(2,1)} %bitcast.41, pred[32,2,32]{2,1,0:T(4,128)(4,1)S(1)} %compare_and_fusion, bf16[1,32,2,64,32]{3,4,2,1,0:T(8,128)(2,1)} %param.15), kind=kOutput, calls=%fused_computation.5 | convolution fusion | flops 274726912 | bytes 12847104 | tf_op jit(solution)/shard_map/sabk,sakc->sabc/dot_general | solution.py:40
  38.3 7.5 %all-to-all-start.1 = ((bf16[32,2,64,1024]{3,2,1,0:T(8,128)(2,1)}), bf16[32,2,64,1024]{3,2,1,0:T(8,128)(2,1)}, u32[]{:S(2)}, u32[]{:S(2)}) async-start(bf16[32,2,64,1024]{3,2,1,0:T(8,128)(2,1)} %convert_bitcast_fusion), calls=%async_computation.1 | async-start | bytes 16777216 | tf_op jit(solution)/shard_map/all_to_all | solution.py:73
  45.8 0.5 reduce-scatter.2.cloned.1.call-start
  46.4 0.1 reshape.136
  46.5 112.8 %all-to-all-done.1 = bf16[32,2,64,1024]{3,2,1,0:T(8,128)(2,1)} async-done(((bf16[32,2,64,1024]{3,2,1,0:T(8,128)(2,1)}), bf16[32,2,64,1024]{3,2,1,0:T(8,128)(2,1)}, u32[]{:S(2)}, u32[]{:S(2)}) %all-to-all-start.1) | async-done | bytes 8388640 | tf_op jit(solution)/shard_map/all_to_all | solution.py:73
  159.3 13.4 %fusion.1 = f32[32,64,1024]{2,0,1:T(8,128)S(1)} fusion(bf16[64,64,1024]{2,1,0:T(8,128)(2,1)} %bitcast.8, f32[64]{0:T(128)S(1)} %reshape.136), kind=kOutput, calls=%fused_computation.3 | convolution fusion | flops 268437504 | bytes 16777472 | tf_op jit(solution)/shard_map/bm,mrc->brc/dot_general | solution.py:82
  172.7 8.2 %copy.31 = f32[32,64,1024]{2,1,0:T(8,128)} copy(f32[32,64,1024]{2,0,1:T(8,128)S(1)} %fusion.1) | data formatting | bytes 16777216 | tf_op jit(solution)/shard_map/bm,mrc->brc/dot_general | solution.py:82
  181.0 0.7 copy-done.7
  181.7 2.8 multiply_sine_fusion
  184.5 1.4 pad_maximum_fusion.1
  185.8 3.0 copy.32
  188.9 0.6 dynamic-slice
  190.1 0.1 convert_reduce_fusion.1
  190.2 11.8 %all-reduce.1 = f32[32]{0:T(128)S(1)} all-reduce(f32[32]{0:T(128)S(1)} %convert_reduce_fusion.1), channel_id=3, replica_groups=mesh['view'=4,'seg'=32] {'view'}, use_global_device_ids=true, to_apply=%region_2.3.clone | all-reduce | flops 32 | bytes 256
  202.0 0.1 dynamic-slice_maximum_fusion
  202.1 0.1 div.46
  202.2 68.8 %reduce-scatter.2.cloned.1.call-done = f32[512,1024]{1,0:T(8,128)} async-done(((f32[2048,1024]{1,0:T(8,128)}), f32[512,1024]{1,0:T(8,128)}) %reduce-scatter.2.cloned.1.call-update) | async-done | bytes 2097168 | tf_op jit(solution)/shard_map/reduce_scatter | solution.py:90
  271.0 7.5 %fusion.50 = (f32[512]{0:T(512)S(1)}, f32[512,768]{1,0:T(8,128)S(1)}) fusion(f32[512,768]{1,0:T(8,128)} %copy.32, f32[512]{0:T(512)S(1)} %div.46, f32[512,1024]{1,0:T(8,128)} %reduce-scatter.2.cloned.1.call-done, f32[1024,768]{1,0:T(8,128)S(1)} %copy-done), kind=kOutput, calls=%fused_computation.76 | convolution fusion | flops 4833017344 | bytes 8392704 | tf_op jit(solution)/shard_map/dot_general | solution.py:93
  278.5 0.3 multiply_reduce_fusion.2
  278.8 0.2 multiply_convert_fusion.1
  279.0 1.3 copy-done.8
  280.3 0.8 convolution_convert_fusion.1
  281.1 0.5 copy-done.9
  281.6 0.8 convolution_convert_fusion.2
  282.4 0.1 collective-permute-start
  282.5 7.4 %collective-permute-start.1 = (bf16[32,1536]{1,0:T(8,128)(2,1)S(1)}, bf16[32,1536]{1,0:T(8,128)(2,1)S(1)}, u32[]{:S(2)}, u32[]{:S(2)}) collective-permute-start(bf16[32,1536]{1,0:T(8,128)(2,1)S(1)} %get-tuple-element.8), channel_id=1, source_target_pairs={{1,0},{2,1},{3,2},{4,3},{5,4},{6,5},{7,6},{8,7},{9,8},{10,9},{11,1... | collective-permute-start | bytes 294920 | tf_op jit(solution)/shard_map/ppermute | solution.py:19
  289.8 0.8 convolution_convert_fusion
  290.6 1.0 pad.4
  291.6 2.9 reshape.132
  294.5 1.3 pad_maximum_fusion
  295.8 1.3 fusion.49
  297.1 4.0 %reshape.133 = bf16[9,64,12,64]{3,2,1,0:T(8,128)(2,1)} reshape(bf16[576,768]{1,0:T(8,128)(2,1)} %get-tuple-element.6) | data formatting | bytes 1769472 | tf_op jit(solution)/shard_map/reshape | solution.py:112
  301.1 2.7 fusion.21
  303.8 2.7 fusion.51
  306.5 2.7 reshape.131
  309.3 3.6 %convert_bitcast_fusion.1 = bf16[9,64,12,64]{1,3,2,0:T(8,128)(2,1)S(1)} fusion(f32[9,12,64,64]{2,3,1,0:T(8,128)} %get-tuple-element.14, f32[9,12,64]{2,1,0:T(8,128)S(1)} %get-tuple-element.13, bf16[9,64,12,64]{3,2,1,0:T(8,128)(2,1)} %reshape.131), kind=kOutput, calls=%fused_computation.28 | convolution fusion | flops 57950208 | bytes 3566592 | tf_op jit(solution)/shard_map/whqk,wkhd->wqhd/dot_general | solution.py:120
  312.8 3.0 copy.37
  315.8 4.2 %reshape.134 = bf16[576,768]{1,0:T(8,128)(2,1)} reshape(bf16[9,64,12,64]{3,2,1,0:T(8,128)(2,1)} %copy.37) | data formatting | bytes 1769472 | tf_op jit(solution)/shard_map/reshape | solution.py:123
  320.0 2.4 fusion.52
  322.4 1.1 copy-done.4
  323.6 0.3 multiply_reduce_fusion.1
  323.9 11.0 %fusion.30 = bf16[1,1,512,768]{3,2,1,0:T(8,128)(2,1)} fusion(f32[512,768]{1,0:T(8,128)} %copy-done.4, bf16[3072,768]{1,0:T(8,128)(2,1)} %param.23, bf16[768,3072]{1,0:T(8,128)(2,1)} %param.22, f32[512]{0:T(512)S(1)} %add_rsqrt_fusion, f32[512]{0:T(512)S(1)} %broadcast_multiply_fusion), kind=kOutput, calls=%fused_computation.42 | convolution fusion | flops 4847960064 | bytes 11800576 | tf_op jit(solution)/shard_map/dot_general | solution.py:129
  (36 shorter events, 0.3 us)
Async XLA Ops:
  6.5 264.5 %copy-start = (f32[1024,768]{1,0:T(8,128)S(1)}, f32[1024,768]{1,0:T(8,128)}, u32[]{:S(2)}) copy-start(f32[1024,768]{1,0:T(8,128)} %param.17) | copy-start | bytes 9437188
  8.1 30.2 %all-to-all-start = ((bf16[32,1,2]{2,1,0:T(2,128)(2,1)}), bf16[32,1,2]{2,1,0:T(2,128)(2,1)S(1)}, u32[]{:S(2)}, u32[]{:S(2)}) async-start(bf16[32,1,2]{2,1,0:T(2,128)(2,1)} %copy.29), calls=%async_computation | async-start | bytes 32768 | tf_op jit(solution)/shard_map/all_to_all | solution.py:76
  38.3 121.0 %all-to-all-start.1 = ((bf16[32,2,64,1024]{3,2,1,0:T(8,128)(2,1)}), bf16[32,2,64,1024]{3,2,1,0:T(8,128)(2,1)}, u32[]{:S(2)}, u32[]{:S(2)}) async-start(bf16[32,2,64,1024]{3,2,1,0:T(8,128)(2,1)} %convert_bitcast_fusion), calls=%async_computation.1 | async-start | bytes 16777216 | tf_op jit(solution)/shard_map/all_to_all | solution.py:73
  45.8 225.2 %reduce-scatter.2.cloned.1.call-start = ((), (), s32[]{:S(2)}) async-start(), calls=%async_computation.3 | async-start | bytes 10485760 | tf_op jit(solution)/shard_map/reduce_scatter | solution.py:90
  181.0 0.7 copy-start.7
  185.8 3.0 copy-start.11
  278.4 2.6 copy-start.2
  278.4 1.8 copy-start.8
  280.3 1.3 copy-start.9
  281.6 8.3 %copy-start.10 = (bf16[768,768]{1,0:T(8,128)(2,1)S(1)}, bf16[768,768]{1,0:T(8,128)(2,1)}, u32[]{:S(2)}) copy-start(bf16[768,768]{1,0:T(8,128)(2,1)} %param.18) | copy-start | bytes 3538948
  282.3 8.3 %copy-start.6 = (bf16[512,768]{1,0:T(8,128)(2,1)}, bf16[512,768]{1,0:T(8,128)(2,1)S(1)}, u32[]{:S(2)}) copy-start(bf16[512,768]{1,0:T(8,128)(2,1)S(1)} %convolution_convert_fusion.2) | copy-start | bytes 2359300
  282.4 12.1 %collective-permute-start = (bf16[32,1536]{1,0:T(8,128)(2,1)S(1)}, bf16[32,1536]{1,0:T(8,128)(2,1)S(1)}, u32[]{:S(2)}, u32[]{:S(2)}) collective-permute-start(bf16[32,1536]{1,0:T(8,128)(2,1)S(1)} %get-tuple-element.7), channel_id=1, source_target_pairs={{0,1},{1,2},{2,3},{3,4},{4,5},{5,6},{6,7},{7,8},{8,9},{9,10},{10,1... | collective-permute-start | bytes 294920 | tf_op jit(solution)/shard_map/ppermute | solution.py:18
  282.5 12.0 %collective-permute-start.1 = (bf16[32,1536]{1,0:T(8,128)(2,1)S(1)}, bf16[32,1536]{1,0:T(8,128)(2,1)S(1)}, u32[]{:S(2)}, u32[]{:S(2)}) collective-permute-start(bf16[32,1536]{1,0:T(8,128)(2,1)S(1)} %get-tuple-element.8), channel_id=1, source_target_pairs={{1,0},{2,1},{3,2},{4,3},{5,4},{6,5},{7,6},{8,7},{9,8},{10,9},{11,1... | collective-permute-start | bytes 294920 | tf_op jit(solution)/shard_map/ppermute | solution.py:19
  303.8 2.8 copy-start.5
  315.8 4.2 %copy-start.3 = (f32[512,768]{1,0:T(8,128)S(1)}, f32[512,768]{1,0:T(8,128)}, u32[]{:S(2)}) copy-start(f32[512,768]{1,0:T(8,128)} %copy-done.2) | copy-start | bytes 4718596
  322.4 1.2 copy-start.4
  323.9 11.0 %copy-start.1 = (f32[1024,768]{1,0:T(8,128)S(1)}, f32[1024,768]{1,0:T(8,128)}, u32[]{:S(2)}) copy-start(f32[1024,768]{1,0:T(8,128)} %param.17) | copy-start | bytes 9437188
Sparse Core Ops, SparseCore 0:
  181.1 89.8 reduce-scatter.1
where the time goes:
time: 347 us; the launch traced here: 342 us
  waiting for transfers between devices  182 us (52%)
  matrix products  50.7 us (15%)
  local copies, waits for them, and re-layouts  49.5 us (14%)
  starting transfers between devices  22.9 us (7%)
  between operations  14.5 us (4%)
  blocking collectives  11.8 us (3%)
  other arithmetic  10.9 us (3%)
    all_to_all x1, waiting for transfers between devices, shards(): lax.all_to_all(lift_blocks(weights, patches), 'seg', split_axis=0, concat...  113 us
    reduce_scatter x1, waiting for transfers between devices, shards(): lax.psum_scatter(dense_rows, 'view', scatter_dimension=0, tiled=True)  68.8 us
    dot_general x1, matrix products, shards(): jnp.einsum('bm,mrc->brc', onehot.astype(jnp.bfloat16), lifted.reshape(slo...  13.4 us
    gather x1, local copies, waits for them, and re-layouts, shards(): jnp.take(view_table, patch_picks.reshape(-1), axis=0)  13.2 us
    unnamed x1, blocking collectives  11.8 us
    dot_general x1, matrix products, shards(): jnp.dot(hidden, w_down, preferred_element_type=jnp.float32)  11 us
    dot_general x1, local copies, waits for them, and re-layouts, shards(): jnp.einsum('bm,mrc->brc', onehot.astype(jnp.bfloat16), lifted.reshape(slo...  8.25 us
    dot_general x1, matrix products, lift_blocks(): jnp.einsum('sabk,sakc->sabc', weights, patches, preferred_element_type=jn...  7.91 us
  transfers between devices with their start and end apart: 5, of which 2 were waited for; matrix products, arithmetic and copies ran while one was open for 10% of the time, Pallas kernels for 0%

commit v1 on v0

v1 whole, which is shorter than its diff:
```python
import functools
import math

import jax
import jax.numpy as jnp
from jax import lax
from jax.experimental import pallas as pl
from jax.experimental.pallas import tpu as pltpu
from jax.sharding import PartitionSpec as P

HEAD_DIM = 64
F32 = jnp.float32
BF16 = jnp.bfloat16
EXTRA = 8
VMEM_LIMIT = 60 * 1024 * 1024
VM = pl.BlockSpec(memory_space=pltpu.VMEM)
ANY = pl.BlockSpec(memory_space=pl.ANY)


def params(**kw):
    return pltpu.CompilerParams(vmem_limit_bytes=VMEM_LIMIT, **kw)


def dot(a, b):
    return lax.dot_general(a, b, (((1,), (0,)), ((), ())), preferred_element_type=F32)


def pack_kernel(patches, per_step, feat_ref, win_ref, idx_ref, extra_ref, out_ref, table):
    table_rows, width = table.shape
    full = (patches // 256) * 256

    @pl.when(pl.program_id(0) == 0)
    def _():
        table[full:, :] = jnp.zeros((table_rows - full, width), BF16)
        high = win_ref[...].astype(BF16)
        low = (win_ref[...] - high.astype(F32)).astype(BF16)
        for start in range(0, patches, 256):
            rows = feat_ref[start : min(start + 256, patches), :]
            table[start : start + rows.shape[0], :] = (dot(rows, high) + dot(rows, low)).astype(BF16)

    count = idx_ref.shape[0]
    picked = lax.broadcasted_iota(jnp.int32, (count, table_rows), 1) == idx_ref[...]
    rows = dot(picked.astype(F32).astype(BF16), table[...]).astype(BF16)
    each = count // per_step
    for i in range(per_step):
        out_ref[i, :each, :] = rows[i * each : (i + 1) * each, :]
        out_ref[i, each:, :] = extra_ref[i]


def pack(features, w_in, indices, extra):
    patches, channels = features.shape
    width = w_in.shape[1]
    segments = extra.shape[0]
    each = indices.shape[0] // segments
    per_step = 4
    table_rows = -(-patches // 128) * 128
    return pl.pallas_call(
        functools.partial(pack_kernel, patches, per_step),
        grid=(segments // per_step,),
        in_specs=[
            pl.BlockSpec((patches, channels), lambda i: (0, 0)),
            pl.BlockSpec((channels, width), lambda i: (0, 0)),
            pl.BlockSpec((per_step * each, 1), lambda i: (i, 0)),
            pl.BlockSpec((per_step, EXTRA, width), lambda i: (i, 0, 0)),
        ],
        out_specs=pl.BlockSpec((per_step, each + EXTRA, width), lambda i: (i, 0, 0)),
        out_shape=jax.ShapeDtypeStruct((segments, each + EXTRA, width), BF16),
        scratch_shapes=[pltpu.VMEM((table_rows, width), BF16)],
        compiler_params=params(),
        name="pack",
    )(features, w_in, indices, extra)


def gather_sums_kernel(slots_per, block, picks, place_ref, count_ref, recv_ref, *rest):
    outs, total = rest[:-1], rest[-1]
    total[...] = jnp.zeros_like(total)
    views = recv_ref.shape[0]
    width = recv_ref.shape[2]

    def add_view(j, carry):
        weights = recv_ref[j, slots_per * picks :, :].astype(F32)
        weights = jnp.concatenate(
            [weights[:, g * 128 : (g + 1) * 128] for g in range(picks // EXTRA)], axis=0
        ).astype(BF16)
        for c in range(slots_per):
            rows = recv_ref[j, c * picks : (c + 1) * picks, :]
            lifted = lax.dot_general(
                weights[:, c * block : (c + 1) * block],
                rows,
                (((0,), (0,)), ((), ())),
                preferred_element_type=F32,
            )
            start = pl.multiple_of(place_ref[j * slots_per + c], 8)
            total[pl.ds(start, block), :] += lifted
            mark = count_ref[j * slots_per + c]
            total[pl.ds(mark, 1), :] += jnp.ones((1, width), F32)
        return carry

    lax.fori_loop(0, views, add_view, 0)
    size = outs[0].shape[0]
    for i, out in enumerate(outs):
        out[...] = total[i * size : (i + 1) * size, :].astype(BF16)


def gather_sums(place, count, recv, slots_per, block, picks, half_blocks, parts):
    size = half_blocks * block + 8
    width = recv.shape[2]
    return pl.pallas_call(
        functools.partial(gather_sums_kernel, slots_per, block, picks),
        grid_spec=pltpu.PrefetchScalarGridSpec(
            num_scalar_prefetch=2,
            grid=(1,),
            in_specs=[pl.BlockSpec(recv.shape, lambda i, a, b: (0, 0, 0))],
            out_specs=[pl.BlockSpec((size, width), lambda i, a, b: (0, 0))] * parts,
            scratch_shapes=[pltpu.VMEM((parts * size + block + 8, width), F32)],
        ),
        out_shape=[jax.ShapeDtypeStruct((size, width), BF16)] * parts,
        compiler_params=params(dimension_semantics=("arbitrary",)),
        name="gather_sums",
    )(place, count, recv)


def normalize(values):
    average = jnp.mean(values, axis=-1, keepdims=True)
    centred = values - average
    spread = jnp.mean(centred * centred, axis=-1, keepdims=True)
    return (centred * lax.rsqrt(spread + 1e-05)).astype(BF16)


def project_kernel(block, half_blocks, *refs):
    sums = (refs[0:3], refs[3:6])
    pos_ref, wq_ref, wk_ref, wv_ref, stream_ref, q_ref, k_ref, v_ref = refs[6:]
    half_rows = half_blocks * block
    for h in range(2):
        base = h * half_rows

        def load(lo, hi):
            a, b, c = sums[h]
            return a[lo:hi, :].astype(F32) + b[lo:hi, :].astype(F32) + c[lo:hi, :].astype(F32)

        tally = jnp.maximum(load(half_rows, half_rows + 8), 1.0)
        for i in range(half_blocks):
            lo = i * block
            averaged = load(lo, lo + block) / tally[i : i + 1, :]
            stream_ref[base + lo : base + lo + block, :] = (
                averaged + pos_ref[base + lo : base + lo + block, :]
            )
        normed = normalize(stream_ref[base : base + half_rows, :])
        for w_ref, o_ref in ((wk_ref, k_ref), (wv_ref, v_ref), (wq_ref, q_ref)):
            o_ref[base : base + half_rows, :] = dot(normed, w_ref[...]).astype(BF16)


def project(sums, pos, w_query, w_key, w_value, block, half_blocks):
    rows, width = pos.shape
    return pl.pallas_call(
        functools.partial(project_kernel, block, half_blocks),
        in_specs=[VM] * 10,
        out_specs=[VM] * 4,
        out_shape=[jax.ShapeDtypeStruct((rows, width), F32)]
        + [jax.ShapeDtypeStruct((rows, width), BF16)] * 3,
        compiler_params=params(),
        name="project",
    )(*sums, pos, w_query, w_key, w_value)


def attend_kernel(
    block, stream_ref, q_ref, k_ref, v_ref, before_ref, after_ref, wout_ref, wup_hbm, wdown_hbm,
    out_ref, qx, kx, vx, mixed, attended, normed, total, wup, wdown, sems,
):
    rows, width = stream_ref.shape
    half = block // 2
    hidden_width = wup.shape[1]
    copies = [
        pltpu.make_async_copy(wup_hbm, wup, sems.at[0]),
        pltpu.make_async_copy(wdown_hbm, wdown, sems.at[1]),
    ]
    for c in copies:
        c.start()
    qx[:half, :] = jnp.zeros((half, width), BF16)
    qx[half : half + rows, :] = q_ref[...]
    qx[half + rows :, :] = jnp.zeros((half, width), BF16)
    for x, own, lane in ((kx, k_ref, 0), (vx, v_ref, width)):
        x[:half, :] = before_ref[:, lane : lane + width]
        x[half : half + rows, :] = own[...]
        x[half + rows :, :] = after_ref[:, lane : lane + width]
    low_lanes = lax.broadcasted_iota(jnp.int32, (block, 128), 1) < HEAD_DIM

    def window(w, carry):
        span = pl.ds(pl.multiple_of(w * block, block), block)
        for pair in range(width // 128):
            lanes = slice(pair * 128, (pair + 1) * 128)
            q, k, v = qx[span, lanes], kx[span, lanes], vx[span, lanes]
            zero = jnp.zeros_like(q)
            both = jnp.concatenate(
                [jnp.where(low_lanes, q, zero), jnp.where(low_lanes, zero, q)], axis=0
            )
            scores = lax.dot_general(
                both, k, (((1,), (1,)), ((), ())), preferred_element_type=F32
            ) * (1.0 / math.sqrt(HEAD_DIM))
            weights = jnp.exp(scores - jnp.max(scores, axis=-1, keepdims=True))
            probs = (weights / jnp.sum(weights, axis=-1, keepdims=True)).astype(BF16)
            out = dot(probs, v)
            mixed[span, lanes] = jnp.where(low_lanes, out[:block], out[block:]).astype(BF16)
        return carry

    lax.fori_loop(0, (rows + block) // block, window, 0)

    step = 256
    for start in range(0, rows, step):
        values = stream_ref[start : start + step, :] + dot(
            mixed[half + start : half + start + step, :], wout_ref[...]
        )
        attended[start : start + step, :] = values
        normed[start : start + step, :] = normalize(values)
    total[...] = attended[...]
    for c in copies:
        c.wait()
    chunk = 512

    def feed(i, carry):
        cols = pl.ds(pl.multiple_of(i * chunk, chunk), chunk)
        hidden = jax.nn.gelu(dot(normed[...], wup[:, cols]), approximate=True).astype(BF16)
        total[...] += dot(hidden, wdown[cols, :])
        return carry

    lax.fori_loop(0, hidden_width // chunk, feed, 0)
    out_ref[...] = total[...].astype(BF16)


def attend(stream, query, keys, values, before, after, w_out, w_up, w_down, block):
    rows, width = stream.shape
    hidden_width = w_up.shape[1]
    return pl.pallas_call(
        functools.partial(attend_kernel, block),
        in_specs=[VM] * 7 + [ANY] * 2,
        out_specs=VM,
        out_shape=jax.ShapeDtypeStruct((rows, width), BF16),
        scratch_shapes=[pltpu.VMEM((rows + block, width), BF16)] * 4
        + [
            pltpu.VMEM((rows, width), F32),
            pltpu.VMEM((rows, width), BF16),
            pltpu.VMEM((rows, width), F32),
            pltpu.VMEM((width, hidden_width), BF16),
            pltpu.VMEM((hidden_width, width), BF16),
            pltpu.SemaphoreType.DMA((2,)),
        ],
        compiler_params=params(),
        name="attend",
    )(stream, query, keys, values, before, after, w_out, w_up, w_down)


def position_code(places, model_width):
    freq_count = model_width // 6
    frequency = jnp.exp(-math.log(10000.0) * jnp.arange(freq_count, dtype=F32) / freq_count)
    columns = places.astype(F32).T
    pieces = []
    for a in range(3):
        angles = columns[:, a : a + 1] * frequency[None, :]
        pieces += [jnp.sin(angles), jnp.cos(angles)]
    return jnp.concatenate(pieces, axis=-1)


def shards(
    features, block_ids, patch_rows, lift_weights, coords, w_in,
    w_query, w_key, w_value, w_out, w_up, w_down,
):
    view_count, segments = lax.axis_size("view"), lax.axis_size("seg")
    rows_here = coords.shape[-1]
    _, _, slots, block, picks = lift_weights.shape
    width = w_in.shape[1]
    quarter = rows_here // block
    empty = view_count * quarter

    weights = jnp.transpose(lift_weights[0], (0, 3, 1, 2)).reshape(
        segments, picks // EXTRA, EXTRA, slots * block
    )
    weights = jnp.transpose(weights, (0, 2, 1, 3)).reshape(segments, EXTRA, -1)
    marks = jnp.broadcast_to(
        jnp.pad(block_ids[0].astype(BF16), ((0, 0), (0, 128 - slots)))[:, None, :],
        (segments, EXTRA, 128),
    )
    extra = jnp.concatenate([weights, marks], axis=-1)
    extra = jnp.pad(extra, ((0, 0), (0, 0), (0, width - extra.shape[-1])))
    payload = pack(features[0], w_in, patch_rows[0].reshape(-1, 1), extra)
    received = lax.all_to_all(payload, "seg", split_axis=0, concat_axis=0, tiled=True)

    pos = position_code(coords[0, 0], width)

    me = lax.axis_index("view")
    lane = slots * block * (picks // EXTRA)
    ids = received[:, slots * picks, lane : lane + slots].astype(jnp.int32).reshape(-1)
    half_blocks = quarter // 2
    size = half_blocks * block + 8
    parts = 2 * view_count
    within = ids % quarter
    part = ((ids // quarter - me) % view_count) * 2 + within // half_blocks
    place = jnp.where(
        ids == empty, parts * size, part * size + (within % half_blocks) * block
    ).astype(jnp.int32)
    count = jnp.where(
        ids == empty, parts * size + block, part * size + half_blocks * block + within % half_blocks
    ).astype(jnp.int32)
    own0, own1, up0, up1, far0, far1, down0, down1 = gather_sums(
        place, count, received, slots, block, picks, half_blocks, parts
    )
    up = [(i, (i + 1) % view_count) for i in range(view_count)]
    down = [(j, i) for i, j in up]

    def join(a, b):
        return (a.astype(F32) + b.astype(F32)).astype(BF16)

    far_up = lax.ppermute(far0, "view", up)
    far_down = lax.ppermute(far1, "view", down)
    near_up1 = lax.ppermute(up1, "view", up)
    near_down0 = lax.ppermute(down0, "view", down)
    near_up0 = lax.ppermute(join(up0, far_up), "view", up)
    near_down1 = lax.ppermute(join(down1, far_down), "view", down)

    stream, query, keys, values = project(
        (own0, near_down0, near_up0, own1, near_up1, near_down1),
        pos, w_query, w_key, w_value, block, half_blocks,
    )
    half = block // 2
    device_count = view_count * segments
    ring_up = [(i, (i + 1) % device_count) for i in range(device_count)]
    ring_down = [(j, i) for i, j in ring_up]
    last = jnp.concatenate([keys[rows_here - half :], values[rows_here - half :]], axis=1)
    first = jnp.concatenate([keys[:half], values[:half]], axis=1)
    before = lax.ppermute(last, ("view", "seg"), ring_up)
    after = lax.ppermute(first, ("view", "seg"), ring_down)
    encoded = attend(stream, query, keys, values, before, after, w_out, w_up, w_down, block)
    return encoded.reshape(1, 1, rows_here, width)


def solution(mesh):
    in_specs = (
        P(("view", "seg"), None, None),
        P(("view", "seg"), None, None),
        P(("view", "seg"), None, None, None),
        P(("view", "seg"), None, None, None, None),
        P("view", "seg", None, None),
        P(),
        P(),
        P(),
        P(),
        P(),
        P(),
        P(),
    )
    out_specs = P("view", "seg", None, None)
    return jax.shard_map(shards, mesh=mesh, in_specs=in_specs, out_specs=out_specs, check_vma=False)
```

time: 347 us -> 163 us (0.47); the launches traced: 342 us -> 162 us
  waiting for transfers between devices: 182 us -> 57.3 us
  Pallas kernels: 0 us -> 56.4 us
  matrix products: 50.7 us -> 0 us
  local copies, waits for them, and re-layouts: 49.5 us -> 8.46 us
  between operations: 14.5 us -> 0.32 us
  blocking collectives: 11.8 us -> 0 us
  other arithmetic: 10.9 us -> 15.1 us
    all_to_all x2 -> x1, waiting for transfers between devices: 113 us -> 40.6 us  [shards(): lax.all_to_all(payload, 'seg', split_axis=0, concat_axis=0, tiled=True)]
    reduce_scatter x1 -> x0, waiting for transfers between devices: 68.8 us -> none  [shards(): lax.psum_scatter(dense_rows, 'view', scatter_dimension=0, tiled=True)]
    pallas_call x0 -> x4, Pallas kernels: none -> 56.4 us  [the longest x1 19 us: attend(): pl.pallas_call(functools.partial(attend_kernel, block), in_specs=[VM] * 7...]
    dot_general x10 -> x0, matrix products: 50.7 us -> none  [the longest x1 13.4 us: shards(): jnp.einsum('bm,mrc->brc', onehot.astype(jnp.bfloat16), lifted.reshape(slo...]
    ppermute x2 -> x8, waiting for transfers between devices: 0.01 us -> 16.7 us  [the longest x1 5.95 us: shards(): near_up0 = lax.ppermute(join(up0, far_up), 'view', up)]
    reshape x5 -> x1, local copies, waits for them, and re-layouts: 16.8 us -> 0.25 us  [shards(): jnp.transpose(lift_weights[0], (0, 3, 1, 2))]
    gather x1 -> x0, local copies, waits for them, and re-layouts: 13.2 us -> none  [shards(): jnp.take(view_table, patch_picks.reshape(-1), axis=0)]
    unnamed x1 -> x0, blocking collectives: 11.8 us -> none
  transfers between devices with their start and end apart: 5 -> 9, of which waited for: 2 -> 7; matrix products, arithmetic and copies ran while one was open for 10% -> 7% of each run, Pallas kernels for 0% -> 0%
where the time goes in v1:
time: 163 us; the launch traced here: 162 us
  waiting for transfers between devices  57.3 us (35%)
  Pallas kernels  56.4 us (35%)
  starting transfers between devices  24.4 us (15%)
  other arithmetic  15.1 us (9%)
  local copies, waits for them, and re-layouts  8.46 us (5%)
    all_to_all x1, waiting for transfers between devices, shards(): lax.all_to_all(payload, 'seg', split_axis=0, concat_axis=0, tiled=True)  40.6 us
    pallas_call x1, Pallas kernels, attend(): pl.pallas_call(functools.partial(attend_kernel, block), in_specs=[VM] * 7...  19 us
    pallas_call x1, Pallas kernels, pack(): pl.pallas_call(functools.partial(pack_kernel, patches, per_step), grid=(s...  16.1 us
    pallas_call x1, Pallas kernels, gather_sums(): pl.pallas_call(functools.partial(gather_sums_kernel, slots_per, block, pi...  14.4 us
    unnamed x5, other arithmetic  8.3 us
    all_to_all x1, starting transfers between devices, shards(): lax.all_to_all(payload, 'seg', split_axis=0, concat_axis=0, tiled=True)  7.56 us
    ppermute x1, starting transfers between devices, shards(): after = lax.ppermute(first, ('view', 'seg'), ring_down)  7.22 us
    pallas_call x1, Pallas kernels, project(): pl.pallas_call(functools.partial(project_kernel, block, half_blocks), in_...  6.79 us
  transfers between devices with their start and end apart: 9, of which 7 were waited for; matrix products, arithmetic and copies ran while one was open for 7% of the time, Pallas kernels for 0%

profile of v1, /device:TPU:0, one launch (start us, length us, event | category | flops | bytes accessed | tf_op | source)
XLA Modules:
  0.0 162.0 jit_solution(18187864812813631700)
XLA Ops:
  0.0 2.9 %reshape_squeeze.4.idx_ref = s32[2048,1]{1,0:T(8,128)} reshape(s32[1,32,2,32]{3,2,1,0:T(2,128)} %param.14) | data formatting | bytes 16384 | tf_op jit(solution)/shard_map/reshape;squeeze | solution.py:284
  2.9 0.7 convert_bitcast_fusion
  3.5 0.1 copy.18
  3.7 1.6 copy.14
  5.2 0.3 reshape.21
  5.5 0.8 fusion.2.extra_ref
  6.3 16.1 %pack.1 = bf16[32,72,768]{2,1,0:T(8,128)(2,1)} custom-call(bf16[1369,1024]{1,0:T(8,128)(2,1)} %bitcast.18, f32[1024,768]{1,0:T(8,128)} %win_ref.1, s32[2048,1]{1,0:T(8,128)} %reshape_squeeze.4.idx_ref, bf16[32,8,768]{2,1,0:T(8,128)(2,1)} %fusion.2.extra_ref), custom_call_target="tpu_custom_call" | custom-call | tf_op jit(solution)/shard_map/pack/pallas_call | solution.py:57
  22.4 7.6 %all-to-all-start = ((bf16[32,72,768]{2,1,0:T(8,128)(2,1)}), bf16[32,72,768]{2,1,0:T(8,128)(2,1)S(1)}, u32[]{:S(2)}, u32[]{:S(2)}) async-start(bf16[32,72,768]{2,1,0:T(8,128)(2,1)} %pack.1), calls=%async_computation | async-start | bytes 7077888 | tf_op jit(solution)/shard_map/all_to_all | solution.py:285
  30.0 0.0 copy-start.8
  30.0 0.6 fusion.17
  30.6 1.7 %fusion.3 = f32[512,768]{1,0:T(8,128)} fusion(f32[128]{0:T(128)S(1)} %multiply_exponential_fusion, f32[512]{0:T(512)S(1)} %bitcast.26), kind=kLoop, calls=%fused_computation.12 | loop fusion | flops 65535 | bytes 264704
  32.3 1.6 %fusion.4 = f32[512,768]{1,0:T(8,128)} fusion(f32[512,768]{1,0:T(8,128)} %fusion.3, f32[128]{0:T(128)S(1)} %multiply_exponential_fusion, f32[512]{0:T(512)S(1)} %bitcast.27), kind=kLoop, calls=%fused_computation.13 | loop fusion | flops 65536 | bytes 264704
  34.0 40.6 %all-to-all-done.recv_ref = bf16[32,72,768]{2,1,0:T(8,128)(2,1)S(1)} async-done(((bf16[32,72,768]{2,1,0:T(8,128)(2,1)}), bf16[32,72,768]{2,1,0:T(8,128)(2,1)S(1)}, u32[]{:S(2)}, u32[]{:S(2)}) %all-to-all-start) | async-done | bytes 3538976 | tf_op jit(solution)/shard_map/all_to_all | solution.py:285
  74.6 0.1 fusion.9
  74.6 0.8 reshape.24
  75.4 1.2 compare_select_fusion.8
  76.6 1.2 compare_select_fusion.9.place_ref
  77.8 14.4 %gather_sums.1 = (bf16[264,768]{1,0:T(8,128)(2,1)}, bf16[264,768]{1,0:T(8,128)(2,1)}, bf16[264,768]{1,0:T(8,128)(2,1)}, bf16[264,768]{1,0:T(8,128)(2,1)}, bf16[2...) custom-call(s32[64]{0:T(128)} %compare_select_fusion.9.place_ref, ...), custom_call_target="tpu_custom_call" | custom-call | tf_op jit(solution)/shard_map/gather_sums/pallas_call | solution.py:108
  92.2 1.9 %collective-permute-start.1 = (bf16[264,768]{1,0:T(8,128)(2,1)}, bf16[264,768]{1,0:T(8,128)(2,1)S(1)}, u32[]{:S(2)}, u32[]{:S(2)}) collective-permute-start(bf16[264,768]{1,0:T(8,128)(2,1)} %get-tuple-element.20), channel_id=1, source_target_pairs={{0,32},{32,64},{64,96},{96,0},{1,33},{33,65},{65,97},{97,1},{2,34}... | collective-permute-start | bytes 1216520 | tf_op jit(solution)/shard_map/ppermute | solution.py:312
  94.2 1.7 %fusion.5 = f32[512,768]{1,0:T(8,128)} fusion(f32[512,768]{1,0:T(8,128)} %fusion.4, f32[512]{0:T(512)S(1)} %bitcast.24, f32[128]{0:T(128)S(1)} %copy-done.9), kind=kLoop, calls=%fused_computation.14 | loop fusion | flops 65536 | bytes 264704
  95.8 2.1 %collective-permute-start.4 = (bf16[264,768]{1,0:T(8,128)(2,1)}, bf16[264,768]{1,0:T(8,128)(2,1)S(1)}, u32[]{:S(2)}, u32[]{:S(2)}) collective-permute-start(bf16[264,768]{1,0:T(8,128)(2,1)} %get-tuple-element.24), channel_id=1, source_target_pairs={{32,0},{64,32},{96,64},{0,96},{33,1},{65,33},{97,65},{1,97},{34,2}... | collective-permute-start | bytes 1216520 | tf_op jit(solution)/shard_map/ppermute | solution.py:313
  98.0 1.7 %fusion.6 = f32[512,768]{1,0:T(8,128)} fusion(f32[512,768]{1,0:T(8,128)} %fusion.5, f32[512]{0:T(512)S(1)} %bitcast.25, f32[128]{0:T(128)S(1)} %copy-done.9), kind=kLoop, calls=%fused_computation.15 | loop fusion | flops 65536 | bytes 264704
  99.6 2.0 %collective-permute-start = (bf16[264,768]{1,0:T(8,128)(2,1)}, bf16[264,768]{1,0:T(8,128)(2,1)S(1)}, u32[]{:S(2)}, u32[]{:S(2)}) collective-permute-start(bf16[264,768]{1,0:T(8,128)(2,1)} %get-tuple-element.18), channel_id=1, source_target_pairs={{32,0},{64,32},{96,64},{0,96},{33,1},{65,33},{97,65},{1,97},{34,2}... | collective-permute-start | bytes 1216520 | tf_op jit(solution)/shard_map/ppermute | solution.py:315
  101.6 0.0 collective-permute-start.3
  101.7 5.0 %collective-permute-done.1 = bf16[264,768]{1,0:T(8,128)(2,1)S(1)} collective-permute-done((bf16[264,768]{1,0:T(8,128)(2,1)}, bf16[264,768]{1,0:T(8,128)(2,1)S(1)}, u32[]{:S(2)}, u32[]{:S(2)}) %collective-permute-start.1) | collective-permute-done | bytes 405536 | tf_op jit(solution)/shard_map/ppermute | solution.py:312
  106.7 1.1 add_convert_fusion.1
  107.8 0.1 collective-permute-start.2
  107.9 0.4 collective-permute-done.4
  108.3 0.0 copy-done.5
  108.3 0.1 add_convert_fusion
  108.4 3.4 %collective-permute-start.5 = (bf16[264,768]{1,0:T(8,128)(2,1)S(1)}, bf16[264,768]{1,0:T(8,128)(2,1)S(1)}, u32[]{:S(2)}, u32[]{:S(2)}) collective-permute-start(bf16[264,768]{1,0:T(8,128)(2,1)S(1)} %add_convert_fusion), channel_id=1, source_target_pairs={{32,0},{64,32},{96,64},{0,96},{33,1},{65,33},{97,65},{1,97},{34,2}... | collective-permute-start | bytes 1216520 | tf_op jit(solution)/shard_map/ppermute | solution.py:317
  111.8 1.7 %fusion.7 = f32[512,768]{1,0:T(8,128)} fusion(f32[512,768]{1,0:T(8,128)} %fusion.6, f32[512]{0:T(512)S(1)} %bitcast.22, f32[128]{0:T(128)S(1)} %copy-done.9), kind=kLoop, calls=%fused_computation.16 | loop fusion | flops 65536 | bytes 264704
  113.5 1.6 %fusion.8.refs_6_ = f32[512,768]{1,0:T(8,128)} fusion(f32[512,768]{1,0:T(8,128)} %fusion.7, f32[512]{0:T(512)S(1)} %bitcast.23, f32[128]{0:T(128)S(1)} %copy-done.9), kind=kLoop, calls=%fused_computation.17 | loop fusion | flops 65536 | bytes 264704 | tf_op jit(solution)/shard_map/concatenate | solution.py:260
  115.1 1.9 %collective-permute-done.refs_1_ = bf16[264,768]{1,0:T(8,128)(2,1)S(1)} collective-permute-done((bf16[264,768]{1,0:T(8,128)(2,1)}, bf16[264,768]{1,0:T(8,128)(2,1)S(1)}, u32[]{:S(2)}, u32[]{:S(2)}) %collective-permute-start) | collective-permute-done | bytes 405536 | tf_op jit(solution)/shard_map/ppermute | solution.py:315
  117.0 0.0 collective-permute-done.3.refs_4_
  117.0 6.0 %collective-permute-done.2.refs_2_ = bf16[264,768]{1,0:T(8,128)(2,1)S(1)} collective-permute-done((bf16[264,768]{1,0:T(8,128)(2,1)S(1)}, bf16[264,768]{1,0:T(8,128)(2,1)S(1)}, u32[]{:S(2)}, u32[]{:S(2)}) %collective-permute-start.2) | collective-permute-done | bytes 405536 | tf_op jit(solution)/shard_map/ppermute | solution.py:316
  122.9 1.2 collective-permute-done.5.refs_5_
  124.1 0.0 copy-done.2
  124.1 0.7 copy-done.4
  124.9 6.8 %project.1 = (f32[512,768]{1,0:T(8,128)}, bf16[512,768]{1,0:T(8,128)(2,1)}, bf16[512,768]{1,0:T(8,128)(2,1)}, bf16[512,768]{1,0:T(8,128)(2,1)}) custom-call(bf16[264,768]{1,0:T(8,128)(2,1)} %get-tuple-element.17.refs_0_, bf16[264,768]{1,0:T(8,128)(2,1)} %copy-done.1, bf16[264,768]{1,0:T(8,128)(2,1)} %copy-done.3, ...), custom_call_target="tpu_custom_call" | custom-call | tf_op jit(solution)/shard_map/project/pallas_call | solution.py:155
  131.6 0.9 fusion.15
  132.5 0.1 collective-permute-start.6
  132.6 7.2 %collective-permute-start.7 = (bf16[32,1536]{1,0:T(8,128)(2,1)S(1)}, bf16[32,1536]{1,0:T(8,128)(2,1)S(1)}, u32[]{:S(2)}, u32[]{:S(2)}) collective-permute-start(bf16[32,1536]{1,0:T(8,128)(2,1)S(1)} %pad_maximum_fusion.1), channel_id=1, source_target_pairs={{1,0},{2,1},{3,2},{4,3},{5,4},{6,5},{7,6},{8,7},{9,8},{10,9},{11,1... | collective-permute-start | bytes 294920 | tf_op jit(solution)/shard_map/ppermute | solution.py:330
  139.9 2.2 %collective-permute-done.6.before_ref = bf16[32,1536]{1,0:T(8,128)(2,1)S(1)} collective-permute-done((bf16[32,1536]{1,0:T(8,128)(2,1)S(1)}, bf16[32,1536]{1,0:T(8,128)(2,1)S(1)}, u32[]{:S(2)}, u32[]{:S(2)}) %collective-permute-start.6) | collective-permute-done | bytes 98336 | tf_op jit(solution)/shard_map/ppermute | solution.py:329
  142.1 0.0 collective-permute-done.7.after_ref
  142.1 0.6 copy-done.6
  142.7 0.0 copy-done.7
  142.8 19.0 %attend.1 = bf16[512,768]{1,0:T(8,128)(2,1)} custom-call(f32[512,768]{1,0:T(8,128)} %get-tuple-element.25.stream_ref, bf16[512,768]{1,0:T(8,128)(2,1)} %get-tuple-element.26.q_ref, bf16[512,768]{1,0:T(8,128)(2,1)} %get-tuple-element.27.k_ref, bf16[512,768]{1,0:T(8,128)(2,1)} %get-tuple-element.28.v_ref, bf16[32,1536]{1,0:T(8,128)(2,1)} %copy-done.6, ...), custom_call_target="tpu_custom_call" | custom-call | tf_op jit(solution)/shard_map/attend/pallas_call | solution.py:233
  (27 shorter events, 0.1 us)
Async XLA Ops:
  22.4 7.6 %copy-start.12 = (s32[1,1,3,512]{3,1,2,0:T(1,128)S(1)}, s32[1,1,3,512]{3,1,2,0:T(1,128)}, u32[]{:S(2)}) copy-start(s32[1,1,3,512]{3,1,2,0:T(1,128)} %param.16) | copy-start | bytes 18436
  22.4 52.2 %all-to-all-start = ((bf16[32,72,768]{2,1,0:T(8,128)(2,1)}), bf16[32,72,768]{2,1,0:T(8,128)(2,1)S(1)}, u32[]{:S(2)}, u32[]{:S(2)}) async-start(bf16[32,72,768]{2,1,0:T(8,128)(2,1)} %pack.1), calls=%async_computation | async-start | bytes 7077888 | tf_op jit(solution)/shard_map/all_to_all | solution.py:285
  30.0 2.3 %copy-start.8 = (f32[128]{0:T(128)}, f32[128]{0:T(128)S(1)}, u32[]{:S(2)}) copy-start(f32[128]{0:T(128)S(1)} %multiply_exponential_fusion) | copy-start | bytes 1540
  74.6 3.2 %copy-start = (bf16[32,72,768]{2,1,0:T(8,128)(2,1)}, bf16[32,72,768]{2,1,0:T(8,128)(2,1)S(1)}, u32[]{:S(2)}) copy-start(bf16[32,72,768]{2,1,0:T(8,128)(2,1)S(1)} %all-to-all-done.recv_ref) | copy-start | bytes 10616836
  77.8 16.3 %copy-start.9 = (f32[128]{0:T(128)S(1)}, f32[128]{0:T(128)}, u32[]{:S(2)}) copy-start(f32[128]{0:T(128)} %copy-done.8) | copy-start | bytes 1540
  77.8 16.3 %copy-start.11 = (f32[512,1]{0,1:T(1,128)S(1)}, f32[512,1]{0,1:T(1,128)}, u32[]{:S(2)}) copy-start(f32[512,1]{0,1:T(1,128)} %get-tuple-element.37) | copy-start | bytes 6148
  92.2 16.1 %copy-start.5 = (bf16[264,768]{1,0:T(8,128)(2,1)S(1)}, bf16[264,768]{1,0:T(8,128)(2,1)}, u32[]{:S(2)}) copy-start(bf16[264,768]{1,0:T(8,128)(2,1)} %get-tuple-element.23) | copy-start | bytes 1216516
  92.2 19.6 %copy-start.10 = (f32[512,1]{0,1:T(1,128)S(1)}, f32[512,1]{0,1:T(1,128)}, u32[]{:S(2)}) copy-start(f32[512,1]{0,1:T(1,128)} %get-tuple-element.36) | copy-start | bytes 6148
  92.2 14.5 %collective-permute-start.1 = (bf16[264,768]{1,0:T(8,128)(2,1)}, bf16[264,768]{1,0:T(8,128)(2,1)S(1)}, u32[]{:S(2)}, u32[]{:S(2)}) collective-permute-start(bf16[264,768]{1,0:T(8,128)(2,1)} %get-tuple-element.20), channel_id=1, source_target_pairs={{0,32},{32,64},{64,96},{96,0},{1,33},{33,65},{65,97},{97,1},{2,34}... | collective-permute-start | bytes 1216520 | tf_op jit(solution)/shard_map/ppermute | solution.py:312
  95.8 12.5 %collective-permute-start.4 = (bf16[264,768]{1,0:T(8,128)(2,1)}, bf16[264,768]{1,0:T(8,128)(2,1)S(1)}, u32[]{:S(2)}, u32[]{:S(2)}) collective-permute-start(bf16[264,768]{1,0:T(8,128)(2,1)} %get-tuple-element.24), channel_id=1, source_target_pairs={{32,0},{64,32},{96,64},{0,96},{33,1},{65,33},{97,65},{1,97},{34,2}... | collective-permute-start | bytes 1216520 | tf_op jit(solution)/shard_map/ppermute | solution.py:313
  99.6 17.3 %collective-permute-start = (bf16[264,768]{1,0:T(8,128)(2,1)}, bf16[264,768]{1,0:T(8,128)(2,1)S(1)}, u32[]{:S(2)}, u32[]{:S(2)}) collective-permute-start(bf16[264,768]{1,0:T(8,128)(2,1)} %get-tuple-element.18), channel_id=1, source_target_pairs={{32,0},{64,32},{96,64},{0,96},{33,1},{65,33},{97,65},{1,97},{34,2}... | collective-permute-start | bytes 1216520 | tf_op jit(solution)/shard_map/ppermute | solution.py:315
  101.6 15.3 %collective-permute-start.3 = (bf16[264,768]{1,0:T(8,128)(2,1)}, bf16[264,768]{1,0:T(8,128)(2,1)S(1)}, u32[]{:S(2)}, u32[]{:S(2)}) collective-permute-start(bf16[264,768]{1,0:T(8,128)(2,1)} %get-tuple-element.22), channel_id=1, source_target_pairs={{0,32},{32,64},{64,96},{96,0},{1,33},{33,65},{65,97},{97,1},{2,34}... | collective-permute-start | bytes 1216520 | tf_op jit(solution)/shard_map/ppermute | solution.py:314
  107.8 15.1 %collective-permute-start.2 = (bf16[264,768]{1,0:T(8,128)(2,1)S(1)}, bf16[264,768]{1,0:T(8,128)(2,1)S(1)}, u32[]{:S(2)}, u32[]{:S(2)}) collective-permute-start(bf16[264,768]{1,0:T(8,128)(2,1)S(1)} %add_convert_fusion.1), channel_id=1, source_target_pairs={{0,32},{32,64},{64,96},{96,0},{1,33},{33,65},{65,97},{97,1},{2,34}... | collective-permute-start | bytes 1216520 | tf_op jit(solution)/shard_map/ppermute | solution.py:316
  108.4 15.7 %collective-permute-start.5 = (bf16[264,768]{1,0:T(8,128)(2,1)S(1)}, bf16[264,768]{1,0:T(8,128)(2,1)S(1)}, u32[]{:S(2)}, u32[]{:S(2)}) collective-permute-start(bf16[264,768]{1,0:T(8,128)(2,1)S(1)} %add_convert_fusion), channel_id=1, source_target_pairs={{32,0},{64,32},{96,64},{0,96},{33,1},{65,33},{97,65},{1,97},{34,2}... | collective-permute-start | bytes 1216520 | tf_op jit(solution)/shard_map/ppermute | solution.py:317
  117.0 7.2 %copy-start.1 = (bf16[264,768]{1,0:T(8,128)(2,1)}, bf16[264,768]{1,0:T(8,128)(2,1)S(1)}, u32[]{:S(2)}) copy-start(bf16[264,768]{1,0:T(8,128)(2,1)S(1)} %collective-permute-done.refs_1_) | copy-start | bytes 1216516
  117.0 7.2 %copy-start.2 = (bf16[264,768]{1,0:T(8,128)(2,1)}, bf16[264,768]{1,0:T(8,128)(2,1)S(1)}, u32[]{:S(2)}) copy-start(bf16[264,768]{1,0:T(8,128)(2,1)S(1)} %collective-permute-done.3.refs_4_) | copy-start | bytes 1216516
  122.9 1.2 copy-start.3
  124.1 0.7 copy-start.4
  132.5 9.5 %collective-permute-start.6 = (bf16[32,1536]{1,0:T(8,128)(2,1)S(1)}, bf16[32,1536]{1,0:T(8,128)(2,1)S(1)}, u32[]{:S(2)}, u32[]{:S(2)}) collective-permute-start(bf16[32,1536]{1,0:T(8,128)(2,1)S(1)} %pad_maximum_fusion), channel_id=1, source_target_pairs={{0,1},{1,2},{2,3},{3,4},{4,5},{5,6},{6,7},{7,8},{8,9},{9,10},{10,1... | collective-permute-start | bytes 294920 | tf_op jit(solution)/shard_map/ppermute | solution.py:329
  132.6 9.4 %collective-permute-start.7 = (bf16[32,1536]{1,0:T(8,128)(2,1)S(1)}, bf16[32,1536]{1,0:T(8,128)(2,1)S(1)}, u32[]{:S(2)}, u32[]{:S(2)}) collective-permute-start(bf16[32,1536]{1,0:T(8,128)(2,1)S(1)} %pad_maximum_fusion.1), channel_id=1, source_target_pairs={{1,0},{2,1},{3,2},{4,3},{5,4},{6,5},{7,6},{8,7},{9,8},{10,9},{11,1... | collective-permute-start | bytes 294920 | tf_op jit(solution)/shard_map/ppermute | solution.py:330
  142.1 0.6 copy-start.6
  142.1 0.7 copy-start.7

commit v2 on v1

v2 whole, which is shorter than its diff:
```python
import functools
import math

import jax
import jax.numpy as jnp
from jax import lax
from jax.experimental import pallas as pl
from jax.experimental.pallas import tpu as pltpu
from jax.sharding import PartitionSpec as P


HEAD_DIM = 64
F32 = jnp.float32
BF16 = jnp.bfloat16
EXTRA = 16
VMEM_LIMIT = 60 * 1024 * 1024
VM = pl.BlockSpec(memory_space=pltpu.VMEM)
ANY = pl.BlockSpec(memory_space=pl.ANY)


def params(**kw):
    return pltpu.CompilerParams(vmem_limit_bytes=VMEM_LIMIT, **kw)


def dot(a, b):
    return lax.dot_general(a, b, (((1,), (0,)), ((), ())), preferred_element_type=F32)


def pack_kernel(patches, row_step, per_step, weighted, *refs):
    if weighted:
        ids_ref, feat_ref, win_ref, idx_ref, lift_ref, out_ref, table, places, high, low = refs
    else:
        feat_ref, win_ref, idx_ref, out_ref, table, places, high, low = refs
    table_rows, width = table.shape
    step = pl.program_id(0)
    row_steps = -(-patches // row_step)

    @pl.when(step == 0)
    def _():
        high[...] = win_ref[...].astype(BF16)
        low[...] = (win_ref[...] - high[...].astype(F32)).astype(BF16)
        turned = jnp.transpose(idx_ref[...].astype(F32)).astype(jnp.int32)
        for i in range(turned.shape[1]):
            places[i * 128 : (i + 1) * 128, :] = turned[:, i : i + 1]

    for s in range(row_steps):

        @pl.when(step == s)
        def _(s=s):
            start = s * row_step
            keep = min(row_step, table_rows - start)
            rows = feat_ref[:keep, :]
            values = (dot(rows, high[...]) + dot(rows, low[...])).astype(BF16)
            if start + keep > patches:
                live = lax.broadcasted_iota(jnp.int32, (keep, width), 0) < patches - start
                values = jnp.where(live, values, jnp.zeros_like(values))
            table[start : start + keep, :] = values

    @pl.when(step >= row_steps)
    def _():
        base = step - row_steps
        each = places.shape[0] // (per_step * (pl.num_programs(0) - row_steps))
        count = per_step * each
        spot = places[pl.ds(pl.multiple_of(base * count, count), count), :]
        picked = lax.broadcasted_iota(jnp.int32, (count, table_rows), 1) == spot
        rows = dot(picked.astype(F32).astype(BF16), table[...]).astype(BF16)
        for i in range(per_step):
            out_ref[i, :each, :] = rows[i * each : (i + 1) * each, :]
            if weighted:
                slots, _, block = lift_ref.shape[1:]
                both = jnp.concatenate([lift_ref[i, c].astype(F32) for c in range(slots)], axis=1)
                turned = jnp.transpose(both)
                for c in range(slots):
                    groups = [
                        turned[c * block + g * EXTRA : c * block + (g + 1) * EXTRA, :]
                        for g in range(block // EXTRA)
                    ]
                    out_ref[i, each:, c * 128 : (c + 1) * 128] = jnp.concatenate(
                        groups, axis=1
                    ).astype(BF16)
                lane = lax.broadcasted_iota(jnp.int32, (EXTRA, 128), 1)
                marks = jnp.zeros((EXTRA, 128), jnp.int32)
                for c in range(slots):
                    marks = jnp.where(lane == c, ids_ref[c, base * per_step + i], marks)
                out_ref[i, each:, slots * 128 : (slots + 1) * 128] = marks.astype(F32).astype(BF16)
                out_ref[i, each:, (slots + 1) * 128 :] = jnp.zeros(
                    (EXTRA, width - (slots + 1) * 128), BF16
                )


def pack(features, w_in, indices, segments, start, width, ids=None, lift=None):
    patches, channels = features.shape
    count = indices.shape[0] * indices.shape[1]
    each = count // segments
    per_step, row_step = 8, 512
    row_steps = -(-patches // row_step)
    table_rows = -(-patches // 128) * 128
    weighted = lift is not None

    def later(i):
        return jnp.maximum(i - row_steps, 0)

    in_specs = [
        pl.BlockSpec((row_step, channels), lambda i, *_: (jnp.minimum(i, row_steps - 1), 0)),
        pl.BlockSpec((channels, width), lambda i, *_: (0, start // width)),
        pl.BlockSpec(indices.shape, lambda i, *_: (0, 0)),
    ]
    operands = [features, w_in, indices]
    rows = each
    if weighted:
        in_specs.append(
            pl.BlockSpec((per_step,) + lift.shape[1:], lambda i, *_: (later(i), 0, 0, 0))
        )
        operands = [ids] + operands + [lift]
        rows += EXTRA
    return pl.pallas_call(
        functools.partial(pack_kernel, patches, row_step, per_step, weighted),
        grid_spec=pltpu.PrefetchScalarGridSpec(
            num_scalar_prefetch=int(weighted),
            grid=(row_steps + segments // per_step,),
            in_specs=in_specs,
            out_specs=pl.BlockSpec((per_step, rows, width), lambda i, *_: (later(i), 0, 0)),
            scratch_shapes=[
                pltpu.VMEM((table_rows, width), BF16),
                pltpu.VMEM((count, 1), jnp.int32),
                pltpu.VMEM((channels, width), BF16),
                pltpu.VMEM((channels, width), BF16),
            ],
        ),
        out_shape=jax.ShapeDtypeStruct((segments, rows, width), BF16),
        compiler_params=params(dimension_semantics=("arbitrary",)),
        name="pack",
    )(*operands)


def gather_sums_kernel(block, picks, half_blocks, counted, ids_ref, me_ref, rows_ref, weight_ref, *rest):
    outs, total = rest[-6:-1], rest[-1]
    total[...] = jnp.zeros_like(total)
    views, _, width = rows_ref.shape
    slots = ids_ref.shape[1]
    size = outs[2].shape[0]
    parts = 8
    depth = slots * picks * 4
    group = lax.broadcasted_iota(jnp.int32, (EXTRA, depth), 1) // picks
    me = me_ref[0]

    def add_view(j, carry):
        weights = weight_ref[j, :, :depth]
        zero = jnp.zeros_like(weights)
        left = jnp.concatenate([jnp.where(group == r, weights, zero) for r in range(slots * 4)], axis=0)
        rows = [rows_ref[j, c * picks : (c + 1) * picks, :] for c in range(slots)]
        right = jnp.concatenate([rows[c] for c in range(slots) for _ in range(4)], axis=0)
        lifted = dot(left, right)
        for c in range(slots):
            name = ids_ref[j, c]
            owner = name // (2 * half_blocks)
            within = name - owner * (2 * half_blocks)
            half = within // half_blocks
            within = within - half * half_blocks
            away = owner - me + jnp.where(owner < me, parts // 2, 0)
            start = (away * 2 + half) * size
            empty = name == parts * half_blocks
            place = jnp.where(empty, parts * size, start + within * block)
            place = pl.multiple_of(place, 8)
            total[pl.ds(place, block), :] += lifted[c * block : (c + 1) * block, :]
            if counted:
                mark = jnp.where(empty, parts * size + block, start + half_blocks * block + within)
                total[pl.ds(mark, 1), :] += jnp.ones((1, width), F32)
        return carry

    lax.fori_loop(0, views, add_view, 0, unroll=4)

    def part(away, half):
        first = (away * 2 + half) * size
        return total[first : first + size, :].astype(BF16)

    own, up_first, up_last, down_first, down_last = outs
    up_first[:size, :], up_first[size:, :] = part(1, 1), part(2, 0)
    down_first[:size, :], down_first[size:, :] = part(3, 0), part(2, 1)
    up_last[...], down_last[...] = part(1, 0), part(3, 1)
    own[:size, :], own[size:, :] = part(0, 0), part(0, 1)


def gather_sums(ids, me, rows, weights, block, picks, half_blocks, counted, *after):
    views, _, width = rows.shape
    count = ids.shape[1] * picks
    size = half_blocks * block + (8 if counted else 0)
    sizes = [2 * size, 2 * size, size, 2 * size, size]
    return pl.pallas_call(
        functools.partial(gather_sums_kernel, block, picks, half_blocks, counted),
        grid_spec=pltpu.PrefetchScalarGridSpec(
            num_scalar_prefetch=2,
            grid=(1,),
            in_specs=[
                pl.BlockSpec((views, count, width), lambda i, *_: (0, 0, 0)),
                pl.BlockSpec((views, EXTRA, weights.shape[2]), lambda i, *_: (0, count // EXTRA, 0)),
            ]
            + [ANY] * len(after),
            out_specs=[pl.BlockSpec((s, width), lambda i, *_: (0, 0)) for s in sizes],
            scratch_shapes=[pltpu.VMEM((8 * size + block + 8, width), F32)],
        ),
        out_shape=[jax.ShapeDtypeStruct((s, width), BF16) for s in sizes],
        compiler_params=params(dimension_semantics=("arbitrary",)),
        name="gather_sums",
    )(ids, me, rows, weights, *after)


def normalize(values):
    average = jnp.mean(values, axis=-1, keepdims=True)
    centred = values - average
    spread = jnp.mean(centred * centred, axis=-1, keepdims=True)
    return (centred * lax.rsqrt(spread + 1e-05)).astype(BF16)


def project_kernel(block, half_blocks, *refs):
    sums = (refs[0:5], refs[5:10])
    pos_ref, wq_ref, wk_ref, wv_ref, stream_ref, q_ref, k_ref, v_ref = refs[10:]
    half_rows = half_blocks * block
    for h in range(2):
        base = h * half_rows

        def load(column, lo, hi):
            own, below_first, above_first, below_last, above_last = sums[column]
            size = below_last.shape[0]
            first, last = (above_first, below_last) if h == 0 else (below_first, above_last)
            here = slice(h * size + lo, h * size + hi)
            return own[here, :].astype(F32) + first[lo:hi, :].astype(F32) + last[lo:hi, :].astype(F32)

        tally = jnp.maximum(load(0, half_rows, half_rows + 8), 1.0)
        for i in range(half_blocks):
            lo = i * block
            for column in range(2):
                start = sums[0][0].shape[1] * column
                lanes = slice(start, start + sums[column][0].shape[1])
                averaged = load(column, lo, lo + block) / tally[i : i + 1, : lanes.stop - lanes.start]
                stream_ref[base + lo : base + lo + block, lanes] = (
                    averaged + pos_ref[base + lo : base + lo + block, lanes]
                )
        normed = normalize(stream_ref[base : base + half_rows, :])
        for w_ref, o_ref in ((wk_ref, k_ref), (wv_ref, v_ref), (wq_ref, q_ref)):
            o_ref[base : base + half_rows, :] = dot(normed, w_ref[...]).astype(BF16)


def project(sums, pos, w_query, w_key, w_value, block, half_blocks):
    rows, width = pos.shape
    return pl.pallas_call(
        functools.partial(project_kernel, block, half_blocks),
        in_specs=[VM] * (len(sums) + 4),
        out_specs=[VM] * 4,
        out_shape=[jax.ShapeDtypeStruct((rows, width), F32)]
        + [jax.ShapeDtypeStruct((rows, width), BF16)] * 3,
        compiler_params=params(),
        name="project",
    )(*sums, pos, w_query, w_key, w_value)


def attend_kernel(
    block, stream_ref, q_ref, k_ref, v_ref, before_ref, after_ref, wout_ref, wup_hbm, wdown_hbm,
    out_ref, qx, kx, vx, mixed, attended, normed, total, wup, wdown, sems,
):
    rows, width = stream_ref.shape
    half = block // 2
    hidden_width = wup.shape[1]
    copies = [
        pltpu.make_async_copy(wup_hbm, wup, sems.at[0]),
        pltpu.make_async_copy(wdown_hbm, wdown, sems.at[1]),
    ]
    for c in copies:
        c.start()
    qx[:half, :] = jnp.zeros((half, width), BF16)
    qx[half : half + rows, :] = q_ref[...]
    qx[half + rows :, :] = jnp.zeros((half, width), BF16)
    for x, own, lane in ((kx, k_ref, 0), (vx, v_ref, width)):
        x[:half, :] = before_ref[:, lane : lane + width]
        x[half : half + rows, :] = own[...]
        x[half + rows :, :] = after_ref[:, lane : lane + width]
    low_lanes = lax.broadcasted_iota(jnp.int32, (block, 128), 1) < HEAD_DIM

    def window(w, carry):
        span = pl.ds(pl.multiple_of(w * block, block), block)
        for pair in range(width // 128):
            lanes = slice(pair * 128, (pair + 1) * 128)
            q, k, v = qx[span, lanes], kx[span, lanes], vx[span, lanes]
            zero = jnp.zeros_like(q)
            both = jnp.concatenate(
                [jnp.where(low_lanes, q, zero), jnp.where(low_lanes, zero, q)], axis=0
            )
            scores = lax.dot_general(
                both, k, (((1,), (1,)), ((), ())), preferred_element_type=F32
            ) * (1.0 / math.sqrt(HEAD_DIM))
            weights = jnp.exp(scores - jnp.max(scores, axis=-1, keepdims=True))
            probs = (weights / jnp.sum(weights, axis=-1, keepdims=True)).astype(BF16)
            out = dot(probs, v)
            mixed[span, lanes] = jnp.where(low_lanes, out[:block], out[block:]).astype(BF16)
        return carry

    lax.fori_loop(0, (rows + block) // block, window, 0)

    step = 256
    for start in range(0, rows, step):
        values = stream_ref[start : start + step, :] + dot(
            mixed[half + start : half + start + step, :], wout_ref[...]
        )
        attended[start : start + step, :] = values
        normed[start : start + step, :] = normalize(values)
    total[...] = attended[...]
    for c in copies:
        c.wait()
    chunk = 512

    def feed(i, carry):
        cols = pl.ds(pl.multiple_of(i * chunk, chunk), chunk)
        hidden = jax.nn.gelu(dot(normed[...], wup[:, cols]), approximate=True).astype(BF16)
        total[...] += dot(hidden, wdown[cols, :])
        return carry

    lax.fori_loop(0, hidden_width // chunk, feed, 0)
    out_ref[...] = total[...].astype(BF16)


def attend(stream, query, keys, values, before, after, w_out, w_up, w_down, block):
    rows, width = stream.shape
    hidden_width = w_up.shape[1]
    return pl.pallas_call(
        functools.partial(attend_kernel, block),
        in_specs=[VM] * 7 + [ANY] * 2,
        out_specs=VM,
        out_shape=jax.ShapeDtypeStruct((rows, width), BF16),
        scratch_shapes=[pltpu.VMEM((rows + block, width), BF16)] * 4
        + [
            pltpu.VMEM((rows, width), F32),
            pltpu.VMEM((rows, width), BF16),
            pltpu.VMEM((rows, width), F32),
            pltpu.VMEM((width, hidden_width), BF16),
            pltpu.VMEM((hidden_width, width), BF16),
            pltpu.SemaphoreType.DMA((2,)),
        ],
        compiler_params=params(),
        name="attend",
    )(stream, query, keys, values, before, after, w_out, w_up, w_down)


def position_kernel(coords_ref, freq_ref, out_ref):
    axes, rows = coords_ref.shape
    places = coords_ref[...].astype(F32)
    places = jnp.concatenate([places, jnp.zeros((8 - axes, rows), F32)], axis=0)
    columns = jnp.transpose(places)
    count = freq_ref.shape[1]
    for a in range(axes):
        angles = columns[:, a : a + 1] * freq_ref[...]
        out_ref[:, 2 * a * count : (2 * a + 1) * count] = jnp.sin(angles)
        out_ref[:, (2 * a + 1) * count : (2 * a + 2) * count] = jnp.cos(angles)


def position_code(places, model_width):
    freq_count = model_width // 6
    frequency = jnp.exp(-math.log(10000.0) * jnp.arange(freq_count, dtype=F32) / freq_count)
    return pl.pallas_call(
        position_kernel,
        in_specs=[VM] * 2,
        out_specs=VM,
        out_shape=jax.ShapeDtypeStruct((places.shape[1], model_width), F32),
        compiler_params=params(),
        name="position",
    )(places, frequency[None, :])


def share(parts, axis, count, half):
    own, up_first, up_last, down_first, down_last = parts
    up = [(i, (i + 1) % count) for i in range(count)]
    down = [(j, i) for i, j in up]

    def join(a, b):
        return (a.astype(F32) + b[half:].astype(F32)).astype(BF16)

    from_below = lax.ppermute(up_first, axis, up)
    from_above = lax.ppermute(down_first, axis, down)
    up_last, down_last = join(up_last, from_below), join(down_last, from_above)
    up_last, down_last = lax.ppermute(up_last, axis, up), lax.ppermute(down_last, axis, down)
    return [own, from_below, from_above, up_last, down_last]


def shards(
    features, block_ids, patch_rows, lift_weights, coords, w_in,
    w_query, w_key, w_value, w_out, w_up, w_down,
):
    view_count, segments = lax.axis_size("view"), lax.axis_size("seg")
    rows_here = coords.shape[-1]
    _, _, slots, block, picks = lift_weights.shape
    width = w_in.shape[1]
    quarter = rows_here // block
    half_blocks = quarter // 2

    indices = patch_rows[0].reshape(-1, 128)

    def send(payload):
        return lax.all_to_all(payload, "seg", split_axis=0, concat_axis=0, tiled=True)

    wide = width // 3 * 2
    by_row = jnp.transpose(lift_weights[0], (0, 1, 3, 2))
    first = send(pack(features[0], w_in, indices, segments, 0, wide, block_ids[0].T, by_row))
    second = send(pack(features[0], w_in, indices, segments, wide, width - wide))
    pos = position_code(coords[0, 0], width)
    me = lax.axis_index("view").astype(jnp.int32).reshape(1)
    ids = first[:, slots * picks, slots * 128 : slots * 128 + slots].astype(jnp.int32)

    def sums(rows, counted, *after):
        parts = gather_sums(ids, me, rows, first, block, picks, half_blocks, counted, *after)
        return share(parts, "view", view_count, parts[2].shape[0])

    shares = sums(first, True, pos)
    shares += sums(second, False)
    stream, query, keys, values = project(
        shares, pos, w_query, w_key, w_value, block, half_blocks
    )
    half = block // 2
    device_count = view_count * segments
    ring_up = [(i, (i + 1) % device_count) for i in range(device_count)]
    ring_down = [(j, i) for i, j in ring_up]
    last = jnp.concatenate([keys[rows_here - half :], values[rows_here - half :]], axis=1)
    first = jnp.concatenate([keys[:half], values[:half]], axis=1)
    before = lax.ppermute(last, ("view", "seg"), ring_up)
    after = lax.ppermute(first, ("view", "seg"), ring_down)
    encoded = attend(stream, query, keys, values, before, after, w_out, w_up, w_down, block)
    return encoded.reshape(1, 1, rows_here, width)


def solution(mesh):
    in_specs = (
        P(("view", "seg"), None, None),
        P(("view", "seg"), None, None),
        P(("view", "seg"), None, None, None),
        P(("view", "seg"), None, None, None, None),
        P("view", "seg", None, None),
        P(),
        P(),
        P(),
        P(),
        P(),
        P(),
        P(),
    )
    out_specs = P("view", "seg", None, None)

    return jax.shard_map(shards, mesh=mesh, in_specs=in_specs, out_specs=out_specs, check_vma=False)
```

time: 163 us -> 152 us (0.933)
  waiting for transfers between devices: 57.3 us -> 44.4 us
  other arithmetic: 15.1 us -> 3.38 us
  starting transfers between devices: 24.4 us -> 36 us
  Pallas kernels: 56.4 us -> 62.8 us
  local copies, waits for them, and re-layouts: 8.46 us -> 4.4 us
    all_to_all x1 -> x2, waiting for transfers between devices: 40.6 us -> 28.5 us  [send(): lax.all_to_all(payload, 'seg', split_axis=0, concat_axis=0, tiled=True)]
    unnamed x5 -> x0, other arithmetic: 8.3 us -> none
    ppermute x6 -> x8, starting transfers between devices: 9.58 us -> 16.6 us  [the longest x2 6.93 us: share(): lax.ppermute(down_last, axis, down)]
    pallas_call x2 -> x5, Pallas kernels: 30.5 us -> 36.7 us  [the longest x2 19.6 us: pack(): pl.pallas_call(functools.partial(pack_kernel, patches, row_step, per_step...]
    all_to_all x1 -> x2, starting transfers between devices: 7.56 us -> 12.1 us  [send(): lax.all_to_all(payload, 'seg', split_axis=0, concat_axis=0, tiled=True)]
    select_n x2 -> x0, other arithmetic: 2.42 us -> none  [the longest x1 1.24 us: shards(): jnp.where(ids == empty, parts * size, part * size + within % half_blocks...]
    concatenate x2 -> x0, other arithmetic: 2.4 us -> none  [the longest x1 1.62 us: position_code(): return jnp.concatenate(pieces, axis=-1)]
    ppermute x6 -> x8, waiting for transfers between devices: 14.5 us -> 13.7 us  [the longest x2 7.52 us: share(): from_below = lax.ppermute(up_first, axis, up)]
  transfers between devices with their start and end apart: 9 -> 12, of which waited for: 7 -> 7; matrix products, arithmetic and copies ran while one was open for 7% -> 3% of each run, Pallas kernels for 0% -> 16%
where the time goes in v2:
time: 152 us; the launch traced here: 151 us
  Pallas kernels  62.8 us (41%)
  waiting for transfers between devices  44.4 us (29%)
  starting transfers between devices  36 us (24%)
  local copies, waits for them, and re-layouts  4.4 us (3%)
  other arithmetic  3.38 us (2%)
    all_to_all x2, waiting for transfers between devices, send(): lax.all_to_all(payload, 'seg', split_axis=0, concat_axis=0, tiled=True)  28.5 us
    pallas_call x2, Pallas kernels, pack(): pl.pallas_call(functools.partial(pack_kernel, patches, row_step, per_step...  19.6 us
    pallas_call x1, Pallas kernels, attend(): pl.pallas_call(functools.partial(attend_kernel, block), in_specs=[VM] * 7...  19 us
    pallas_call x2, Pallas kernels, gather_sums(): pl.pallas_call(functools.partial(gather_sums_kernel, block, picks, half_b...  12.4 us
    all_to_all x2, starting transfers between devices, send(): lax.all_to_all(payload, 'seg', split_axis=0, concat_axis=0, tiled=True)  12.1 us
    ppermute x2, waiting for transfers between devices, share(): from_below = lax.ppermute(up_first, axis, up)  7.52 us
    ppermute x1, starting transfers between devices, shards(): after = lax.ppermute(first, ('view', 'seg'), ring_down)  7.22 us
    pallas_call x1, Pallas kernels, project(): pl.pallas_call(functools.partial(project_kernel, block, half_blocks), in_...  6.99 us
  transfers between devices with their start and end apart: 12, of which 7 were waited for; matrix products, arithmetic and copies ran while one was open for 3% of the time, Pallas kernels for 16%

profile of v2, /device:TPU:0, one launch (start us, length us, event | category | flops | bytes accessed | tf_op | source)
XLA Modules:
  0.0 151.4 jit_solution(13201573922909935817)
XLA Ops:
  0.0 1.4 reshape_squeeze.3.refs_3_.refs_2_
  1.4 12.2 %pack.2 = bf16[32,80,512]{2,1,0:T(8,128)(2,1)} custom-call(s32[2,32]{1,0:T(2,128)} %bitcast.19, bf16[1369,1024]{1,0:T(8,128)(2,1)} %bitcast.13, f32[1024,768]{1,0:T(8,128)} %refs_1_.1, s32[16,128]{1,0:T(8,128)} %reshape_squeeze.3.refs_3_.refs_2_, bf16[32,2,32,64]{3,2,1,0:T(8,128)(2,1)} %bitcast.15), custom_call_target="tpu_custom_call" | custom-call | tf_op jit(solution)/shard_map/pack/pallas_call | solution.py:116
  13.7 7.4 %all-to-all-start = ((bf16[32,80,512]{2,1,0:T(8,128)(2,1)}), bf16[32,80,512]{2,1,0:T(8,128)(2,1)S(1)}, u32[]{:S(2)}, u32[]{:S(2)}) async-start(bf16[32,80,512]{2,1,0:T(8,128)(2,1)} %pack.2), calls=%async_computation | async-start | bytes 5242880 | tf_op jit(solution)/shard_map/all_to_all | solution.py:397
  21.1 0.0 copy-start.13
  21.1 7.4 %pack.3 = bf16[32,64,256]{2,1,0:T(8,128)(2,1)} custom-call(bf16[1369,1024]{1,0:T(8,128)(2,1)} %bitcast.14, f32[1024,768]{1,0:T(8,128)} %refs_1_.1, s32[16,128]{1,0:T(8,128)} %reshape_squeeze.3.refs_3_.refs_2_), custom_call_target="tpu_custom_call" | custom-call | tf_op jit(solution)/shard_map/pack/pallas_call | solution.py:116
  28.5 27.2 %all-to-all-done.rows_ref.weight_ref = bf16[32,80,512]{2,1,0:T(8,128)(2,1)S(1)} async-done(((bf16[32,80,512]{2,1,0:T(8,128)(2,1)}), bf16[32,80,512]{2,1,0:T(8,128)(2,1)S(1)}, u32[]{:S(2)}, u32[]{:S(2)}) %all-to-all-start) | async-done | bytes 2621472 | tf_op jit(solution)/shard_map/all_to_all | solution.py:397
  55.7 4.7 %all-to-all-start.1 = ((bf16[32,64,256]{2,1,0:T(8,128)(2,1)}), bf16[32,64,256]{2,1,0:T(8,128)(2,1)}, u32[]{:S(2)}, u32[]{:S(2)}) async-start(bf16[32,64,256]{2,1,0:T(8,128)(2,1)} %pack.3), calls=%async_computation.1 | async-start | bytes 2097152 | tf_op jit(solution)/shard_map/all_to_all | solution.py:397
  60.4 0.6 copy.22
  61.0 0.5 multiply_exponential_fusion.freq_ref
  61.5 4.7 %position.1.rest_0_.refs_10_ = f32[512,768]{1,0:T(8,128)} custom-call(s32[3,512]{1,0:T(4,128)} %bitcast.18, f32[1,128]{1,0:T(1,128)} %multiply_exponential_fusion.freq_ref), custom_call_target="tpu_custom_call" | custom-call | tf_op jit(solution)/shard_map/position/pallas_call | solution.py:358
  66.3 0.6 slice_convert_fusion
  66.9 6.8 %gather_sums.2 = (bf16[528,512]{1,0:T(8,128)(2,1)}, bf16[528,512]{1,0:T(8,128)(2,1)}, bf16[264,512]{1,0:T(8,128)(2,1)}, bf16[528,512]{1,0:T(8,128)(2,1)}, bf16[264,512]{1,0:T(8,128)(2,1)}) custom-call(s32[32,2]{1,0:T(8,128)} %bitcast.16, s32[1]{0:T(128)} %bitcast.6.me_ref, bf16[32,80,512]{2,1,0:T(8,128)(2,1)} %copy-done, bf16[32,80,512]{2,1,0:T(8,128)(2,1)} %copy-done, ...), custom_call_target="tpu_custom_call" | custom-call | tf_op jit(solution)/shard_map/gather_sums/pallas_call | solution.py:189
  73.8 2.0 %collective-permute-start = (bf16[528,512]{1,0:T(8,128)(2,1)}, bf16[528,512]{1,0:T(8,128)(2,1)S(1)}, u32[]{:S(2)}, u32[]{:S(2)}) collective-permute-start(bf16[528,512]{1,0:T(8,128)(2,1)} %get-tuple-element.20), channel_id=1, source_target_pairs={{0,32},{32,64},{64,96},{96,0},{1,33},{33,65},{65,97},{97,1},{2,34}... | collective-permute-start | bytes 1622024 | tf_op jit(solution)/shard_map/ppermute | solution.py:376
  75.7 1.4 all-to-all-done.1.rows_ref
  77.1 5.5 %gather_sums.3 = (bf16[512,256]{1,0:T(8,128)(2,1)}, bf16[512,256]{1,0:T(8,128)(2,1)}, bf16[256,256]{1,0:T(8,128)(2,1)}, bf16[512,256]{1,0:T(8,128)(2,1)}, bf16[256,256]{1,0:T(8,128)(2,1)}) custom-call(s32[32,2]{1,0:T(8,128)} %bitcast.17, s32[1]{0:T(128)} %bitcast.6.me_ref, bf16[32,64,256]{2,1,0:T(8,128)(2,1)} %all-to-all-done.1.rows_ref, ...), custom_call_target="tpu_custom_call" | custom-call | tf_op jit(solution)/shard_map/gather_sums/pallas_call | solution.py:189
  82.6 1.9 %collective-permute-start.4 = (bf16[512,256]{1,0:T(8,128)(2,1)}, bf16[512,256]{1,0:T(8,128)(2,1)S(1)}, u32[]{:S(2)}, u32[]{:S(2)}) collective-permute-start(bf16[512,256]{1,0:T(8,128)(2,1)} %get-tuple-element.25), channel_id=1, source_target_pairs={{0,32},{32,64},{64,96},{96,0},{1,33},{33,65},{65,97},{97,1},{2,34}... | collective-permute-start | bytes 786440 | tf_op jit(solution)/shard_map/ppermute | solution.py:376
  84.6 2.2 %collective-permute-start.1 = (bf16[528,512]{1,0:T(8,128)(2,1)S(1)}, bf16[528,512]{1,0:T(8,128)(2,1)S(1)}, u32[]{:S(2)}, u32[]{:S(2)}) collective-permute-start(bf16[528,512]{1,0:T(8,128)(2,1)S(1)} %copy-done.14), channel_id=1, source_target_pairs={{32,0},{64,32},{96,64},{0,96},{33,1},{65,33},{97,65},{1,97},{34,2}... | collective-permute-start | bytes 1622024 | tf_op jit(solution)/shard_map/ppermute | solution.py:377
  86.7 2.0 %collective-permute-start.5 = (bf16[512,256]{1,0:T(8,128)(2,1)}, bf16[512,256]{1,0:T(8,128)(2,1)S(1)}, u32[]{:S(2)}, u32[]{:S(2)}) collective-permute-start(bf16[512,256]{1,0:T(8,128)(2,1)} %get-tuple-element.26), channel_id=1, source_target_pairs={{32,0},{64,32},{96,64},{0,96},{33,1},{65,33},{97,65},{1,97},{34,2}... | collective-permute-start | bytes 786440 | tf_op jit(solution)/shard_map/ppermute | solution.py:377
  88.7 7.5 %collective-permute-done.4.refs_6_ = bf16[512,256]{1,0:T(8,128)(2,1)S(1)} collective-permute-done((bf16[512,256]{1,0:T(8,128)(2,1)}, bf16[512,256]{1,0:T(8,128)(2,1)S(1)}, u32[]{:S(2)}, u32[]{:S(2)}) %collective-permute-start.4) | collective-permute-done | bytes 262176 | tf_op jit(solution)/shard_map/ppermute | solution.py:376
  96.2 1.0 add_convert_fusion.3
  97.2 0.1 collective-permute-start.6
  97.3 0.0 collective-permute-done.refs_1_
  97.3 0.0 copy-start.1
  97.4 0.0 copy-done.8
  97.4 0.1 add_convert_fusion.1
  97.4 1.6 %collective-permute-start.2 = (bf16[264,512]{1,0:T(8,128)(2,1)S(1)}, bf16[264,512]{1,0:T(8,128)(2,1)S(1)}, u32[]{:S(2)}, u32[]{:S(2)}) collective-permute-start(bf16[264,512]{1,0:T(8,128)(2,1)S(1)} %add_convert_fusion.1), channel_id=1, source_target_pairs={{0,32},{32,64},{64,96},{96,0},{1,33},{33,65},{65,97},{97,1},{2,34}... | collective-permute-start | bytes 811016 | tf_op jit(solution)/shard_map/ppermute | solution.py:379
  99.0 0.7 collective-permute-done.1.refs_2_
  99.7 0.1 add_convert_fusion
  99.8 3.5 %collective-permute-start.3 = (bf16[264,512]{1,0:T(8,128)(2,1)S(1)}, bf16[264,512]{1,0:T(8,128)(2,1)S(1)}, u32[]{:S(2)}, u32[]{:S(2)}) collective-permute-start(bf16[264,512]{1,0:T(8,128)(2,1)S(1)} %add_convert_fusion), channel_id=1, source_target_pairs={{32,0},{64,32},{96,64},{0,96},{33,1},{65,33},{97,65},{1,97},{34,2}... | collective-permute-start | bytes 811016 | tf_op jit(solution)/shard_map/ppermute | solution.py:379
  103.3 2.0 %collective-permute-done.5.refs_7_ = bf16[512,256]{1,0:T(8,128)(2,1)S(1)} collective-permute-done((bf16[512,256]{1,0:T(8,128)(2,1)}, bf16[512,256]{1,0:T(8,128)(2,1)S(1)}, u32[]{:S(2)}, u32[]{:S(2)}) %collective-permute-start.5) | collective-permute-done | bytes 262176 | tf_op jit(solution)/shard_map/ppermute | solution.py:377
  105.3 1.0 add_convert_fusion.2
  106.4 3.5 %collective-permute-start.7 = (bf16[256,256]{1,0:T(8,128)(2,1)S(1)}, bf16[256,256]{1,0:T(8,128)(2,1)S(1)}, u32[]{:S(2)}, u32[]{:S(2)}) collective-permute-start(bf16[256,256]{1,0:T(8,128)(2,1)S(1)} %add_convert_fusion.2), channel_id=1, source_target_pairs={{32,0},{64,32},{96,64},{0,96},{33,1},{65,33},{97,65},{1,97},{34,2}... | collective-permute-start | bytes 393224 | tf_op jit(solution)/shard_map/ppermute | solution.py:379
  109.8 0.0 collective-permute-done.6.refs_8_
  109.8 3.4 %collective-permute-done.7.refs_9_ = bf16[256,256]{1,0:T(8,128)(2,1)S(1)} collective-permute-done((bf16[256,256]{1,0:T(8,128)(2,1)S(1)}, bf16[256,256]{1,0:T(8,128)(2,1)S(1)}, u32[]{:S(2)}, u32[]{:S(2)}) %collective-permute-start.7) | collective-permute-done | bytes 131104 | tf_op jit(solution)/shard_map/ppermute | solution.py:379
  113.2 0.0 collective-permute-done.2.refs_3_
  113.2 0.0 collective-permute-done.3.refs_4_
  113.3 0.6 copy-done.10
  113.9 0.1 copy-done.5
  114.0 0.1 copy-done.6
  114.1 7.0 %project.1 = (f32[512,768]{1,0:T(8,128)}, bf16[512,768]{1,0:T(8,128)(2,1)}, bf16[512,768]{1,0:T(8,128)(2,1)}, bf16[512,768]{1,0:T(8,128)(2,1)}) custom-call(bf16[528,512]{1,0:T(8,128)(2,1)} %get-tuple-element.19.refs_0_, bf16[528,512]{1,0:T(8,128)(2,1)} %copy-done.1, bf16[528,512]{1,0:T(8,128)(2,1)} %copy-done.2, bf16[264,512]{1,0:T(8,128)(2,1)} %copy-done.5, ...), custom_call_target="tpu_custom_call" | custom-call | tf_op jit(solution)/shard_map/project/pallas_call | solution.py:246
  121.1 0.9 fusion
  122.0 0.1 collective-permute-start.8
  122.1 7.2 %collective-permute-start.9 = (bf16[32,1536]{1,0:T(8,128)(2,1)S(1)}, bf16[32,1536]{1,0:T(8,128)(2,1)S(1)}, u32[]{:S(2)}, u32[]{:S(2)}) collective-permute-start(bf16[32,1536]{1,0:T(8,128)(2,1)S(1)} %pad_maximum_fusion.1), channel_id=1, source_target_pairs={{1,0},{2,1},{3,2},{4,3},{5,4},{6,5},{7,6},{8,7},{9,8},{10,9},{11,1... | collective-permute-start | bytes 294920 | tf_op jit(solution)/shard_map/ppermute | solution.py:423
  129.3 2.2 %collective-permute-done.8.before_ref = bf16[32,1536]{1,0:T(8,128)(2,1)S(1)} collective-permute-done((bf16[32,1536]{1,0:T(8,128)(2,1)S(1)}, bf16[32,1536]{1,0:T(8,128)(2,1)S(1)}, u32[]{:S(2)}, u32[]{:S(2)}) %collective-permute-start.8) | collective-permute-done | bytes 98336 | tf_op jit(solution)/shard_map/ppermute | solution.py:422
  131.5 0.0 collective-permute-done.9.after_ref
  131.5 0.6 copy-done.11
  132.1 0.0 copy-done.12
  132.2 19.0 %attend.1 = bf16[512,768]{1,0:T(8,128)(2,1)} custom-call(f32[512,768]{1,0:T(8,128)} %get-tuple-element.29.stream_ref, bf16[512,768]{1,0:T(8,128)(2,1)} %get-tuple-element.30.q_ref, bf16[512,768]{1,0:T(8,128)(2,1)} %get-tuple-element.31.k_ref, bf16[512,768]{1,0:T(8,128)(2,1)} %get-tuple-element.32.v_ref, bf16[32,1536]{1,0:T(8,128)(2,1)} %copy-done.11, ...), custom_call_target="tpu_custom_call" | custom-call | tf_op jit(solution)/shard_map/attend/pallas_call | solution.py:324
  (24 shorter events, 0.1 us)
Async XLA Ops:
  13.7 42.0 %all-to-all-start = ((bf16[32,80,512]{2,1,0:T(8,128)(2,1)}), bf16[32,80,512]{2,1,0:T(8,128)(2,1)S(1)}, u32[]{:S(2)}, u32[]{:S(2)}) async-start(bf16[32,80,512]{2,1,0:T(8,128)(2,1)} %pack.2), calls=%async_computation | async-start | bytes 5242880 | tf_op jit(solution)/shard_map/all_to_all | solution.py:397
  21.1 39.3 %copy-start.13 = (s32[1,1,3,512]{3,1,2,0:T(1,128)S(1)}, s32[1,1,3,512]{3,1,2,0:T(1,128)}, u32[]{:S(2)}) copy-start(s32[1,1,3,512]{3,1,2,0:T(1,128)} %param.16) | copy-start | bytes 18436
  55.7 11.2 %copy-start = (bf16[32,80,512]{2,1,0:T(8,128)(2,1)}, bf16[32,80,512]{2,1,0:T(8,128)(2,1)S(1)}, u32[]{:S(2)}) copy-start(bf16[32,80,512]{2,1,0:T(8,128)(2,1)S(1)} %all-to-all-done.rows_ref.weight_ref) | copy-start | bytes 7864324
  55.7 21.4 %all-to-all-start.1 = ((bf16[32,64,256]{2,1,0:T(8,128)(2,1)}), bf16[32,64,256]{2,1,0:T(8,128)(2,1)}, u32[]{:S(2)}, u32[]{:S(2)}) async-start(bf16[32,64,256]{2,1,0:T(8,128)(2,1)} %pack.3), calls=%async_computation.1 | async-start | bytes 2097152 | tf_op jit(solution)/shard_map/all_to_all | solution.py:397
  73.7 10.8 %copy-start.14 = (bf16[528,512]{1,0:T(8,128)(2,1)S(1)}, bf16[528,512]{1,0:T(8,128)(2,1)}, u32[]{:S(2)}) copy-start(bf16[528,512]{1,0:T(8,128)(2,1)} %get-tuple-element.21) | copy-start | bytes 1622020
  73.7 23.6 %copy-start.8 = (bf16[264,512]{1,0:T(8,128)(2,1)S(1)}, bf16[264,512]{1,0:T(8,128)(2,1)}, u32[]{:S(2)}) copy-start(bf16[264,512]{1,0:T(8,128)(2,1)} %get-tuple-element.22) | copy-start | bytes 811012
  73.7 26.0 %copy-start.7 = (bf16[264,512]{1,0:T(8,128)(2,1)S(1)}, bf16[264,512]{1,0:T(8,128)(2,1)}, u32[]{:S(2)}) copy-start(bf16[264,512]{1,0:T(8,128)(2,1)} %get-tuple-element.23) | copy-start | bytes 811012
  73.8 23.6 %collective-permute-start = (bf16[528,512]{1,0:T(8,128)(2,1)}, bf16[528,512]{1,0:T(8,128)(2,1)S(1)}, u32[]{:S(2)}, u32[]{:S(2)}) collective-permute-start(bf16[528,512]{1,0:T(8,128)(2,1)} %get-tuple-element.20), channel_id=1, source_target_pairs={{0,32},{32,64},{64,96},{96,0},{1,33},{33,65},{65,97},{97,1},{2,34}... | collective-permute-start | bytes 1622024 | tf_op jit(solution)/shard_map/ppermute | solution.py:376
  82.6 13.6 %collective-permute-start.4 = (bf16[512,256]{1,0:T(8,128)(2,1)}, bf16[512,256]{1,0:T(8,128)(2,1)S(1)}, u32[]{:S(2)}, u32[]{:S(2)}) collective-permute-start(bf16[512,256]{1,0:T(8,128)(2,1)} %get-tuple-element.25), channel_id=1, source_target_pairs={{0,32},{32,64},{64,96},{96,0},{1,33},{33,65},{65,97},{97,1},{2,34}... | collective-permute-start | bytes 786440 | tf_op jit(solution)/shard_map/ppermute | solution.py:376
  84.6 15.1 %collective-permute-start.1 = (bf16[528,512]{1,0:T(8,128)(2,1)S(1)}, bf16[528,512]{1,0:T(8,128)(2,1)S(1)}, u32[]{:S(2)}, u32[]{:S(2)}) collective-permute-start(bf16[528,512]{1,0:T(8,128)(2,1)S(1)} %copy-done.14), channel_id=1, source_target_pairs={{32,0},{64,32},{96,64},{0,96},{33,1},{65,33},{97,65},{1,97},{34,2}... | collective-permute-start | bytes 1622024 | tf_op jit(solution)/shard_map/ppermute | solution.py:377
  86.7 18.6 %collective-permute-start.5 = (bf16[512,256]{1,0:T(8,128)(2,1)}, bf16[512,256]{1,0:T(8,128)(2,1)S(1)}, u32[]{:S(2)}, u32[]{:S(2)}) collective-permute-start(bf16[512,256]{1,0:T(8,128)(2,1)} %get-tuple-element.26), channel_id=1, source_target_pairs={{32,0},{64,32},{96,64},{0,96},{33,1},{65,33},{97,65},{1,97},{34,2}... | collective-permute-start | bytes 786440 | tf_op jit(solution)/shard_map/ppermute | solution.py:377
  96.2 17.1 %copy-start.3 = (bf16[512,256]{1,0:T(8,128)(2,1)}, bf16[512,256]{1,0:T(8,128)(2,1)S(1)}, u32[]{:S(2)}) copy-start(bf16[512,256]{1,0:T(8,128)(2,1)S(1)} %collective-permute-done.4.refs_6_) | copy-start | bytes 786436
  97.2 12.6 %collective-permute-start.6 = (bf16[256,256]{1,0:T(8,128)(2,1)S(1)}, bf16[256,256]{1,0:T(8,128)(2,1)S(1)}, u32[]{:S(2)}, u32[]{:S(2)}) collective-permute-start(bf16[256,256]{1,0:T(8,128)(2,1)S(1)} %add_convert_fusion.3), channel_id=1, source_target_pairs={{0,32},{32,64},{64,96},{96,0},{1,33},{33,65},{65,97},{97,1},{2,34}... | collective-permute-start | bytes 393224 | tf_op jit(solution)/shard_map/ppermute | solution.py:379
  97.3 15.9 %copy-start.1 = (bf16[528,512]{1,0:T(8,128)(2,1)}, bf16[528,512]{1,0:T(8,128)(2,1)S(1)}, u32[]{:S(2)}) copy-start(bf16[528,512]{1,0:T(8,128)(2,1)S(1)} %collective-permute-done.refs_1_) | copy-start | bytes 1622020
  97.4 15.8 %collective-permute-start.2 = (bf16[264,512]{1,0:T(8,128)(2,1)S(1)}, bf16[264,512]{1,0:T(8,128)(2,1)S(1)}, u32[]{:S(2)}, u32[]{:S(2)}) collective-permute-start(bf16[264,512]{1,0:T(8,128)(2,1)S(1)} %add_convert_fusion.1), channel_id=1, source_target_pairs={{0,32},{32,64},{64,96},{96,0},{1,33},{33,65},{65,97},{97,1},{2,34}... | collective-permute-start | bytes 811016 | tf_op jit(solution)/shard_map/ppermute | solution.py:379
  99.7 13.6 %copy-start.2 = (bf16[528,512]{1,0:T(8,128)(2,1)}, bf16[528,512]{1,0:T(8,128)(2,1)S(1)}, u32[]{:S(2)}) copy-start(bf16[528,512]{1,0:T(8,128)(2,1)S(1)} %collective-permute-done.1.refs_2_) | copy-start | bytes 1622020
  99.8 13.4 %collective-permute-start.3 = (bf16[264,512]{1,0:T(8,128)(2,1)S(1)}, bf16[264,512]{1,0:T(8,128)(2,1)S(1)}, u32[]{:S(2)}, u32[]{:S(2)}) collective-permute-start(bf16[264,512]{1,0:T(8,128)(2,1)S(1)} %add_convert_fusion), channel_id=1, source_target_pairs={{32,0},{64,32},{96,64},{0,96},{33,1},{65,33},{97,65},{1,97},{34,2}... | collective-permute-start | bytes 811016 | tf_op jit(solution)/shard_map/ppermute | solution.py:379
  105.3 8.0 %copy-start.4 = (bf16[512,256]{1,0:T(8,128)(2,1)}, bf16[512,256]{1,0:T(8,128)(2,1)S(1)}, u32[]{:S(2)}) copy-start(bf16[512,256]{1,0:T(8,128)(2,1)S(1)} %collective-permute-done.5.refs_7_) | copy-start | bytes 786436
  106.4 6.9 %collective-permute-start.7 = (bf16[256,256]{1,0:T(8,128)(2,1)S(1)}, bf16[256,256]{1,0:T(8,128)(2,1)S(1)}, u32[]{:S(2)}, u32[]{:S(2)}) collective-permute-start(bf16[256,256]{1,0:T(8,128)(2,1)S(1)} %add_convert_fusion.2), channel_id=1, source_target_pairs={{32,0},{64,32},{96,64},{0,96},{33,1},{65,33},{97,65},{1,97},{34,2}... | collective-permute-start | bytes 393224 | tf_op jit(solution)/shard_map/ppermute | solution.py:379
  109.8 3.5 %copy-start.9 = (bf16[256,256]{1,0:T(8,128)(2,1)}, bf16[256,256]{1,0:T(8,128)(2,1)S(1)}, u32[]{:S(2)}) copy-start(bf16[256,256]{1,0:T(8,128)(2,1)S(1)} %collective-permute-done.6.refs_8_) | copy-start | bytes 393220
  113.2 0.7 copy-start.10
  113.2 0.8 copy-start.5
  113.3 0.8 copy-start.6
  122.0 9.5 %collective-permute-start.8 = (bf16[32,1536]{1,0:T(8,128)(2,1)S(1)}, bf16[32,1536]{1,0:T(8,128)(2,1)S(1)}, u32[]{:S(2)}, u32[]{:S(2)}) collective-permute-start(bf16[32,1536]{1,0:T(8,128)(2,1)S(1)} %pad_maximum_fusion), channel_id=1, source_target_pairs={{0,1},{1,2},{2,3},{3,4},{4,5},{5,6},{6,7},{7,8},{8,9},{9,10},{10,1... | collective-permute-start | bytes 294920 | tf_op jit(solution)/shard_map/ppermute | solution.py:422
  122.1 9.4 %collective-permute-start.9 = (bf16[32,1536]{1,0:T(8,128)(2,1)S(1)}, bf16[32,1536]{1,0:T(8,128)(2,1)S(1)}, u32[]{:S(2)}, u32[]{:S(2)}) collective-permute-start(bf16[32,1536]{1,0:T(8,128)(2,1)S(1)} %pad_maximum_fusion.1), channel_id=1, source_target_pairs={{1,0},{2,1},{3,2},{4,3},{5,4},{6,5},{7,6},{8,7},{9,8},{10,9},{11,1... | collective-permute-start | bytes 294920 | tf_op jit(solution)/shard_map/ppermute | solution.py:423
  131.5 0.6 copy-start.11
  131.5 0.7 copy-start.12

commit v3 on v2

--- a/solution.py
+++ b/solution.py
@@ -13,130 +13,131 @@
 F32 = jnp.float32
 BF16 = jnp.bfloat16
 EXTRA = 16
-VMEM_LIMIT = 60 * 1024 * 1024
 VM = pl.BlockSpec(memory_space=pltpu.VMEM)
 ANY = pl.BlockSpec(memory_space=pl.ANY)
 
 
-def params(**kw):
-    return pltpu.CompilerParams(vmem_limit_bytes=VMEM_LIMIT, **kw)
+def params(megabytes, **kw):
+    return pltpu.CompilerParams(vmem_limit_bytes=megabytes * 1024 * 1024, **kw)
 
 
 def dot(a, b):
     return lax.dot_general(a, b, (((1,), (0,)), ((), ())), preferred_element_type=F32)
 
 
-def pack_kernel(patches, row_step, per_step, weighted, *refs):
+def pack_kernel(start, per_step, weighted, *refs):
     if weighted:
-        ids_ref, feat_ref, win_ref, idx_ref, lift_ref, out_ref, table, places, high, low = refs
+        ids_ref, feat_hbm, win_hbm, idx_ref, lift_ref, out_hbm = refs[:6]
     else:
-        feat_ref, win_ref, idx_ref, out_ref, table, places, high, low = refs
+        feat_hbm, win_hbm, idx_ref, out_hbm = refs[:4]
+    feat, win, table, places, packed, feat_sems, win_sem, out_sems = refs[-8:]
+    patches = feat.shape[0]
     table_rows, width = table.shape
-    step = pl.program_id(0)
-    row_steps = -(-patches // row_step)
-
-    @pl.when(step == 0)
-    def _():
-        high[...] = win_ref[...].astype(BF16)
-        low[...] = (win_ref[...] - high[...].astype(F32)).astype(BF16)
-        turned = jnp.transpose(idx_ref[...].astype(F32)).astype(jnp.int32)
-        for i in range(turned.shape[1]):
-            places[i * 128 : (i + 1) * 128, :] = turned[:, i : i + 1]
-
-    for s in range(row_steps):
-
-        @pl.when(step == s)
-        def _(s=s):
-            start = s * row_step
-            keep = min(row_step, table_rows - start)
-            rows = feat_ref[:keep, :]
-            values = (dot(rows, high[...]) + dot(rows, low[...])).astype(BF16)
-            if start + keep > patches:
-                live = lax.broadcasted_iota(jnp.int32, (keep, width), 0) < patches - start
-                values = jnp.where(live, values, jnp.zeros_like(values))
-            table[start : start + keep, :] = values
-
-    @pl.when(step >= row_steps)
-    def _():
-        base = step - row_steps
-        each = places.shape[0] // (per_step * (pl.num_programs(0) - row_steps))
-        count = per_step * each
+    segments = packed.shape[0]
+    count = per_step * (places.shape[0] // segments)
+    each = count // per_step
+    row_step = 256
+
+    win_copy = pltpu.make_async_copy(win_hbm.at[:, start : start + width], win, win_sem)
+    win_copy.start()
+    spans = [slice(s, min(s + row_step, patches)) for s in range(0, patches, row_step)]
+    feat_copies = [
+        pltpu.make_async_copy(feat_hbm.at[span, :], feat.at[span, :], feat_sems.at[i])
+        for i, span in enumerate(spans)
+    ]
+    for copy in feat_copies:
+        copy.start()
+    turned = jnp.transpose(idx_ref[...].astype(F32)).astype(jnp.int32)
+    for i in range(turned.shape[1]):
+        places[i * 128 : (i + 1) * 128, :] = turned[:, i : i + 1]
+    table[spans[-1].start :, :] = jnp.zeros((table_rows - spans[-1].start, width), BF16)
+    win_copy.wait()
+    weights = win[...].astype(BF16)
+    for copy, span in zip(feat_copies, spans):
+        copy.wait()
+        table[span, :] = dot(feat[span, :], weights).astype(BF16)
+
+    def out_copy(base):
+        own = pl.ds(base * per_step, per_step)
+        return pltpu.make_async_copy(packed.at[own], out_hbm.at[own], out_sems.at[base])
+
+    def pick(base, carry):
         spot = places[pl.ds(pl.multiple_of(base * count, count), count), :]
         picked = lax.broadcasted_iota(jnp.int32, (count, table_rows), 1) == spot
         rows = dot(picked.astype(F32).astype(BF16), table[...]).astype(BF16)
         for i in range(per_step):
-            out_ref[i, :each, :] = rows[i * each : (i + 1) * each, :]
+            segment = base * per_step + i
+            packed[segment, :each, :] = rows[i * each : (i + 1) * each, :]
             if weighted:
                 slots, _, block = lift_ref.shape[1:]
-                both = jnp.concatenate([lift_ref[i, c].astype(F32) for c in range(slots)], axis=1)
+                both = jnp.concatenate(
+                    [lift_ref[segment, c].astype(F32) for c in range(slots)], axis=1
+                )
                 turned = jnp.transpose(both)
                 for c in range(slots):
                     groups = [
                         turned[c * block + g * EXTRA : c * block + (g + 1) * EXTRA, :]
                         for g in range(block // EXTRA)
                     ]
-                    out_ref[i, each:, c * 128 : (c + 1) * 128] = jnp.concatenate(
+                    packed[segment, each:, c * 128 : (c + 1) * 128] = jnp.concatenate(
                         groups, axis=1
                     ).astype(BF16)
                 lane = lax.broadcasted_iota(jnp.int32, (EXTRA, 128), 1)
                 marks = jnp.zeros((EXTRA, 128), jnp.int32)
                 for c in range(slots):
-                    marks = jnp.where(lane == c, ids_ref[c, base * per_step + i], marks)
-                out_ref[i, each:, slots * 128 : (slots + 1) * 128] = marks.astype(F32).astype(BF16)
-                out_ref[i, each:, (slots + 1) * 128 :] = jnp.zeros(
+                    marks = jnp.where(lane == c, ids_ref[c, segment], marks)
+                packed[segment, each:, slots * 128 : (slots + 1) * 128] = marks.astype(F32).astype(BF16)
+                packed[segment, each:, (slots + 1) * 128 :] = jnp.zeros(
                     (EXTRA, width - (slots + 1) * 128), BF16
                 )
+        out_copy(base).start()
+        return carry
+
+    steps = segments // per_step
+    lax.fori_loop(0, steps, pick, 0)
+    for base in range(steps):
+        out_copy(base).wait()
 
 
 def pack(features, w_in, indices, segments, start, width, ids=None, lift=None):
     patches, channels = features.shape
     count = indices.shape[0] * indices.shape[1]
-    each = count // segments
-    per_step, row_step = 8, 512
-    row_steps = -(-patches // row_step)
-    table_rows = -(-patches // 128) * 128
+    per_step = 8
     weighted = lift is not None
-
-    def later(i):
-        return jnp.maximum(i - row_steps, 0)
-
-    in_specs = [
-        pl.BlockSpec((row_step, channels), lambda i, *_: (jnp.minimum(i, row_steps - 1), 0)),
-        pl.BlockSpec((channels, width), lambda i, *_: (0, start // width)),
-        pl.BlockSpec(indices.shape, lambda i, *_: (0, 0)),
-    ]
-    operands = [features, w_in, indices]
-    rows = each
+    rows = count // segments + (EXTRA if weighted else 0)
+    operands, in_specs = [features, w_in, indices], [ANY, ANY, VM]
     if weighted:
-        in_specs.append(
-            pl.BlockSpec((per_step,) + lift.shape[1:], lambda i, *_: (later(i), 0, 0, 0))
-        )
         operands = [ids] + operands + [lift]
-        rows += EXTRA
+        in_specs = [pl.BlockSpec(memory_space=pltpu.SMEM)] + in_specs + [VM]
     return pl.pallas_call(
-        functools.partial(pack_kernel, patches, row_step, per_step, weighted),
-        grid_spec=pltpu.PrefetchScalarGridSpec(
-            num_scalar_prefetch=int(weighted),
-            grid=(row_steps + segments // per_step,),
-            in_specs=in_specs,
-            out_specs=pl.BlockSpec((per_step, rows, width), lambda i, *_: (later(i), 0, 0)),
-            scratch_shapes=[
-                pltpu.VMEM((table_rows, width), BF16),
-                pltpu.VMEM((count, 1), jnp.int32),
-                pltpu.VMEM((channels, width), BF16),
-                pltpu.VMEM((channels, width), BF16),
-            ],
-        ),
+        functools.partial(pack_kernel, start, per_step, weighted),
+        in_specs=in_specs,
+        out_specs=ANY,
+        scratch_shapes=[
+            pltpu.VMEM((patches, channels), BF16),
+            pltpu.VMEM((channels, width), F32),
+            pltpu.VMEM((-(-patches // 128) * 128, width), BF16),
+            pltpu.VMEM((count, 1), jnp.int32),
+            pltpu.VMEM((segments, rows, width), BF16),
+            pltpu.SemaphoreType.DMA((-(-patches // 256),)),
+            pltpu.SemaphoreType.DMA(()),
+            pltpu.SemaphoreType.DMA((segments // per_step,)),
+        ],
         out_shape=jax.ShapeDtypeStruct((segments, rows, width), BF16),
-        compiler_params=params(dimension_semantics=("arbitrary",)),
+        compiler_params=params(60),
         name="pack",
     )(*operands)
 
 
 def gather_sums_kernel(block, picks, half_blocks, counted, ids_ref, me_ref, rows_ref, weight_ref, *rest):
     outs, total = rest[-6:-1], rest[-1]
-    total[...] = jnp.zeros_like(total)
+    step = pl.program_id(0)
     views, _, width = rows_ref.shape
+
+    @pl.when(step == 0)
+    def _():
+        total[...] = jnp.zeros_like(total)
+
     slots = ids_ref.shape[1]
     size = outs[2].shape[0]
     parts = 8
@@ -152,7 +153,7 @@
         right = jnp.concatenate([rows[c] for c in range(slots) for _ in range(4)], axis=0)
         lifted = dot(left, right)
         for c in range(slots):
-            name = ids_ref[j, c]
+            name = ids_ref[step * views + j, c]
             owner = name // (2 * half_blocks)
             within = name - owner * (2 * half_blocks)
             half = within // half_blocks
@@ -170,15 +171,17 @@
 
     lax.fori_loop(0, views, add_view, 0, unroll=4)
 
-    def part(away, half):
-        first = (away * 2 + half) * size
-        return total[first : first + size, :].astype(BF16)
-
-    own, up_first, up_last, down_first, down_last = outs
-    up_first[:size, :], up_first[size:, :] = part(1, 1), part(2, 0)
-    down_first[:size, :], down_first[size:, :] = part(3, 0), part(2, 1)
-    up_last[...], down_last[...] = part(1, 0), part(3, 1)
-    own[:size, :], own[size:, :] = part(0, 0), part(0, 1)
+    @pl.when(step == pl.num_programs(0) - 1)
+    def _():
+        def part(away, half):
+            first = (away * 2 + half) * size
+            return total[first : first + size, :].astype(BF16)
+
+        own, up_first, up_last, down_first, down_last = outs
+        up_first[:size, :], up_first[size:, :] = part(1, 1), part(2, 0)
+        down_first[:size, :], down_first[size:, :] = part(3, 0), part(2, 1)
+        up_last[...], down_last[...] = part(1, 0), part(3, 1)
+        own[:size, :], own[size:, :] = part(0, 0), part(0, 1)
 
 
 def gather_sums(ids, me, rows, weights, block, picks, half_blocks, counted, *after):
@@ -190,17 +193,17 @@
         functools.partial(gather_sums_kernel, block, picks, half_blocks, counted),
         grid_spec=pltpu.PrefetchScalarGridSpec(
             num_scalar_prefetch=2,
-            grid=(1,),
+            grid=(views // 8,),
             in_specs=[
-                pl.BlockSpec((views, count, width), lambda i, *_: (0, 0, 0)),
-                pl.BlockSpec((views, EXTRA, weights.shape[2]), lambda i, *_: (0, count // EXTRA, 0)),
+                pl.BlockSpec((8, count, width), lambda i, *_: (i, 0, 0)),
+                pl.BlockSpec((8, EXTRA, weights.shape[2]), lambda i, *_: (i, count // EXTRA, 0)),
             ]
             + [ANY] * len(after),
             out_specs=[pl.BlockSpec((s, width), lambda i, *_: (0, 0)) for s in sizes],
             scratch_shapes=[pltpu.VMEM((8 * size + block + 8, width), F32)],
         ),
         out_shape=[jax.ShapeDtypeStruct((s, width), BF16) for s in sizes],
-        compiler_params=params(dimension_semantics=("arbitrary",)),
+        compiler_params=params(24, dimension_semantics=("arbitrary",)),
         name="gather_sums",
     )(ids, me, rows, weights, *after)
 
@@ -249,24 +252,18 @@
         out_specs=[VM] * 4,
         out_shape=[jax.ShapeDtypeStruct((rows, width), F32)]
         + [jax.ShapeDtypeStruct((rows, width), BF16)] * 3,
-        compiler_params=params(),
+        compiler_params=params(24),
         name="project",
     )(*sums, pos, w_query, w_key, w_value)
 
 
 def attend_kernel(
-    block, stream_ref, q_ref, k_ref, v_ref, before_ref, after_ref, wout_ref, wup_hbm, wdown_hbm,
-    out_ref, qx, kx, vx, mixed, attended, normed, total, wup, wdown, sems,
+    block, stream_ref, q_ref, k_ref, v_ref, before_ref, after_ref, wout_ref, wup, wdown,
+    out_ref, qx, kx, vx, mixed, normed, total,
 ):
     rows, width = stream_ref.shape
     half = block // 2
     hidden_width = wup.shape[1]
-    copies = [
-        pltpu.make_async_copy(wup_hbm, wup, sems.at[0]),
-        pltpu.make_async_copy(wdown_hbm, wdown, sems.at[1]),
-    ]
-    for c in copies:
-        c.start()
     qx[:half, :] = jnp.zeros((half, width), BF16)
     qx[half : half + rows, :] = q_ref[...]
     qx[half + rows :, :] = jnp.zeros((half, width), BF16)
@@ -294,48 +291,36 @@
             mixed[span, lanes] = jnp.where(low_lanes, out[:block], out[block:]).astype(BF16)
         return carry
 
-    lax.fori_loop(0, (rows + block) // block, window, 0)
+    lax.fori_loop(0, (rows + block) // block, window, 0, unroll=3)
 
     step = 256
     for start in range(0, rows, step):
         values = stream_ref[start : start + step, :] + dot(
             mixed[half + start : half + start + step, :], wout_ref[...]
         )
-        attended[start : start + step, :] = values
+        total[start : start + step, :] = values
         normed[start : start + step, :] = normalize(values)
-    total[...] = attended[...]
-    for c in copies:
-        c.wait()
-    chunk = 512
-
-    def feed(i, carry):
-        cols = pl.ds(pl.multiple_of(i * chunk, chunk), chunk)
+    chunk = 768
+    for i in range(hidden_width // chunk):
+        cols = slice(i * chunk, (i + 1) * chunk)
         hidden = jax.nn.gelu(dot(normed[...], wup[:, cols]), approximate=True).astype(BF16)
         total[...] += dot(hidden, wdown[cols, :])
-        return carry
-
-    lax.fori_loop(0, hidden_width // chunk, feed, 0)
     out_ref[...] = total[...].astype(BF16)
 
 
 def attend(stream, query, keys, values, before, after, w_out, w_up, w_down, block):
     rows, width = stream.shape
-    hidden_width = w_up.shape[1]
     return pl.pallas_call(
         functools.partial(attend_kernel, block),
-        in_specs=[VM] * 7 + [ANY] * 2,
+        in_specs=[VM] * 9,
         out_specs=VM,
         out_shape=jax.ShapeDtypeStruct((rows, width), BF16),
         scratch_shapes=[pltpu.VMEM((rows + block, width), BF16)] * 4
         + [
-            pltpu.VMEM((rows, width), F32),
             pltpu.VMEM((rows, width), BF16),
             pltpu.VMEM((rows, width), F32),
-            pltpu.VMEM((width, hidden_width), BF16),
-            pltpu.VMEM((hidden_width, width), BF16),
-            pltpu.SemaphoreType.DMA((2,)),
         ],
-        compiler_params=params(),
+        compiler_params=params(30),
         name="attend",
     )(stream, query, keys, values, before, after, w_out, w_up, w_down)
 
@@ -360,7 +345,7 @@
         in_specs=[VM] * 2,
         out_specs=VM,
         out_shape=jax.ShapeDtypeStruct((places.shape[1], model_width), F32),
-        compiler_params=params(),
+        compiler_params=params(16),
         name="position",
     )(places, frequency[None, :])
 

time: 152 us -> 138 us (0.908)
  Pallas kernels: 62.8 us -> 46.1 us
  waiting for transfers between devices: 44.4 us -> 47.6 us
  other arithmetic: 3.38 us -> 1.21 us
  local copies, waits for them, and re-layouts: 4.4 us -> 6.15 us
    pallas_call x3, Pallas kernels: 38.7 us -> 30.8 us  [the longest x2 19.8 us: pack(): pl.pallas_call(functools.partial(pack_kernel, start, per_step, weighted),...]
    pallas_call x1, Pallas kernels: 6.99 us -> 2.4 us  [project(): pl.pallas_call(functools.partial(project_kernel, block, half_blocks), in_...]
    ppermute x2, waiting for transfers between devices: 2.75 us -> 5.52 us  [share(): from_above = lax.ppermute(down_first, axis, down)]
    ppermute x2, waiting for transfers between devices: 7.52 us -> 4.85 us  [share(): from_below = lax.ppermute(up_first, axis, up)]
    unnamed x31 -> x29, local copies, waits for them, and re-layouts: 2.07 us -> 4.68 us
    pallas_call x2, Pallas kernels: 12.4 us -> 10 us  [gather_sums(): pl.pallas_call(functools.partial(gather_sums_kernel, block, picks, half_b...]
    all_to_all x2, waiting for transfers between devices: 28.5 us -> 30.6 us  [send(): lax.all_to_all(payload, 'seg', split_axis=0, concat_axis=0, tiled=True)]
    pallas_call x1, Pallas kernels: 4.75 us -> 2.89 us  [position_code(): pl.pallas_call(position_kernel, in_specs=[VM] * 2, out_specs=VM, out_shap...]
  transfers between devices with their start and end apart: 12 -> 12, of which waited for: 7 -> 7; matrix products, arithmetic and copies ran while one was open for 3% -> 1% of each run, Pallas kernels for 16% -> 16%
where the time goes in v3:
time: 138 us
  waiting for transfers between devices  47.6 us (34%)
  Pallas kernels  46.1 us (33%)
  starting transfers between devices  36.2 us (26%)
  local copies, waits for them, and re-layouts  6.15 us (4%)
    all_to_all x2, waiting for transfers between devices, send(): lax.all_to_all(payload, 'seg', split_axis=0, concat_axis=0, tiled=True)  30.6 us
    pallas_call x2, Pallas kernels, pack(): pl.pallas_call(functools.partial(pack_kernel, start, per_step, weighted),...  19.8 us
    all_to_all x2, starting transfers between devices, send(): lax.all_to_all(payload, 'seg', split_axis=0, concat_axis=0, tiled=True)  12.1 us
    pallas_call x1, Pallas kernels, attend(): pl.pallas_call(functools.partial(attend_kernel, block), in_specs=[VM] * 9...  10.9 us
    pallas_call x2, Pallas kernels, gather_sums(): pl.pallas_call(functools.partial(gather_sums_kernel, block, picks, half_b...  10 us
    ppermute x1, starting transfers between devices, shards(): after = lax.ppermute(first, ('view', 'seg'), ring_down)  7.22 us
    ppermute x2, starting transfers between devices, share(): lax.ppermute(down_last, axis, down)  6.96 us
    ppermute x2, waiting for transfers between devices, share(): from_above = lax.ppermute(down_first, axis, down)  5.52 us
  transfers between devices with their start and end apart: 12, of which 7 were waited for; matrix products, arithmetic and copies ran while one was open for 1% of the time, Pallas kernels for 16%

profile of v3, /device:TPU:0, one launch (start us, length us, event | category | flops | bytes accessed | tf_op | source)
XLA Modules:
  0.0 137.5 jit_solution(16815551789388563687)
XLA Ops:
  0.0 1.4 %reshape_squeeze.3.refs_3_.refs_2_ = s32[16,128]{1,0:T(8,128)} reshape(s32[1,32,2,32]{3,2,1,0:T(2,128)} %param.14) | data formatting | bytes 16384 | tf_op jit(solution)/shard_map/reshape;squeeze | solution.py:379
  1.4 11.3 %pack.2 = bf16[32,80,512]{2,1,0:T(8,128)(2,1)} custom-call(s32[2,32]{1,0:T(2,128)} %bitcast.21, bf16[1369,1024]{1,0:T(8,128)(2,1)} %bitcast.18, f32[1024,768]{1,0:T(8,128)} %refs_1_.1, s32[16,128]{1,0:T(8,128)} %reshape_squeeze.3.refs_3_.refs_2_, bf16[32,2,32,64]{3,2,1,0:T(8,128)(2,1)} %bitcast.20), custom_call_target="tpu_custom_call" | custom-call | tf_op jit(solution)/shard_map/pack/pallas_call | solution.py:112
  12.8 7.4 %all-to-all-start = ((bf16[32,80,512]{2,1,0:T(8,128)(2,1)}), bf16[32,80,512]{2,1,0:T(8,128)(2,1)S(1)}, u32[]{:S(2)}, u32[]{:S(2)}) async-start(bf16[32,80,512]{2,1,0:T(8,128)(2,1)} %pack.2), calls=%async_computation | async-start | bytes 5242880 | tf_op jit(solution)/shard_map/all_to_all | solution.py:382
  20.2 0.0 copy-start.11
  20.2 8.5 %pack.3 = bf16[32,64,256]{2,1,0:T(8,128)(2,1)} custom-call(bf16[1369,1024]{1,0:T(8,128)(2,1)} %bitcast.19, f32[1024,768]{1,0:T(8,128)} %refs_1_.1, s32[16,128]{1,0:T(8,128)} %reshape_squeeze.3.refs_3_.refs_2_), custom_call_target="tpu_custom_call" | custom-call | tf_op jit(solution)/shard_map/pack/pallas_call | solution.py:112
  28.7 26.1 %all-to-all-done.rows_ref.weight_ref = bf16[32,80,512]{2,1,0:T(8,128)(2,1)S(1)} async-done(((bf16[32,80,512]{2,1,0:T(8,128)(2,1)}), bf16[32,80,512]{2,1,0:T(8,128)(2,1)S(1)}, u32[]{:S(2)}, u32[]{:S(2)}) %all-to-all-start) | async-done | bytes 2621472 | tf_op jit(solution)/shard_map/all_to_all | solution.py:382
  54.8 4.7 %all-to-all-start.1 = ((bf16[32,64,256]{2,1,0:T(8,128)(2,1)}), bf16[32,64,256]{2,1,0:T(8,128)(2,1)}, u32[]{:S(2)}, u32[]{:S(2)}) async-start(bf16[32,64,256]{2,1,0:T(8,128)(2,1)} %pack.3), calls=%async_computation.1 | async-start | bytes 2097152 | tf_op jit(solution)/shard_map/all_to_all | solution.py:382
  59.5 2.9 %position.1.rest_0_.refs_10_ = f32[512,768]{1,0:T(8,128)S(1)} custom-call(s32[3,512]{1,0:T(4,128)S(1)} %bitcast.17, f32[1,128]{1,0:T(1,128)S(1)} %multiply_exponential_fusion.freq_ref), custom_call_target="tpu_custom_call" | custom-call | tf_op jit(solution)/shard_map/position/pallas_call | solution.py:343
  62.5 5.0 %gather_sums.2 = (bf16[528,512]{1,0:T(8,128)(2,1)S(1)}, bf16[528,512]{1,0:T(8,128)(2,1)}, bf16[264,512]{1,0:T(8,128)(2,1)S(1)}, bf16[528,512]{1,0:T(8,128)(2,1)S(1)}, bf16[264,512]{1,0:T(8,128)(2,1)S(1)}) custom-call(s32[32,2]{1,0:T(8,128)S(1)} %bitcast.15, s32[1]{0:T(128)} %bitcast.6.me_ref, bf16[32,80,512]{2,1,0:T(8,128)(2,1)S(1)} %all-to-all-done.rows_ref.weight_ref, ...), custom_call_target="tpu_custom_call" | custom-call | tf_op jit(solution)/shard_map/gather_sums/pallas_call | solution.py:192
  67.5 0.8 copy-done.7
  68.3 0.7 copy-done.9
  69.0 0.8 copy-done.10
  69.8 1.9 %collective-permute-start = (bf16[528,512]{1,0:T(8,128)(2,1)}, bf16[528,512]{1,0:T(8,128)(2,1)S(1)}, u32[]{:S(2)}, u32[]{:S(2)}) collective-permute-start(bf16[528,512]{1,0:T(8,128)(2,1)} %get-tuple-element.20), channel_id=1, source_target_pairs={{0,32},{32,64},{64,96},{96,0},{1,33},{33,65},{65,97},{97,1},{2,34}... | collective-permute-start | bytes 1622024 | tf_op jit(solution)/shard_map/ppermute | solution.py:361
  71.7 4.5 %all-to-all-done.1.rows_ref = bf16[32,64,256]{2,1,0:T(8,128)(2,1)} async-done(((bf16[32,64,256]{2,1,0:T(8,128)(2,1)}), bf16[32,64,256]{2,1,0:T(8,128)(2,1)}, u32[]{:S(2)}, u32[]{:S(2)}) %all-to-all-start.1) | async-done | bytes 1048608 | tf_op jit(solution)/shard_map/all_to_all | solution.py:382
  76.2 0.0 copy-start.8
  76.2 5.0 %gather_sums.3 = (bf16[512,256]{1,0:T(8,128)(2,1)S(1)}, bf16[512,256]{1,0:T(8,128)(2,1)S(1)}, bf16[256,256]{1,0:T(8,128)(2,1)S(1)}, bf16[512,256]{1,0:T(8,128)(2,1)S(1)}, bf16[256,256]{1,0:T(8,128)(2,1)S(1)}) custom-call(s32[32,2]{1,0:T(8,128)S(1)} %bitcast.16, s32[1]{0:T(128)} %bitcast.6.me_ref, bf16[32,64,256]{2,1,0:T(8,128)(2,1)} %all-to-all-done.1.rows_ref, ...), custom_call_target="tpu_custom_call" | custom-call | tf_op jit(solution)/shard_map/gather_sums/pallas_call | solution.py:192
  81.3 2.0 %collective-permute-start.4 = (bf16[512,256]{1,0:T(8,128)(2,1)S(1)}, bf16[512,256]{1,0:T(8,128)(2,1)S(1)}, u32[]{:S(2)}, u32[]{:S(2)}) collective-permute-start(bf16[512,256]{1,0:T(8,128)(2,1)S(1)} %get-tuple-element.25), channel_id=1, source_target_pairs={{0,32},{32,64},{64,96},{96,0},{1,33},{33,65},{65,97},{97,1},{2,34}... | collective-permute-start | bytes 786440 | tf_op jit(solution)/shard_map/ppermute | solution.py:361
  83.3 2.2 %collective-permute-start.1 = (bf16[528,512]{1,0:T(8,128)(2,1)}, bf16[528,512]{1,0:T(8,128)(2,1)S(1)}, u32[]{:S(2)}, u32[]{:S(2)}) collective-permute-start(bf16[528,512]{1,0:T(8,128)(2,1)} %copy-done.10), channel_id=1, source_target_pairs={{32,0},{64,32},{96,64},{0,96},{33,1},{65,33},{97,65},{1,97},{34,2}... | collective-permute-start | bytes 1622024 | tf_op jit(solution)/shard_map/ppermute | solution.py:362
  85.5 1.9 %collective-permute-start.5 = (bf16[512,256]{1,0:T(8,128)(2,1)S(1)}, bf16[512,256]{1,0:T(8,128)(2,1)S(1)}, u32[]{:S(2)}, u32[]{:S(2)}) collective-permute-start(bf16[512,256]{1,0:T(8,128)(2,1)S(1)} %get-tuple-element.26), channel_id=1, source_target_pairs={{32,0},{64,32},{96,64},{0,96},{33,1},{65,33},{97,65},{1,97},{34,2}... | collective-permute-start | bytes 786440 | tf_op jit(solution)/shard_map/ppermute | solution.py:362
  87.4 4.8 %collective-permute-done.4.refs_6_ = bf16[512,256]{1,0:T(8,128)(2,1)S(1)} collective-permute-done((bf16[512,256]{1,0:T(8,128)(2,1)S(1)}, bf16[512,256]{1,0:T(8,128)(2,1)S(1)}, u32[]{:S(2)}, u32[]{:S(2)}) %collective-permute-start.4) | collective-permute-done | bytes 262176 | tf_op jit(solution)/shard_map/ppermute | solution.py:361
  92.3 0.1 collective-permute-start.6
  92.4 0.0 collective-permute-done.refs_1_
  92.4 1.0 add_convert_fusion.1
  93.4 1.8 %collective-permute-start.2 = (bf16[264,512]{1,0:T(8,128)(2,1)S(1)}, bf16[264,512]{1,0:T(8,128)(2,1)S(1)}, u32[]{:S(2)}, u32[]{:S(2)}) collective-permute-start(bf16[264,512]{1,0:T(8,128)(2,1)S(1)} %add_convert_fusion.1), channel_id=1, source_target_pairs={{0,32},{32,64},{64,96},{96,0},{1,33},{33,65},{65,97},{97,1},{2,34}... | collective-permute-start | bytes 811016 | tf_op jit(solution)/shard_map/ppermute | solution.py:364
  95.2 3.4 %collective-permute-done.1.refs_2_ = bf16[528,512]{1,0:T(8,128)(2,1)S(1)} collective-permute-done((bf16[528,512]{1,0:T(8,128)(2,1)}, bf16[528,512]{1,0:T(8,128)(2,1)S(1)}, u32[]{:S(2)}, u32[]{:S(2)}) %collective-permute-start.1) | collective-permute-done | bytes 540704 | tf_op jit(solution)/shard_map/ppermute | solution.py:362
  98.6 0.1 add_convert_fusion
  98.7 3.5 %collective-permute-start.3 = (bf16[264,512]{1,0:T(8,128)(2,1)S(1)}, bf16[264,512]{1,0:T(8,128)(2,1)S(1)}, u32[]{:S(2)}, u32[]{:S(2)}) collective-permute-start(bf16[264,512]{1,0:T(8,128)(2,1)S(1)} %add_convert_fusion), channel_id=1, source_target_pairs={{32,0},{64,32},{96,64},{0,96},{33,1},{65,33},{97,65},{1,97},{34,2}... | collective-permute-start | bytes 811016 | tf_op jit(solution)/shard_map/ppermute | solution.py:364
  102.2 2.1 %collective-permute-done.5.refs_7_ = bf16[512,256]{1,0:T(8,128)(2,1)S(1)} collective-permute-done((bf16[512,256]{1,0:T(8,128)(2,1)S(1)}, bf16[512,256]{1,0:T(8,128)(2,1)S(1)}, u32[]{:S(2)}, u32[]{:S(2)}) %collective-permute-start.5) | collective-permute-done | bytes 262176 | tf_op jit(solution)/shard_map/ppermute | solution.py:362
  104.3 3.5 %collective-permute-start.7 = (bf16[256,256]{1,0:T(8,128)(2,1)S(1)}, bf16[256,256]{1,0:T(8,128)(2,1)S(1)}, u32[]{:S(2)}, u32[]{:S(2)}) collective-permute-start(bf16[256,256]{1,0:T(8,128)(2,1)S(1)} %add_convert_fusion.2), channel_id=1, source_target_pairs={{32,0},{64,32},{96,64},{0,96},{33,1},{65,33},{97,65},{1,97},{34,2}... | collective-permute-start | bytes 393224 | tf_op jit(solution)/shard_map/ppermute | solution.py:364
  107.8 0.0 collective-permute-done.6.refs_8_
  107.8 4.4 %collective-permute-done.7.refs_9_ = bf16[256,256]{1,0:T(8,128)(2,1)S(1)} collective-permute-done((bf16[256,256]{1,0:T(8,128)(2,1)S(1)}, bf16[256,256]{1,0:T(8,128)(2,1)S(1)}, u32[]{:S(2)}, u32[]{:S(2)}) %collective-permute-start.7) | collective-permute-done | bytes 131104 | tf_op jit(solution)/shard_map/ppermute | solution.py:364
  112.2 0.0 collective-permute-done.2.refs_3_
  112.2 0.0 collective-permute-done.3.refs_4_
  112.2 0.0 copy-done.1
  112.2 0.0 copy-done.3
  112.2 0.0 copy-done.4
  112.2 0.0 copy-done.5
  112.2 0.0 copy-done.8
  112.2 0.0 slice-start.1
  112.2 0.0 copy-start.6
  112.2 2.4 %project.1 = (f32[512,768]{1,0:T(8,128)S(1)}, bf16[512,768]{1,0:T(8,128)(2,1)S(1)}, bf16[512,768]{1,0:T(8,128)(2,1)S(1)}, bf16[512,768]{1,0:T(8,128)(2,1)S(1)}) custom-call(bf16[528,512]{1,0:T(8,128)(2,1)S(1)} %copy-done.8, bf16[528,512]{1,0:T(8,128)(2,1)S(1)} %collective-permute-done.refs_1_, bf16[528,512]{1,0:T(8,128)(2,1)S(1)} %collective-permute-done.1.refs_2_, ...), custom_call_target="tpu_custom_call" | custom-call | tf_op jit(solution)/shard_map/project/pallas_call | solution.py:249
  114.7 0.1 collective-permute-start.8
  114.8 7.2 %collective-permute-start.9 = (bf16[32,1536]{1,0:T(8,128)(2,1)S(1)}, bf16[32,1536]{1,0:T(8,128)(2,1)S(1)}, u32[]{:S(2)}, u32[]{:S(2)}) collective-permute-start(bf16[32,1536]{1,0:T(8,128)(2,1)S(1)} %pad_maximum_fusion.1), channel_id=1, source_target_pairs={{1,0},{2,1},{3,2},{4,3},{5,4},{6,5},{7,6},{8,7},{9,8},{10,9},{11,1... | collective-permute-start | bytes 294920 | tf_op jit(solution)/shard_map/ppermute | solution.py:408
  122.0 2.2 %collective-permute-done.8.before_ref = bf16[32,1536]{1,0:T(8,128)(2,1)S(1)} collective-permute-done((bf16[32,1536]{1,0:T(8,128)(2,1)S(1)}, bf16[32,1536]{1,0:T(8,128)(2,1)S(1)}, u32[]{:S(2)}, u32[]{:S(2)}) %collective-permute-start.8) | collective-permute-done | bytes 98336 | tf_op jit(solution)/shard_map/ppermute | solution.py:407
  124.2 0.0 collective-permute-done.9.after_ref
  124.3 0.0 copy-start.2
  124.3 2.3 %copy-done.2 = bf16[3072,768]{1,0:T(8,128)(2,1)S(1)} copy-done((bf16[3072,768]{1,0:T(8,128)(2,1)S(1)}, bf16[3072,768]{1,0:T(8,128)(2,1)}, u32[]{:S(2)}) %copy-start.2) | copy-done | bytes 4718616
  126.6 10.9 %attend.1 = bf16[512,768]{1,0:T(8,128)(2,1)} custom-call(f32[512,768]{1,0:T(8,128)S(1)} %get-tuple-element.29.stream_ref, bf16[512,768]{1,0:T(8,128)(2,1)S(1)} %get-tuple-element.30.q_ref, bf16[512,768]{1,0:T(8,128)(2,1)S(1)} %get-tuple-element.31.k_ref, bf16[512,768]{1,0:T(8,128)(2,1)S(1)} %get-tuple-element.32.v_ref, ...), custom_call_target="tpu_custom_call" | custom-call | tf_op jit(solution)/shard_map/attend/pallas_call | solution.py:313
  (23 shorter events, 0.2 us)
Async XLA Ops:
  12.8 42.0 %all-to-all-start = ((bf16[32,80,512]{2,1,0:T(8,128)(2,1)}), bf16[32,80,512]{2,1,0:T(8,128)(2,1)S(1)}, u32[]{:S(2)}, u32[]{:S(2)}) async-start(bf16[32,80,512]{2,1,0:T(8,128)(2,1)} %pack.2), calls=%async_computation | async-start | bytes 5242880 | tf_op jit(solution)/shard_map/all_to_all | solution.py:382
  20.2 39.3 %copy-start.11 = (s32[1,1,3,512]{3,1,2,0:T(1,128)S(1)}, s32[1,1,3,512]{3,1,2,0:T(1,128)}, u32[]{:S(2)}) copy-start(s32[1,1,3,512]{3,1,2,0:T(1,128)} %param.16) | copy-start | bytes 18436
  54.8 21.4 %all-to-all-start.1 = ((bf16[32,64,256]{2,1,0:T(8,128)(2,1)}), bf16[32,64,256]{2,1,0:T(8,128)(2,1)}, u32[]{:S(2)}, u32[]{:S(2)}) async-start(bf16[32,64,256]{2,1,0:T(8,128)(2,1)} %pack.3), calls=%async_computation.1 | async-start | bytes 2097152 | tf_op jit(solution)/shard_map/all_to_all | solution.py:382
  62.4 5.1 %copy-start = (f32[512,768]{1,0:T(8,128)}, f32[512,768]{1,0:T(8,128)S(1)}, u32[]{:S(2)}) copy-start(f32[512,768]{1,0:T(8,128)S(1)} %position.1.rest_0_.refs_10_) | copy-start | bytes 4718596
  67.5 0.8 copy-start.7
  68.3 0.7 copy-start.9
  69.0 0.8 copy-start.10
  69.8 22.6 %collective-permute-start = (bf16[528,512]{1,0:T(8,128)(2,1)}, bf16[528,512]{1,0:T(8,128)(2,1)S(1)}, u32[]{:S(2)}, u32[]{:S(2)}) collective-permute-start(bf16[528,512]{1,0:T(8,128)(2,1)} %get-tuple-element.20), channel_id=1, source_target_pairs={{0,32},{32,64},{64,96},{96,0},{1,33},{33,65},{65,97},{97,1},{2,34}... | collective-permute-start | bytes 1622024 | tf_op jit(solution)/shard_map/ppermute | solution.py:361
  76.2 35.9 %copy-start.1 = (f32[512,768]{1,0:T(8,128)S(1)}, f32[512,768]{1,0:T(8,128)}, u32[]{:S(2)}) copy-start(f32[512,768]{1,0:T(8,128)} %copy-done) | copy-start | bytes 4718596
  76.2 36.0 %copy-start.3 = (bf16[768,768]{1,0:T(8,128)(2,1)S(1)}, bf16[768,768]{1,0:T(8,128)(2,1)}, u32[]{:S(2)}) copy-start(bf16[768,768]{1,0:T(8,128)(2,1)} %refs_11_.1) | copy-start | bytes 3538948
  76.2 36.0 %copy-start.4 = (bf16[768,768]{1,0:T(8,128)(2,1)S(1)}, bf16[768,768]{1,0:T(8,128)(2,1)}, u32[]{:S(2)}) copy-start(bf16[768,768]{1,0:T(8,128)(2,1)} %refs_12_.1) | copy-start | bytes 3538948
  76.2 36.0 %copy-start.5 = (bf16[768,768]{1,0:T(8,128)(2,1)S(1)}, bf16[768,768]{1,0:T(8,128)(2,1)}, u32[]{:S(2)}) copy-start(bf16[768,768]{1,0:T(8,128)(2,1)} %refs_13_.1) | copy-start | bytes 3538948
  76.2 36.0 %copy-start.8 = (bf16[528,512]{1,0:T(8,128)(2,1)S(1)}, bf16[528,512]{1,0:T(8,128)(2,1)}, u32[]{:S(2)}) copy-start(bf16[528,512]{1,0:T(8,128)(2,1)} %copy-done.7) | copy-start | bytes 1622020
  81.3 11.0 %collective-permute-start.4 = (bf16[512,256]{1,0:T(8,128)(2,1)S(1)}, bf16[512,256]{1,0:T(8,128)(2,1)S(1)}, u32[]{:S(2)}, u32[]{:S(2)}) collective-permute-start(bf16[512,256]{1,0:T(8,128)(2,1)S(1)} %get-tuple-element.25), channel_id=1, source_target_pairs={{0,32},{32,64},{64,96},{96,0},{1,33},{33,65},{65,97},{97,1},{2,34}... | collective-permute-start | bytes 786440 | tf_op jit(solution)/shard_map/ppermute | solution.py:361
  83.3 15.4 %collective-permute-start.1 = (bf16[528,512]{1,0:T(8,128)(2,1)}, bf16[528,512]{1,0:T(8,128)(2,1)S(1)}, u32[]{:S(2)}, u32[]{:S(2)}) collective-permute-start(bf16[528,512]{1,0:T(8,128)(2,1)} %copy-done.10), channel_id=1, source_target_pairs={{32,0},{64,32},{96,64},{0,96},{33,1},{65,33},{97,65},{1,97},{34,2}... | collective-permute-start | bytes 1622024 | tf_op jit(solution)/shard_map/ppermute | solution.py:362
  85.5 18.8 %collective-permute-start.5 = (bf16[512,256]{1,0:T(8,128)(2,1)S(1)}, bf16[512,256]{1,0:T(8,128)(2,1)S(1)}, u32[]{:S(2)}, u32[]{:S(2)}) collective-permute-start(bf16[512,256]{1,0:T(8,128)(2,1)S(1)} %get-tuple-element.26), channel_id=1, source_target_pairs={{32,0},{64,32},{96,64},{0,96},{33,1},{65,33},{97,65},{1,97},{34,2}... | collective-permute-start | bytes 786440 | tf_op jit(solution)/shard_map/ppermute | solution.py:362
  92.3 15.5 %collective-permute-start.6 = (bf16[256,256]{1,0:T(8,128)(2,1)S(1)}, bf16[256,256]{1,0:T(8,128)(2,1)S(1)}, u32[]{:S(2)}, u32[]{:S(2)}) collective-permute-start(bf16[256,256]{1,0:T(8,128)(2,1)S(1)} %add_convert_fusion.3), channel_id=1, source_target_pairs={{0,32},{32,64},{64,96},{96,0},{1,33},{33,65},{65,97},{97,1},{2,34}... | collective-permute-start | bytes 393224 | tf_op jit(solution)/shard_map/ppermute | solution.py:364
  93.4 18.8 %collective-permute-start.2 = (bf16[264,512]{1,0:T(8,128)(2,1)S(1)}, bf16[264,512]{1,0:T(8,128)(2,1)S(1)}, u32[]{:S(2)}, u32[]{:S(2)}) collective-permute-start(bf16[264,512]{1,0:T(8,128)(2,1)S(1)} %add_convert_fusion.1), channel_id=1, source_target_pairs={{0,32},{32,64},{64,96},{96,0},{1,33},{33,65},{65,97},{97,1},{2,34}... | collective-permute-start | bytes 811016 | tf_op jit(solution)/shard_map/ppermute | solution.py:364
  98.7 13.5 %collective-permute-start.3 = (bf16[264,512]{1,0:T(8,128)(2,1)S(1)}, bf16[264,512]{1,0:T(8,128)(2,1)S(1)}, u32[]{:S(2)}, u32[]{:S(2)}) collective-permute-start(bf16[264,512]{1,0:T(8,128)(2,1)S(1)} %add_convert_fusion), channel_id=1, source_target_pairs={{32,0},{64,32},{96,64},{0,96},{33,1},{65,33},{97,65},{1,97},{34,2}... | collective-permute-start | bytes 811016 | tf_op jit(solution)/shard_map/ppermute | solution.py:364
  104.3 7.9 %collective-permute-start.7 = (bf16[256,256]{1,0:T(8,128)(2,1)S(1)}, bf16[256,256]{1,0:T(8,128)(2,1)S(1)}, u32[]{:S(2)}, u32[]{:S(2)}) collective-permute-start(bf16[256,256]{1,0:T(8,128)(2,1)S(1)} %add_convert_fusion.2), channel_id=1, source_target_pairs={{32,0},{64,32},{96,64},{0,96},{33,1},{65,33},{97,65},{1,97},{34,2}... | collective-permute-start | bytes 393224 | tf_op jit(solution)/shard_map/ppermute | solution.py:364
  112.2 12.1 %slice-start = ((s8[4718592]{0:T(1024)(128)(4,1)}), s8[4194304]{0:T(1024)(128)(4,1)S(1)}, s32[]{:S(2)}) async-start(s8[4718592]{0:T(1024)(128)(4,1)} %bitcast.13), calls=%async_computation.2 | async-start | bytes 8388608
  112.2 12.0 %slice-start.1 = ((s8[4718592]{0:T(1024)(128)(4,1)}), s8[524288]{0:T(1024)(128)(4,1)S(1)}, s32[]{:S(2)}) async-start(s8[4718592]{0:T(1024)(128)(4,1)} %bitcast.13), calls=%async_computation.3 | async-start | bytes 1048576
  112.2 12.0 %copy-start.6 = (bf16[768,768]{1,0:T(8,128)(2,1)S(1)}, bf16[768,768]{1,0:T(8,128)(2,1)}, u32[]{:S(2)}) copy-start(bf16[768,768]{1,0:T(8,128)(2,1)} %wout_ref.1) | copy-start | bytes 3538948
  114.7 9.5 %collective-permute-start.8 = (bf16[32,1536]{1,0:T(8,128)(2,1)S(1)}, bf16[32,1536]{1,0:T(8,128)(2,1)S(1)}, u32[]{:S(2)}, u32[]{:S(2)}) collective-permute-start(bf16[32,1536]{1,0:T(8,128)(2,1)S(1)} %pad_maximum_fusion), channel_id=1, source_target_pairs={{0,1},{1,2},{2,3},{3,4},{4,5},{5,6},{6,7},{7,8},{8,9},{9,10},{10,1... | collective-permute-start | bytes 294920 | tf_op jit(solution)/shard_map/ppermute | solution.py:407
  114.8 9.4 %collective-permute-start.9 = (bf16[32,1536]{1,0:T(8,128)(2,1)S(1)}, bf16[32,1536]{1,0:T(8,128)(2,1)S(1)}, u32[]{:S(2)}, u32[]{:S(2)}) collective-permute-start(bf16[32,1536]{1,0:T(8,128)(2,1)S(1)} %pad_maximum_fusion.1), channel_id=1, source_target_pairs={{1,0},{2,1},{3,2},{4,3},{5,4},{6,5},{7,6},{8,7},{9,8},{10,9},{11,1... | collective-permute-start | bytes 294920 | tf_op jit(solution)/shard_map/ppermute | solution.py:408
  124.3 2.3 %copy-start.2 = (bf16[3072,768]{1,0:T(8,128)(2,1)S(1)}, bf16[3072,768]{1,0:T(8,128)(2,1)}, u32[]{:S(2)}) copy-start(bf16[3072,768]{1,0:T(8,128)(2,1)} %wdown.1) | copy-start | bytes 14155780

commit v4 on v3

--- a/solution.py
+++ b/solution.py
@@ -36,21 +36,47 @@
     segments = packed.shape[0]
     count = per_step * (places.shape[0] // segments)
     each = count // per_step
-    row_step = 256
+    row_step = 512
 
     win_copy = pltpu.make_async_copy(win_hbm.at[:, start : start + width], win, win_sem)
-    win_copy.start()
     spans = [slice(s, min(s + row_step, patches)) for s in range(0, patches, row_step)]
     feat_copies = [
         pltpu.make_async_copy(feat_hbm.at[span, :], feat.at[span, :], feat_sems.at[i])
         for i, span in enumerate(spans)
     ]
+    win_copy.start()
     for copy in feat_copies:
         copy.start()
     turned = jnp.transpose(idx_ref[...].astype(F32)).astype(jnp.int32)
     for i in range(turned.shape[1]):
         places[i * 128 : (i + 1) * 128, :] = turned[:, i : i + 1]
     table[spans[-1].start :, :] = jnp.zeros((table_rows - spans[-1].start, width), BF16)
+
+    if weighted:
+        slots, depth, block = lift_ref.shape[1:]
+        line = slots * block
+        lane = lax.broadcasted_iota(jnp.int32, (depth, line), 1) // EXTRA
+        pickers = lax.broadcasted_iota(jnp.int32, (EXTRA, line), 1) % EXTRA
+        pickers = (pickers == lax.broadcasted_iota(jnp.int32, (EXTRA, line), 0)).astype(F32).astype(BF16)
+        mark_lane = lax.broadcasted_iota(jnp.int32, (EXTRA, width - 2 * line), 1)
+
+        def weigh(segment, carry):
+            both = jnp.concatenate([lift_ref[segment, c] for c in range(slots)], axis=1)
+            zero = jnp.zeros_like(both)
+            apart = jnp.concatenate(
+                [jnp.where(lane == g, both, zero) for g in range(line // EXTRA)], axis=0
+            )
+            packed[segment, each:, : 2 * line] = lax.dot_general(
+                pickers, apart, (((1,), (1,)), ((), ())), preferred_element_type=F32
+            ).astype(BF16)
+            marks = jnp.zeros(mark_lane.shape, jnp.int32)
+            for c in range(slots):
+                marks = jnp.where(mark_lane == c, ids_ref[c, segment], marks)
+            packed[segment, each:, 2 * line :] = marks.astype(F32).astype(BF16)
+            return carry
+
+        lax.fori_loop(0, segments, weigh, 0, unroll=8)
+
     win_copy.wait()
     weights = win[...].astype(BF16)
     for copy, span in zip(feat_copies, spans):
@@ -66,35 +92,12 @@
         picked = lax.broadcasted_iota(jnp.int32, (count, table_rows), 1) == spot
         rows = dot(picked.astype(F32).astype(BF16), table[...]).astype(BF16)
         for i in range(per_step):
-            segment = base * per_step + i
-            packed[segment, :each, :] = rows[i * each : (i + 1) * each, :]
-            if weighted:
-                slots, _, block = lift_ref.shape[1:]
-                both = jnp.concatenate(
-                    [lift_ref[segment, c].astype(F32) for c in range(slots)], axis=1
-                )
-                turned = jnp.transpose(both)
-                for c in range(slots):
-                    groups = [
-                        turned[c * block + g * EXTRA : c * block + (g + 1) * EXTRA, :]
-                        for g in range(block // EXTRA)
-                    ]
-                    packed[segment, each:, c * 128 : (c + 1) * 128] = jnp.concatenate(
-                        groups, axis=1
-                    ).astype(BF16)
-                lane = lax.broadcasted_iota(jnp.int32, (EXTRA, 128), 1)
-                marks = jnp.zeros((EXTRA, 128), jnp.int32)
-                for c in range(slots):
-                    marks = jnp.where(lane == c, ids_ref[c, segment], marks)
-                packed[segment, each:, slots * 128 : (slots + 1) * 128] = marks.astype(F32).astype(BF16)
-                packed[segment, each:, (slots + 1) * 128 :] = jnp.zeros(
-                    (EXTRA, width - (slots + 1) * 128), BF16
-                )
+            packed[base * per_step + i, :each, :] = rows[i * each : (i + 1) * each, :]
         out_copy(base).start()
         return carry
 
     steps = segments // per_step
-    lax.fori_loop(0, steps, pick, 0)
+    lax.fori_loop(0, steps, pick, 0, unroll=True)
     for base in range(steps):
         out_copy(base).wait()
 
@@ -119,7 +122,7 @@
             pltpu.VMEM((-(-patches // 128) * 128, width), BF16),
             pltpu.VMEM((count, 1), jnp.int32),
             pltpu.VMEM((segments, rows, width), BF16),
-            pltpu.SemaphoreType.DMA((-(-patches // 256),)),
+            pltpu.SemaphoreType.DMA((-(-patches // 512),)),
             pltpu.SemaphoreType.DMA(()),
             pltpu.SemaphoreType.DMA((segments // per_step,)),
         ],
@@ -130,7 +133,7 @@
 
 
 def gather_sums_kernel(block, picks, half_blocks, counted, ids_ref, me_ref, rows_ref, weight_ref, *rest):
-    outs, total = rest[-6:-1], rest[-1]
+    outs, total, stage, sems = rest[-8:-3], rest[-3], rest[-2], rest[-1]
     step = pl.program_id(0)
     views, _, width = rows_ref.shape
 
@@ -173,18 +176,26 @@
 
     @pl.when(step == pl.num_programs(0) - 1)
     def _():
-        def part(away, half):
+        own, up_first, up_last, down_first, down_last = outs
+        order = (
+            (up_first, 0, 1, 1), (up_first, 1, 2, 0), (down_first, 0, 3, 0), (down_first, 1, 2, 1),
+            (up_last, 0, 1, 0), (down_last, 0, 3, 1), (own, 0, 0, 0), (own, 1, 0, 1),
+        )
+        copies = []
+        for i, (out, place, away, half) in enumerate(order):
             first = (away * 2 + half) * size
-            return total[first : first + size, :].astype(BF16)
-
-        own, up_first, up_last, down_first, down_last = outs
-        up_first[:size, :], up_first[size:, :] = part(1, 1), part(2, 0)
-        down_first[:size, :], down_first[size:, :] = part(3, 0), part(2, 1)
-        up_last[...], down_last[...] = part(1, 0), part(3, 1)
-        own[:size, :], own[size:, :] = part(0, 0), part(0, 1)
-
-
-def gather_sums(ids, me, rows, weights, block, picks, half_blocks, counted, *after):
+            stage[i] = total[first : first + size, :].astype(BF16)
+            copies.append(
+                pltpu.make_async_copy(
+                    stage.at[i], out.at[place * size : (place + 1) * size, :], sems.at[i]
+                )
+            )
+            copies[-1].start()
+        for copy in copies:
+            copy.wait()
+
+
+def gather_sums(ids, me, rows, weights, block, picks, half_blocks, counted):
     views, _, width = rows.shape
     count = ids.shape[1] * picks
     size = half_blocks * block + (8 if counted else 0)
@@ -197,15 +208,21 @@
             in_specs=[
                 pl.BlockSpec((8, count, width), lambda i, *_: (i, 0, 0)),
                 pl.BlockSpec((8, EXTRA, weights.shape[2]), lambda i, *_: (i, count // EXTRA, 0)),
-            ]
-            + [ANY] * len(after),
-            out_specs=[pl.BlockSpec((s, width), lambda i, *_: (0, 0)) for s in sizes],
-            scratch_shapes=[pltpu.VMEM((8 * size + block + 8, width), F32)],
+            ],
+            out_specs=[pl.BlockSpec(memory_space=pltpu.HBM)] * len(sizes),
+            scratch_shapes=[
+                pltpu.VMEM((8 * size + block + 8, width), F32),
+                pltpu.VMEM((8, size, width), BF16),
+                pltpu.SemaphoreType.DMA((8,)),
+            ],
         ),
-        out_shape=[jax.ShapeDtypeStruct((s, width), BF16) for s in sizes],
-        compiler_params=params(24, dimension_semantics=("arbitrary",)),
+        out_shape=[
+            (pltpu.HBM if counted and i in (0, 2, 4) else jax.ShapeDtypeStruct)((s, width), BF16)
+            for i, s in enumerate(sizes)
+        ],
+        compiler_params=params(20, dimension_semantics=("arbitrary",)),
         name="gather_sums",
-    )(ids, me, rows, weights, *after)
+    )(ids, me, rows, weights)
 
 
 def normalize(values):
@@ -252,7 +269,8 @@
         out_specs=[VM] * 4,
         out_shape=[jax.ShapeDtypeStruct((rows, width), F32)]
         + [jax.ShapeDtypeStruct((rows, width), BF16)] * 3,
-        compiler_params=params(24),
+        compiler_params=params(16),
+        cost_estimate=pl.CostEstimate(flops=6 * rows * width * width, bytes_accessed=12 * rows * width, transcendentals=0),
         name="project",
     )(*sums, pos, w_query, w_key, w_value)
 
@@ -320,9 +338,27 @@
             pltpu.VMEM((rows, width), BF16),
             pltpu.VMEM((rows, width), F32),
         ],
-        compiler_params=params(30),
+        compiler_params=params(16),
         name="attend",
     )(stream, query, keys, values, before, after, w_out, w_up, w_down)
+
+
+def hold_kernel(from_ref, to_ref, sem):
+    copy = pltpu.make_async_copy(from_ref, to_ref, sem)
+    copy.start()
+    copy.wait()
+
+
+def hold(array):
+    return pl.pallas_call(
+        hold_kernel,
+        in_specs=[ANY],
+        out_specs=VM,
+        out_shape=pltpu.VMEM(array.shape, array.dtype),
+        scratch_shapes=[pltpu.SemaphoreType.DMA(())],
+        compiler_params=params(1),
+        name="hold",
+    )(array)
 
 
 def position_kernel(coords_ref, freq_ref, out_ref):
@@ -358,10 +394,13 @@
     def join(a, b):
         return (a.astype(F32) + b[half:].astype(F32)).astype(BF16)
 
-    from_below = lax.ppermute(up_first, axis, up)
-    from_above = lax.ppermute(down_first, axis, down)
+    def move(value, pairs):
+        return lax.ppermute(value, axis, pairs)
+
+    from_below = move(up_first, up)
+    from_above = move(down_first, down)
     up_last, down_last = join(up_last, from_below), join(down_last, from_above)
-    up_last, down_last = lax.ppermute(up_last, axis, up), lax.ppermute(down_last, axis, down)
+    up_last, down_last = move(up_last, up), move(down_last, down)
     return [own, from_below, from_above, up_last, down_last]
 
 
@@ -389,11 +428,11 @@
     me = lax.axis_index("view").astype(jnp.int32).reshape(1)
     ids = first[:, slots * picks, slots * 128 : slots * 128 + slots].astype(jnp.int32)
 
-    def sums(rows, counted, *after):
-        parts = gather_sums(ids, me, rows, first, block, picks, half_blocks, counted, *after)
+    def sums(rows, counted):
+        parts = gather_sums(ids, me, rows, first, block, picks, half_blocks, counted)
         return share(parts, "view", view_count, parts[2].shape[0])
 
-    shares = sums(first, True, pos)
+    shares = sums(first, True)
     shares += sums(second, False)
     stream, query, keys, values = project(
         shares, pos, w_query, w_key, w_value, block, half_blocks
@@ -406,6 +445,7 @@
     first = jnp.concatenate([keys[:half], values[:half]], axis=1)
     before = lax.ppermute(last, ("view", "seg"), ring_up)
     after = lax.ppermute(first, ("view", "seg"), ring_down)
+    w_down = hold(w_down)
     encoded = attend(stream, query, keys, values, before, after, w_out, w_up, w_down, block)
     return encoded.reshape(1, 1, rows_here, width)
 

time: 138 us -> 136 us (0.986)
  local copies, waits for them, and re-layouts: 6.15 us -> 2.32 us
  waiting for transfers between devices: 47.6 us -> 50.9 us
  Pallas kernels: 46.1 us -> 44.5 us
    all_to_all x2, waiting for transfers between devices: 30.6 us -> 36.5 us  [send(): lax.all_to_all(payload, 'seg', split_axis=0, concat_axis=0, tiled=True)]
    unnamed x29, local copies, waits for them, and re-layouts: 4.68 us -> 0.86 us
    pallas_call x2, Pallas kernels: 19.8 us -> 16.4 us  [pack(): pl.pallas_call(functools.partial(pack_kernel, start, per_step, weighted),...]
    ppermute x8, waiting for transfers between devices: 14.8 us -> 12.6 us  [move(): return lax.ppermute(value, axis, pairs)]
    pallas_call x2, Pallas kernels: 10 us -> 11.5 us  [gather_sums(): pl.pallas_call(functools.partial(gather_sums_kernel, block, picks, half_b...]
  transfers between devices with their start and end apart: 12 -> 12, of which waited for: 7 -> 8; matrix products, arithmetic and copies ran while one was open for 1% -> 0% of each run, Pallas kernels for 16% -> 16%
where the time goes in v4:
time: 136 us; the launch traced here: 135 us
  waiting for transfers between devices  50.9 us (37%)
  Pallas kernels  44.5 us (33%)
  starting transfers between devices  36.5 us (27%)
  local copies, waits for them, and re-layouts  2.32 us (2%)
    all_to_all x2, waiting for transfers between devices, send(): lax.all_to_all(payload, 'seg', split_axis=0, concat_axis=0, tiled=True)  36.5 us
    ppermute x8, starting transfers between devices, move(): return lax.ppermute(value, axis, pairs)  16.8 us
    pallas_call x2, Pallas kernels, pack(): pl.pallas_call(functools.partial(pack_kernel, start, per_step, weighted),...  16.4 us
    ppermute x8, waiting for transfers between devices, move(): return lax.ppermute(value, axis, pairs)  12.6 us
    all_to_all x2, starting transfers between devices, send(): lax.all_to_all(payload, 'seg', split_axis=0, concat_axis=0, tiled=True)  12.1 us
    pallas_call x2, Pallas kernels, gather_sums(): pl.pallas_call(functools.partial(gather_sums_kernel, block, picks, half_b...  11.5 us
    pallas_call x1, Pallas kernels, attend(): pl.pallas_call(functools.partial(attend_kernel, block), in_specs=[VM] * 9...  11 us
    ppermute x1, starting transfers between devices, shards(): after = lax.ppermute(first, ('view', 'seg'), ring_down)  7.43 us
  transfers between devices with their start and end apart: 12, of which 8 were waited for; matrix products, arithmetic and copies ran while one was open for 0% of the time, Pallas kernels for 16%

profile of v4, /device:TPU:0, one launch (start us, length us, event | category | flops | bytes accessed | tf_op | source)
XLA Modules:
  0.0 134.8 jit_solution(11952222094894294586)
XLA Ops:
  0.0 1.4 %reshape_squeeze.3.refs_3_.refs_2_ = s32[16,128]{1,0:T(8,128)} reshape(s32[1,32,2,32]{3,2,1,0:T(2,128)} %param.14) | data formatting | bytes 16384 | tf_op jit(solution)/shard_map/reshape;squeeze | solution.py:418
  1.4 9.6 %pack.2 = bf16[32,80,512]{2,1,0:T(8,128)(2,1)} custom-call(s32[2,32]{1,0:T(2,128)} %bitcast.23, bf16[1369,1024]{1,0:T(8,128)(2,1)} %bitcast.20, f32[1024,768]{1,0:T(8,128)} %refs_1_.1, s32[16,128]{1,0:T(8,128)} %reshape_squeeze.3.refs_3_.refs_2_, bf16[32,2,32,64]{3,2,1,0:T(8,128)(2,1)} %bitcast.22), custom_call_target="tpu_custom_call" | custom-call | tf_op jit(solution)/shard_map/pack/pallas_call | solution.py:115
  11.0 7.4 %all-to-all-start = ((bf16[32,80,512]{2,1,0:T(8,128)(2,1)}), bf16[32,80,512]{2,1,0:T(8,128)(2,1)S(1)}, u32[]{:S(2)}, u32[]{:S(2)}) async-start(bf16[32,80,512]{2,1,0:T(8,128)(2,1)} %pack.2), calls=%async_computation | async-start | bytes 5242880 | tf_op jit(solution)/shard_map/all_to_all | solution.py:421
  18.5 6.8 %pack.3 = bf16[32,64,256]{2,1,0:T(8,128)(2,1)} custom-call(bf16[1369,1024]{1,0:T(8,128)(2,1)} %bitcast.21, f32[1024,768]{1,0:T(8,128)} %refs_1_.1, s32[16,128]{1,0:T(8,128)} %reshape_squeeze.3.refs_3_.refs_2_), custom_call_target="tpu_custom_call" | custom-call | tf_op jit(solution)/shard_map/pack/pallas_call | solution.py:115
  25.3 27.8 %all-to-all-done.rows_ref.weight_ref = bf16[32,80,512]{2,1,0:T(8,128)(2,1)S(1)} async-done(((bf16[32,80,512]{2,1,0:T(8,128)(2,1)}), bf16[32,80,512]{2,1,0:T(8,128)(2,1)S(1)}, u32[]{:S(2)}, u32[]{:S(2)}) %all-to-all-start) | async-done | bytes 2621472 | tf_op jit(solution)/shard_map/all_to_all | solution.py:421
  53.0 4.7 %all-to-all-start.1 = ((bf16[32,64,256]{2,1,0:T(8,128)(2,1)}), bf16[32,64,256]{2,1,0:T(8,128)(2,1)}, u32[]{:S(2)}, u32[]{:S(2)}) async-start(bf16[32,64,256]{2,1,0:T(8,128)(2,1)} %pack.3), calls=%async_computation.1 | async-start | bytes 2097152 | tf_op jit(solution)/shard_map/all_to_all | solution.py:421
  57.8 5.2 %gather_sums.2 = (bf16[528,512]{1,0:T(8,128)(2,1)}, bf16[528,512]{1,0:T(8,128)(2,1)}, bf16[264,512]{1,0:T(8,128)(2,1)}, bf16[528,512]{1,0:T(8,128)(2,1)S(1)}, bf16[264,512]{1,0:T(8,128)(2,1)}) custom-call(s32[32,2]{1,0:T(8,128)S(1)} %bitcast.17, s32[1]{0:T(128)} %bitcast.6.me_ref, bf16[32,80,512]{2,1,0:T(8,128)(2,1)S(1)} %all-to-all-done.rows_ref.weight_ref, ...), custom_call_target="tpu_custom_call" | custom-call | tf_op jit(solution)/shard_map/gather_sums/pallas_call | solution.py:203
  63.0 0.8 copy-done.5
  63.8 1.9 %collective-permute-start = (bf16[528,512]{1,0:T(8,128)(2,1)}, bf16[528,512]{1,0:T(8,128)(2,1)S(1)}, u32[]{:S(2)}, u32[]{:S(2)}) collective-permute-start(bf16[528,512]{1,0:T(8,128)(2,1)} %get-tuple-element.20), channel_id=1, source_target_pairs={{0,32},{32,64},{64,96},{96,0},{1,33},{33,65},{65,97},{97,1},{2,34}... | collective-permute-start | bytes 1622024 | tf_op jit(solution)/shard_map/ppermute | solution.py:398
  65.7 8.7 %all-to-all-done.1.rows_ref = bf16[32,64,256]{2,1,0:T(8,128)(2,1)} async-done(((bf16[32,64,256]{2,1,0:T(8,128)(2,1)}), bf16[32,64,256]{2,1,0:T(8,128)(2,1)}, u32[]{:S(2)}, u32[]{:S(2)}) %all-to-all-start.1) | async-done | bytes 1048608 | tf_op jit(solution)/shard_map/all_to_all | solution.py:421
  74.5 6.3 %gather_sums.3 = (bf16[512,256]{1,0:T(8,128)(2,1)S(1)}, bf16[512,256]{1,0:T(8,128)(2,1)S(1)}, bf16[256,256]{1,0:T(8,128)(2,1)S(1)}, bf16[512,256]{1,0:T(8,128)(2,1)S(1)}, bf16[256,256]{1,0:T(8,128)(2,1)S(1)}) custom-call(s32[32,2]{1,0:T(8,128)S(1)} %bitcast.18, s32[1]{0:T(128)} %bitcast.6.me_ref, bf16[32,64,256]{2,1,0:T(8,128)(2,1)} %all-to-all-done.1.rows_ref, ...), custom_call_target="tpu_custom_call" | custom-call | tf_op jit(solution)/shard_map/gather_sums/pallas_call | solution.py:203
  80.8 0.0 copy-start
  80.8 0.0 copy-start.1
  80.8 0.0 copy-start.2
  80.8 2.0 %collective-permute-start.4 = (bf16[512,256]{1,0:T(8,128)(2,1)S(1)}, bf16[512,256]{1,0:T(8,128)(2,1)S(1)}, u32[]{:S(2)}, u32[]{:S(2)}) collective-permute-start(bf16[512,256]{1,0:T(8,128)(2,1)S(1)} %get-tuple-element.25), channel_id=1, source_target_pairs={{0,32},{32,64},{64,96},{96,0},{1,33},{33,65},{65,97},{97,1},{2,34}... | collective-permute-start | bytes 786440 | tf_op jit(solution)/shard_map/ppermute | solution.py:398
  82.8 0.0 copy-done.6
  82.8 2.2 %collective-permute-start.1 = (bf16[528,512]{1,0:T(8,128)(2,1)S(1)}, bf16[528,512]{1,0:T(8,128)(2,1)S(1)}, u32[]{:S(2)}, u32[]{:S(2)}) collective-permute-start(bf16[528,512]{1,0:T(8,128)(2,1)S(1)} %copy-done.6), channel_id=1, source_target_pairs={{32,0},{64,32},{96,64},{0,96},{33,1},{65,33},{97,65},{1,97},{34,2}... | collective-permute-start | bytes 1622024 | tf_op jit(solution)/shard_map/ppermute | solution.py:398
  85.0 1.9 %collective-permute-start.5 = (bf16[512,256]{1,0:T(8,128)(2,1)S(1)}, bf16[512,256]{1,0:T(8,128)(2,1)S(1)}, u32[]{:S(2)}, u32[]{:S(2)}) collective-permute-start(bf16[512,256]{1,0:T(8,128)(2,1)S(1)} %get-tuple-element.26), channel_id=1, source_target_pairs={{32,0},{64,32},{96,64},{0,96},{33,1},{65,33},{97,65},{1,97},{34,2}... | collective-permute-start | bytes 786440 | tf_op jit(solution)/shard_map/ppermute | solution.py:398
  86.9 4.8 %collective-permute-done.4.refs_6_ = bf16[512,256]{1,0:T(8,128)(2,1)S(1)} collective-permute-done((bf16[512,256]{1,0:T(8,128)(2,1)S(1)}, bf16[512,256]{1,0:T(8,128)(2,1)S(1)}, u32[]{:S(2)}, u32[]{:S(2)}) %collective-permute-start.4) | collective-permute-done | bytes 262176 | tf_op jit(solution)/shard_map/ppermute | solution.py:398
  91.8 0.1 collective-permute-start.6
  91.9 0.0 collective-permute-done.refs_1_
  91.9 0.1 add_convert_fusion.1
  92.0 1.6 %collective-permute-start.2 = (bf16[264,512]{1,0:T(8,128)(2,1)S(1)}, bf16[264,512]{1,0:T(8,128)(2,1)S(1)}, u32[]{:S(2)}, u32[]{:S(2)}) collective-permute-start(bf16[264,512]{1,0:T(8,128)(2,1)S(1)} %add_convert_fusion.1), channel_id=1, source_target_pairs={{0,32},{32,64},{64,96},{96,0},{1,33},{33,65},{65,97},{97,1},{2,34}... | collective-permute-start | bytes 811016 | tf_op jit(solution)/shard_map/ppermute | solution.py:398
  93.6 4.3 %collective-permute-done.1.refs_2_ = bf16[528,512]{1,0:T(8,128)(2,1)S(1)} collective-permute-done((bf16[528,512]{1,0:T(8,128)(2,1)S(1)}, bf16[528,512]{1,0:T(8,128)(2,1)S(1)}, u32[]{:S(2)}, u32[]{:S(2)}) %collective-permute-start.1) | collective-permute-done | bytes 540704 | tf_op jit(solution)/shard_map/ppermute | solution.py:398
  97.9 0.1 add_convert_fusion
  98.0 3.7 %collective-permute-start.3 = (bf16[264,512]{1,0:T(8,128)(2,1)S(1)}, bf16[264,512]{1,0:T(8,128)(2,1)S(1)}, u32[]{:S(2)}, u32[]{:S(2)}) collective-permute-start(bf16[264,512]{1,0:T(8,128)(2,1)S(1)} %add_convert_fusion), channel_id=1, source_target_pairs={{32,0},{64,32},{96,64},{0,96},{33,1},{65,33},{97,65},{1,97},{34,2}... | collective-permute-start | bytes 811016 | tf_op jit(solution)/shard_map/ppermute | solution.py:398
  101.7 1.9 %collective-permute-done.5.refs_7_ = bf16[512,256]{1,0:T(8,128)(2,1)S(1)} collective-permute-done((bf16[512,256]{1,0:T(8,128)(2,1)S(1)}, bf16[512,256]{1,0:T(8,128)(2,1)S(1)}, u32[]{:S(2)}, u32[]{:S(2)}) %collective-permute-start.5) | collective-permute-done | bytes 262176 | tf_op jit(solution)/shard_map/ppermute | solution.py:398
  103.6 3.5 %collective-permute-start.7 = (bf16[256,256]{1,0:T(8,128)(2,1)S(1)}, bf16[256,256]{1,0:T(8,128)(2,1)S(1)}, u32[]{:S(2)}, u32[]{:S(2)}) collective-permute-start(bf16[256,256]{1,0:T(8,128)(2,1)S(1)} %add_convert_fusion.2), channel_id=1, source_target_pairs={{32,0},{64,32},{96,64},{0,96},{33,1},{65,33},{97,65},{1,97},{34,2}... | collective-permute-start | bytes 393224 | tf_op jit(solution)/shard_map/ppermute | solution.py:398
  107.1 2.9 %position.1.refs_10_ = f32[512,768]{1,0:T(8,128)S(1)} custom-call(s32[3,512]{1,0:T(4,128)S(1)} %bitcast.19, f32[1,128]{1,0:T(1,128)S(1)} %multiply_exponential_fusion.freq_ref), custom_call_target="tpu_custom_call" | custom-call | tf_op jit(solution)/shard_map/position/pallas_call | solution.py:379
  110.0 0.0 collective-permute-done.6.refs_8_
  110.0 1.5 %collective-permute-done.7.refs_9_ = bf16[256,256]{1,0:T(8,128)(2,1)S(1)} collective-permute-done((bf16[256,256]{1,0:T(8,128)(2,1)S(1)}, bf16[256,256]{1,0:T(8,128)(2,1)S(1)}, u32[]{:S(2)}, u32[]{:S(2)}) %collective-permute-start.7) | collective-permute-done | bytes 131104 | tf_op jit(solution)/shard_map/ppermute | solution.py:398
  111.5 0.0 collective-permute-done.2.refs_3_
  111.5 0.0 collective-permute-done.3.refs_4_
  111.5 0.0 copy-done.4
  111.5 0.0 copy-done
  111.5 0.0 copy-done.1
  111.5 0.0 copy-done.2
  111.5 0.0 slice-start.1
  111.5 2.4 %project.1 = (f32[512,768]{1,0:T(8,128)S(1)}, bf16[512,768]{1,0:T(8,128)(2,1)S(1)}, bf16[512,768]{1,0:T(8,128)(2,1)S(1)}, bf16[512,768]{1,0:T(8,128)(2,1)S(1)}) custom-call(bf16[528,512]{1,0:T(8,128)(2,1)S(1)} %copy-done.4, bf16[528,512]{1,0:T(8,128)(2,1)S(1)} %collective-permute-done.refs_1_, bf16[528,512]{1,0:T(8,128)(2,1)S(1)} %collective-permute-done.1.refs_2_, ...), custom_call_target="tpu_custom_call" | custom-call | flops 1811939328 | bytes 4718592 | tf_op jit(solution)/shard_map/project/pallas_call | solution.py:266
  114.0 0.1 collective-permute-start.8
  114.1 0.0 slice-start.2
  114.1 0.0 slice-start.3
  114.2 0.0 copy-start.3
  114.2 7.4 %collective-permute-start.9 = (bf16[32,1536]{1,0:T(8,128)(2,1)S(1)}, bf16[32,1536]{1,0:T(8,128)(2,1)S(1)}, u32[]{:S(2)}, u32[]{:S(2)}) collective-permute-start(bf16[32,1536]{1,0:T(8,128)(2,1)S(1)} %pad_maximum_fusion.1), channel_id=1, source_target_pairs={{1,0},{2,1},{3,2},{4,3},{5,4},{6,5},{7,6},{8,7},{9,8},{10,9},{11,1... | collective-permute-start | bytes 294920 | tf_op jit(solution)/shard_map/ppermute | solution.py:447
  121.6 0.3 hold.1.wdown
  121.9 1.6 %collective-permute-done.8.before_ref = bf16[32,1536]{1,0:T(8,128)(2,1)S(1)} collective-permute-done((bf16[32,1536]{1,0:T(8,128)(2,1)S(1)}, bf16[32,1536]{1,0:T(8,128)(2,1)S(1)}, u32[]{:S(2)}, u32[]{:S(2)}) %collective-permute-start.8) | collective-permute-done | bytes 98336 | tf_op jit(solution)/shard_map/ppermute | solution.py:446
  123.6 0.2 collective-permute-done.9.after_ref
  123.8 11.0 %attend.1 = bf16[512,768]{1,0:T(8,128)(2,1)} custom-call(f32[512,768]{1,0:T(8,128)S(1)} %get-tuple-element.29.stream_ref, bf16[512,768]{1,0:T(8,128)(2,1)S(1)} %get-tuple-element.30.q_ref, bf16[512,768]{1,0:T(8,128)(2,1)S(1)} %get-tuple-element.31.k_ref, bf16[512,768]{1,0:T(8,128)(2,1)S(1)} %get-tuple-element.32.v_ref, ...), custom_call_target="tpu_custom_call" | custom-call | tf_op jit(solution)/shard_map/attend/pallas_call | solution.py:331
  (25 shorter events, 0.2 us)
Async XLA Ops:
  11.0 42.0 %all-to-all-start = ((bf16[32,80,512]{2,1,0:T(8,128)(2,1)}), bf16[32,80,512]{2,1,0:T(8,128)(2,1)S(1)}, u32[]{:S(2)}, u32[]{:S(2)}) async-start(bf16[32,80,512]{2,1,0:T(8,128)(2,1)} %pack.2), calls=%async_computation | async-start | bytes 5242880 | tf_op jit(solution)/shard_map/all_to_all | solution.py:421
  53.0 21.4 %all-to-all-start.1 = ((bf16[32,64,256]{2,1,0:T(8,128)(2,1)}), bf16[32,64,256]{2,1,0:T(8,128)(2,1)}, u32[]{:S(2)}, u32[]{:S(2)}) async-start(bf16[32,64,256]{2,1,0:T(8,128)(2,1)} %pack.3), calls=%async_computation.1 | async-start | bytes 2097152 | tf_op jit(solution)/shard_map/all_to_all | solution.py:421
  63.0 0.8 copy-start.5
  63.8 34.1 %copy-start.7 = (bf16[264,512]{1,0:T(8,128)(2,1)S(1)}, bf16[264,512]{1,0:T(8,128)(2,1)}, u32[]{:S(2)}) copy-start(bf16[264,512]{1,0:T(8,128)(2,1)} %get-tuple-element.23) | copy-start | bytes 811012
  63.8 43.3 %copy-start.9 = (s32[1,1,3,512]{3,1,2,0:T(1,128)S(1)}, s32[1,1,3,512]{3,1,2,0:T(1,128)}, u32[]{:S(2)}) copy-start(s32[1,1,3,512]{3,1,2,0:T(1,128)} %param.16) | copy-start | bytes 18436
  63.8 28.1 %collective-permute-start = (bf16[528,512]{1,0:T(8,128)(2,1)}, bf16[528,512]{1,0:T(8,128)(2,1)S(1)}, u32[]{:S(2)}, u32[]{:S(2)}) collective-permute-start(bf16[528,512]{1,0:T(8,128)(2,1)} %get-tuple-element.20), channel_id=1, source_target_pairs={{0,32},{32,64},{64,96},{96,0},{1,33},{33,65},{65,97},{97,1},{2,34}... | collective-permute-start | bytes 1622024 | tf_op jit(solution)/shard_map/ppermute | solution.py:398
  74.5 8.3 %copy-start.6 = (bf16[528,512]{1,0:T(8,128)(2,1)S(1)}, bf16[528,512]{1,0:T(8,128)(2,1)}, u32[]{:S(2)}) copy-start(bf16[528,512]{1,0:T(8,128)(2,1)} %copy-done.5) | copy-start | bytes 1622020
  74.5 17.4 %copy-start.8 = (bf16[264,512]{1,0:T(8,128)(2,1)S(1)}, bf16[264,512]{1,0:T(8,128)(2,1)}, u32[]{:S(2)}) copy-start(bf16[264,512]{1,0:T(8,128)(2,1)} %get-tuple-element.22) | copy-start | bytes 811012
  74.5 37.0 %copy-start.4 = (bf16[528,512]{1,0:T(8,128)(2,1)S(1)}, bf16[528,512]{1,0:T(8,128)(2,1)}, u32[]{:S(2)}) copy-start(bf16[528,512]{1,0:T(8,128)(2,1)} %get-tuple-element.19.refs_0_) | copy-start | bytes 1622020
  80.8 30.7 %copy-start = (bf16[768,768]{1,0:T(8,128)(2,1)S(1)}, bf16[768,768]{1,0:T(8,128)(2,1)}, u32[]{:S(2)}) copy-start(bf16[768,768]{1,0:T(8,128)(2,1)} %refs_11_.1) | copy-start | bytes 3538948
  80.8 30.7 %copy-start.1 = (bf16[768,768]{1,0:T(8,128)(2,1)S(1)}, bf16[768,768]{1,0:T(8,128)(2,1)}, u32[]{:S(2)}) copy-start(bf16[768,768]{1,0:T(8,128)(2,1)} %refs_12_.1) | copy-start | bytes 3538948
  80.8 30.7 %copy-start.2 = (bf16[768,768]{1,0:T(8,128)(2,1)S(1)}, bf16[768,768]{1,0:T(8,128)(2,1)}, u32[]{:S(2)}) copy-start(bf16[768,768]{1,0:T(8,128)(2,1)} %refs_13_.1) | copy-start | bytes 3538948
  80.8 11.0 %collective-permute-start.4 = (bf16[512,256]{1,0:T(8,128)(2,1)S(1)}, bf16[512,256]{1,0:T(8,128)(2,1)S(1)}, u32[]{:S(2)}, u32[]{:S(2)}) collective-permute-start(bf16[512,256]{1,0:T(8,128)(2,1)S(1)} %get-tuple-element.25), channel_id=1, source_target_pairs={{0,32},{32,64},{64,96},{96,0},{1,33},{33,65},{65,97},{97,1},{2,34}... | collective-permute-start | bytes 786440 | tf_op jit(solution)/shard_map/ppermute | solution.py:398
  82.8 15.1 %collective-permute-start.1 = (bf16[528,512]{1,0:T(8,128)(2,1)S(1)}, bf16[528,512]{1,0:T(8,128)(2,1)S(1)}, u32[]{:S(2)}, u32[]{:S(2)}) collective-permute-start(bf16[528,512]{1,0:T(8,128)(2,1)S(1)} %copy-done.6), channel_id=1, source_target_pairs={{32,0},{64,32},{96,64},{0,96},{33,1},{65,33},{97,65},{1,97},{34,2}... | collective-permute-start | bytes 1622024 | tf_op jit(solution)/shard_map/ppermute | solution.py:398
  85.0 18.6 %collective-permute-start.5 = (bf16[512,256]{1,0:T(8,128)(2,1)S(1)}, bf16[512,256]{1,0:T(8,128)(2,1)S(1)}, u32[]{:S(2)}, u32[]{:S(2)}) collective-permute-start(bf16[512,256]{1,0:T(8,128)(2,1)S(1)} %get-tuple-element.26), channel_id=1, source_target_pairs={{32,0},{64,32},{96,64},{0,96},{33,1},{65,33},{97,65},{1,97},{34,2}... | collective-permute-start | bytes 786440 | tf_op jit(solution)/shard_map/ppermute | solution.py:398
  91.8 18.2 %collective-permute-start.6 = (bf16[256,256]{1,0:T(8,128)(2,1)S(1)}, bf16[256,256]{1,0:T(8,128)(2,1)S(1)}, u32[]{:S(2)}, u32[]{:S(2)}) collective-permute-start(bf16[256,256]{1,0:T(8,128)(2,1)S(1)} %add_convert_fusion.3), channel_id=1, source_target_pairs={{0,32},{32,64},{64,96},{96,0},{1,33},{33,65},{65,97},{97,1},{2,34}... | collective-permute-start | bytes 393224 | tf_op jit(solution)/shard_map/ppermute | solution.py:398
  92.0 19.5 %collective-permute-start.2 = (bf16[264,512]{1,0:T(8,128)(2,1)S(1)}, bf16[264,512]{1,0:T(8,128)(2,1)S(1)}, u32[]{:S(2)}, u32[]{:S(2)}) collective-permute-start(bf16[264,512]{1,0:T(8,128)(2,1)S(1)} %add_convert_fusion.1), channel_id=1, source_target_pairs={{0,32},{32,64},{64,96},{96,0},{1,33},{33,65},{65,97},{97,1},{2,34}... | collective-permute-start | bytes 811016 | tf_op jit(solution)/shard_map/ppermute | solution.py:398
  98.0 13.5 %collective-permute-start.3 = (bf16[264,512]{1,0:T(8,128)(2,1)S(1)}, bf16[264,512]{1,0:T(8,128)(2,1)S(1)}, u32[]{:S(2)}, u32[]{:S(2)}) collective-permute-start(bf16[264,512]{1,0:T(8,128)(2,1)S(1)} %add_convert_fusion), channel_id=1, source_target_pairs={{32,0},{64,32},{96,64},{0,96},{33,1},{65,33},{97,65},{1,97},{34,2}... | collective-permute-start | bytes 811016 | tf_op jit(solution)/shard_map/ppermute | solution.py:398
  103.6 7.9 %collective-permute-start.7 = (bf16[256,256]{1,0:T(8,128)(2,1)S(1)}, bf16[256,256]{1,0:T(8,128)(2,1)S(1)}, u32[]{:S(2)}, u32[]{:S(2)}) collective-permute-start(bf16[256,256]{1,0:T(8,128)(2,1)S(1)} %add_convert_fusion.2), channel_id=1, source_target_pairs={{32,0},{64,32},{96,64},{0,96},{33,1},{65,33},{97,65},{1,97},{34,2}... | collective-permute-start | bytes 393224 | tf_op jit(solution)/shard_map/ppermute | solution.py:398
  111.5 10.1 %slice-start = ((s8[4718592]{0:T(1024)(128)(4,1)}), s8[4194304]{0:T(1024)(128)(4,1)S(1)}, s32[]{:S(2)}) async-start(s8[4718592]{0:T(1024)(128)(4,1)} %bitcast.13), calls=%async_computation.2 | async-start | bytes 8388608
  111.5 10.1 %slice-start.1 = ((s8[4718592]{0:T(1024)(128)(4,1)}), s8[524288]{0:T(1024)(128)(4,1)S(1)}, s32[]{:S(2)}) async-start(s8[4718592]{0:T(1024)(128)(4,1)} %bitcast.13), calls=%async_computation.3 | async-start | bytes 1048576
  114.0 9.5 %collective-permute-start.8 = (bf16[32,1536]{1,0:T(8,128)(2,1)S(1)}, bf16[32,1536]{1,0:T(8,128)(2,1)S(1)}, u32[]{:S(2)}, u32[]{:S(2)}) collective-permute-start(bf16[32,1536]{1,0:T(8,128)(2,1)S(1)} %pad_maximum_fusion), channel_id=1, source_target_pairs={{0,1},{1,2},{2,3},{3,4},{4,5},{5,6},{6,7},{7,8},{8,9},{9,10},{10,1... | collective-permute-start | bytes 294920 | tf_op jit(solution)/shard_map/ppermute | solution.py:446
  114.1 9.7 %slice-start.2 = ((s8[4718592]{0:T(1024)(128)(4,1)}), s8[4194304]{0:T(1024)(128)(4,1)S(1)}, s32[]{:S(2)}) async-start(s8[4718592]{0:T(1024)(128)(4,1)} %bitcast.15), calls=%async_computation.4 | async-start | bytes 8388608
  114.1 9.7 %slice-start.3 = ((s8[4718592]{0:T(1024)(128)(4,1)}), s8[524288]{0:T(1024)(128)(4,1)S(1)}, s32[]{:S(2)}) async-start(s8[4718592]{0:T(1024)(128)(4,1)} %bitcast.15), calls=%async_computation.5 | async-start | bytes 1048576
  114.2 9.7 %copy-start.3 = (bf16[768,768]{1,0:T(8,128)(2,1)S(1)}, bf16[768,768]{1,0:T(8,128)(2,1)}, u32[]{:S(2)}) copy-start(bf16[768,768]{1,0:T(8,128)(2,1)} %wout_ref.1) | copy-start | bytes 3538948
  114.2 9.6 %collective-permute-start.9 = (bf16[32,1536]{1,0:T(8,128)(2,1)S(1)}, bf16[32,1536]{1,0:T(8,128)(2,1)S(1)}, u32[]{:S(2)}, u32[]{:S(2)}) collective-permute-start(bf16[32,1536]{1,0:T(8,128)(2,1)S(1)} %pad_maximum_fusion.1), channel_id=1, source_target_pairs={{1,0},{2,1},{3,2},{4,3},{5,4},{6,5},{7,6},{8,7},{9,8},{10,9},{11,1... | collective-permute-start | bytes 294920 | tf_op jit(solution)/shard_map/ppermute | solution.py:447

commit v5 on v4

--- a/solution.py
+++ b/solution.py
@@ -172,7 +172,7 @@
                 total[pl.ds(mark, 1), :] += jnp.ones((1, width), F32)
         return carry
 
-    lax.fori_loop(0, views, add_view, 0, unroll=4)
+    lax.fori_loop(0, views, add_view, 0, unroll=8)
 
     @pl.when(step == pl.num_programs(0) - 1)
     def _():
@@ -304,12 +304,12 @@
                 both, k, (((1,), (1,)), ((), ())), preferred_element_type=F32
             ) * (1.0 / math.sqrt(HEAD_DIM))
             weights = jnp.exp(scores - jnp.max(scores, axis=-1, keepdims=True))
-            probs = (weights / jnp.sum(weights, axis=-1, keepdims=True)).astype(BF16)
+            probs = (weights * (1.0 / jnp.sum(weights, axis=-1, keepdims=True))).astype(BF16)
             out = dot(probs, v)
             mixed[span, lanes] = jnp.where(low_lanes, out[:block], out[block:]).astype(BF16)
         return carry
 
-    lax.fori_loop(0, (rows + block) // block, window, 0, unroll=3)
+    lax.fori_loop(0, (rows + block) // block, window, 0, unroll=True)
 
     step = 256
     for start in range(0, rows, step):
@@ -318,12 +318,14 @@
         )
         total[start : start + step, :] = values
         normed[start : start + step, :] = normalize(values)
-    chunk = 768
+    chunk = 1536
     for i in range(hidden_width // chunk):
         cols = slice(i * chunk, (i + 1) * chunk)
         hidden = jax.nn.gelu(dot(normed[...], wup[:, cols]), approximate=True).astype(BF16)
-        total[...] += dot(hidden, wdown[cols, :])
-    out_ref[...] = total[...].astype(BF16)
+        if i < hidden_width // chunk - 1:
+            total[...] += dot(hidden, wdown[cols, :])
+        else:
+            out_ref[...] = (total[...] + dot(hidden, wdown[cols, :])).astype(BF16)
 
 
 def attend(stream, query, keys, values, before, after, w_out, w_up, w_down, block):

time: 136 us -> 133 us (0.978)
  Pallas kernels: 44.5 us -> 41.4 us
    pallas_call x1, Pallas kernels: 11 us -> 9.39 us  [attend(): pl.pallas_call(functools.partial(attend_kernel, block), in_specs=[VM] * 9...]
    pallas_call x2, Pallas kernels: 11.5 us -> 10 us  [gather_sums(): pl.pallas_call(functools.partial(gather_sums_kernel, block, picks, half_b...]
  transfers between devices with their start and end apart: 12 -> 12, of which waited for: 8 -> 8; matrix products, arithmetic and copies ran while one was open for 0% -> 0% of each run, Pallas kernels for 16% -> 15%
where the time goes in v5:
time: 133 us; the launch traced here: 132 us
  waiting for transfers between devices  51.7 us (39%)
  Pallas kernels  41.4 us (31%)
  starting transfers between devices  36.5 us (27%)
  local copies, waits for them, and re-layouts  2.32 us (2%)
    all_to_all x2, waiting for transfers between devices, send(): lax.all_to_all(payload, 'seg', split_axis=0, concat_axis=0, tiled=True)  37.3 us
    ppermute x8, starting transfers between devices, move(): return lax.ppermute(value, axis, pairs)  16.9 us
    pallas_call x2, Pallas kernels, pack(): pl.pallas_call(functools.partial(pack_kernel, start, per_step, weighted),...  16.4 us
    ppermute x8, waiting for transfers between devices, move(): return lax.ppermute(value, axis, pairs)  12.5 us
    all_to_all x2, starting transfers between devices, send(): lax.all_to_all(payload, 'seg', split_axis=0, concat_axis=0, tiled=True)  12.1 us
    pallas_call x2, Pallas kernels, gather_sums(): pl.pallas_call(functools.partial(gather_sums_kernel, block, picks, half_b...  10 us
    pallas_call x1, Pallas kernels, attend(): pl.pallas_call(functools.partial(attend_kernel, block), in_specs=[VM] * 9...  9.39 us
    ppermute x1, starting transfers between devices, shards(): after = lax.ppermute(first, ('view', 'seg'), ring_down)  7.43 us
  transfers between devices with their start and end apart: 12, of which 8 were waited for; matrix products, arithmetic and copies ran while one was open for 0% of the time, Pallas kernels for 15%

profile of v5, /device:TPU:0, one launch (start us, length us, event | category | flops | bytes accessed | tf_op | source)
XLA Modules:
  0.0 132.5 jit_solution(15377640186561807875)
XLA Ops:
  0.0 1.4 %reshape_squeeze.3.refs_3_.refs_2_ = s32[16,128]{1,0:T(8,128)} reshape(s32[1,32,2,32]{3,2,1,0:T(2,128)} %param.14) | data formatting | bytes 16384 | tf_op jit(solution)/shard_map/reshape;squeeze | solution.py:420
  1.4 9.6 %pack.2 = bf16[32,80,512]{2,1,0:T(8,128)(2,1)} custom-call(s32[2,32]{1,0:T(2,128)} %bitcast.23, bf16[1369,1024]{1,0:T(8,128)(2,1)} %bitcast.20, f32[1024,768]{1,0:T(8,128)} %refs_1_.1, s32[16,128]{1,0:T(8,128)} %reshape_squeeze.3.refs_3_.refs_2_, bf16[32,2,32,64]{3,2,1,0:T(8,128)(2,1)} %bitcast.22), custom_call_target="tpu_custom_call" | custom-call | tf_op jit(solution)/shard_map/pack/pallas_call | solution.py:115
  11.0 7.4 %all-to-all-start = ((bf16[32,80,512]{2,1,0:T(8,128)(2,1)}), bf16[32,80,512]{2,1,0:T(8,128)(2,1)S(1)}, u32[]{:S(2)}, u32[]{:S(2)}) async-start(bf16[32,80,512]{2,1,0:T(8,128)(2,1)} %pack.2), calls=%async_computation | async-start | bytes 5242880 | tf_op jit(solution)/shard_map/all_to_all | solution.py:423
  18.5 6.8 %pack.3 = bf16[32,64,256]{2,1,0:T(8,128)(2,1)} custom-call(bf16[1369,1024]{1,0:T(8,128)(2,1)} %bitcast.21, f32[1024,768]{1,0:T(8,128)} %refs_1_.1, s32[16,128]{1,0:T(8,128)} %reshape_squeeze.3.refs_3_.refs_2_), custom_call_target="tpu_custom_call" | custom-call | tf_op jit(solution)/shard_map/pack/pallas_call | solution.py:115
  25.3 27.8 %all-to-all-done.rows_ref.weight_ref = bf16[32,80,512]{2,1,0:T(8,128)(2,1)S(1)} async-done(((bf16[32,80,512]{2,1,0:T(8,128)(2,1)}), bf16[32,80,512]{2,1,0:T(8,128)(2,1)S(1)}, u32[]{:S(2)}, u32[]{:S(2)}) %all-to-all-start) | async-done | bytes 2621472 | tf_op jit(solution)/shard_map/all_to_all | solution.py:423
  53.0 4.7 %all-to-all-start.1 = ((bf16[32,64,256]{2,1,0:T(8,128)(2,1)}), bf16[32,64,256]{2,1,0:T(8,128)(2,1)}, u32[]{:S(2)}, u32[]{:S(2)}) async-start(bf16[32,64,256]{2,1,0:T(8,128)(2,1)} %pack.3), calls=%async_computation.1 | async-start | bytes 2097152 | tf_op jit(solution)/shard_map/all_to_all | solution.py:423
  57.8 4.5 %gather_sums.2 = (bf16[528,512]{1,0:T(8,128)(2,1)}, bf16[528,512]{1,0:T(8,128)(2,1)}, bf16[264,512]{1,0:T(8,128)(2,1)}, bf16[528,512]{1,0:T(8,128)(2,1)S(1)}, bf16[264,512]{1,0:T(8,128)(2,1)}) custom-call(s32[32,2]{1,0:T(8,128)S(1)} %bitcast.17, s32[1]{0:T(128)} %bitcast.6.me_ref, bf16[32,80,512]{2,1,0:T(8,128)(2,1)S(1)} %all-to-all-done.rows_ref.weight_ref, ...), custom_call_target="tpu_custom_call" | custom-call | tf_op jit(solution)/shard_map/gather_sums/pallas_call | solution.py:203
  62.3 0.8 copy-done.5
  63.1 1.9 %collective-permute-start = (bf16[528,512]{1,0:T(8,128)(2,1)}, bf16[528,512]{1,0:T(8,128)(2,1)S(1)}, u32[]{:S(2)}, u32[]{:S(2)}) collective-permute-start(bf16[528,512]{1,0:T(8,128)(2,1)} %get-tuple-element.20), channel_id=1, source_target_pairs={{0,32},{32,64},{64,96},{96,0},{1,33},{33,65},{65,97},{97,1},{2,34}... | collective-permute-start | bytes 1622024 | tf_op jit(solution)/shard_map/ppermute | solution.py:400
  65.0 9.5 %all-to-all-done.1.rows_ref = bf16[32,64,256]{2,1,0:T(8,128)(2,1)} async-done(((bf16[32,64,256]{2,1,0:T(8,128)(2,1)}), bf16[32,64,256]{2,1,0:T(8,128)(2,1)}, u32[]{:S(2)}, u32[]{:S(2)}) %all-to-all-start.1) | async-done | bytes 1048608 | tf_op jit(solution)/shard_map/all_to_all | solution.py:423
  74.5 5.5 %gather_sums.3 = (bf16[512,256]{1,0:T(8,128)(2,1)S(1)}, bf16[512,256]{1,0:T(8,128)(2,1)S(1)}, bf16[256,256]{1,0:T(8,128)(2,1)S(1)}, bf16[512,256]{1,0:T(8,128)(2,1)S(1)}, bf16[256,256]{1,0:T(8,128)(2,1)S(1)}) custom-call(s32[32,2]{1,0:T(8,128)S(1)} %bitcast.18, s32[1]{0:T(128)} %bitcast.6.me_ref, bf16[32,64,256]{2,1,0:T(8,128)(2,1)} %all-to-all-done.1.rows_ref, ...), custom_call_target="tpu_custom_call" | custom-call | tf_op jit(solution)/shard_map/gather_sums/pallas_call | solution.py:203
  80.0 0.0 copy-start
  80.0 0.0 copy-start.1
  80.0 0.0 copy-start.2
  80.0 2.0 %collective-permute-start.4 = (bf16[512,256]{1,0:T(8,128)(2,1)S(1)}, bf16[512,256]{1,0:T(8,128)(2,1)S(1)}, u32[]{:S(2)}, u32[]{:S(2)}) collective-permute-start(bf16[512,256]{1,0:T(8,128)(2,1)S(1)} %get-tuple-element.25), channel_id=1, source_target_pairs={{0,32},{32,64},{64,96},{96,0},{1,33},{33,65},{65,97},{97,1},{2,34}... | collective-permute-start | bytes 786440 | tf_op jit(solution)/shard_map/ppermute | solution.py:400
  82.0 2.2 %collective-permute-start.1 = (bf16[528,512]{1,0:T(8,128)(2,1)S(1)}, bf16[528,512]{1,0:T(8,128)(2,1)S(1)}, u32[]{:S(2)}, u32[]{:S(2)}) collective-permute-start(bf16[528,512]{1,0:T(8,128)(2,1)S(1)} %copy-done.6), channel_id=1, source_target_pairs={{32,0},{64,32},{96,64},{0,96},{33,1},{65,33},{97,65},{1,97},{34,2}... | collective-permute-start | bytes 1622024 | tf_op jit(solution)/shard_map/ppermute | solution.py:400
  84.2 1.9 %collective-permute-start.5 = (bf16[512,256]{1,0:T(8,128)(2,1)S(1)}, bf16[512,256]{1,0:T(8,128)(2,1)S(1)}, u32[]{:S(2)}, u32[]{:S(2)}) collective-permute-start(bf16[512,256]{1,0:T(8,128)(2,1)S(1)} %get-tuple-element.26), channel_id=1, source_target_pairs={{32,0},{64,32},{96,64},{0,96},{33,1},{65,33},{97,65},{1,97},{34,2}... | collective-permute-start | bytes 786440 | tf_op jit(solution)/shard_map/ppermute | solution.py:400
  86.2 4.8 %collective-permute-done.4.refs_6_ = bf16[512,256]{1,0:T(8,128)(2,1)S(1)} collective-permute-done((bf16[512,256]{1,0:T(8,128)(2,1)S(1)}, bf16[512,256]{1,0:T(8,128)(2,1)S(1)}, u32[]{:S(2)}, u32[]{:S(2)}) %collective-permute-start.4) | collective-permute-done | bytes 262176 | tf_op jit(solution)/shard_map/ppermute | solution.py:400
  91.0 0.1 collective-permute-start.6
  91.1 0.0 collective-permute-done.refs_1_
  91.2 0.1 add_convert_fusion.1
  91.3 1.8 %collective-permute-start.2 = (bf16[264,512]{1,0:T(8,128)(2,1)S(1)}, bf16[264,512]{1,0:T(8,128)(2,1)S(1)}, u32[]{:S(2)}, u32[]{:S(2)}) collective-permute-start(bf16[264,512]{1,0:T(8,128)(2,1)S(1)} %add_convert_fusion.1), channel_id=1, source_target_pairs={{0,32},{32,64},{64,96},{96,0},{1,33},{33,65},{65,97},{97,1},{2,34}... | collective-permute-start | bytes 811016 | tf_op jit(solution)/shard_map/ppermute | solution.py:400
  93.0 4.2 %collective-permute-done.1.refs_2_ = bf16[528,512]{1,0:T(8,128)(2,1)S(1)} collective-permute-done((bf16[528,512]{1,0:T(8,128)(2,1)S(1)}, bf16[528,512]{1,0:T(8,128)(2,1)S(1)}, u32[]{:S(2)}, u32[]{:S(2)}) %collective-permute-start.1) | collective-permute-done | bytes 540704 | tf_op jit(solution)/shard_map/ppermute | solution.py:400
  97.2 0.0 copy-done.7
  97.2 0.1 add_convert_fusion
  97.2 3.5 %collective-permute-start.3 = (bf16[264,512]{1,0:T(8,128)(2,1)S(1)}, bf16[264,512]{1,0:T(8,128)(2,1)S(1)}, u32[]{:S(2)}, u32[]{:S(2)}) collective-permute-start(bf16[264,512]{1,0:T(8,128)(2,1)S(1)} %add_convert_fusion), channel_id=1, source_target_pairs={{32,0},{64,32},{96,64},{0,96},{33,1},{65,33},{97,65},{1,97},{34,2}... | collective-permute-start | bytes 811016 | tf_op jit(solution)/shard_map/ppermute | solution.py:400
  100.7 2.0 %collective-permute-done.5.refs_7_ = bf16[512,256]{1,0:T(8,128)(2,1)S(1)} collective-permute-done((bf16[512,256]{1,0:T(8,128)(2,1)S(1)}, bf16[512,256]{1,0:T(8,128)(2,1)S(1)}, u32[]{:S(2)}, u32[]{:S(2)}) %collective-permute-start.5) | collective-permute-done | bytes 262176 | tf_op jit(solution)/shard_map/ppermute | solution.py:400
  102.8 3.5 %collective-permute-start.7 = (bf16[256,256]{1,0:T(8,128)(2,1)S(1)}, bf16[256,256]{1,0:T(8,128)(2,1)S(1)}, u32[]{:S(2)}, u32[]{:S(2)}) collective-permute-start(bf16[256,256]{1,0:T(8,128)(2,1)S(1)} %add_convert_fusion.2), channel_id=1, source_target_pairs={{32,0},{64,32},{96,64},{0,96},{33,1},{65,33},{97,65},{1,97},{34,2}... | collective-permute-start | bytes 393224 | tf_op jit(solution)/shard_map/ppermute | solution.py:400
  106.3 2.9 %position.1.refs_10_ = f32[512,768]{1,0:T(8,128)S(1)} custom-call(s32[3,512]{1,0:T(4,128)S(1)} %bitcast.19, f32[1,128]{1,0:T(1,128)S(1)} %multiply_exponential_fusion.freq_ref), custom_call_target="tpu_custom_call" | custom-call | tf_op jit(solution)/shard_map/position/pallas_call | solution.py:381
  109.2 0.0 collective-permute-done.6.refs_8_
  109.2 1.5 %collective-permute-done.7.refs_9_ = bf16[256,256]{1,0:T(8,128)(2,1)S(1)} collective-permute-done((bf16[256,256]{1,0:T(8,128)(2,1)S(1)}, bf16[256,256]{1,0:T(8,128)(2,1)S(1)}, u32[]{:S(2)}, u32[]{:S(2)}) %collective-permute-start.7) | collective-permute-done | bytes 131104 | tf_op jit(solution)/shard_map/ppermute | solution.py:400
  110.7 0.0 collective-permute-done.2.refs_3_
  110.7 0.0 collective-permute-done.3.refs_4_
  110.7 0.0 copy-done.4
  110.7 0.0 copy-done
  110.7 0.0 copy-done.1
  110.8 0.0 copy-done.2
  110.8 0.0 slice-start.1
  110.8 2.4 %project.1 = (f32[512,768]{1,0:T(8,128)S(1)}, bf16[512,768]{1,0:T(8,128)(2,1)S(1)}, bf16[512,768]{1,0:T(8,128)(2,1)S(1)}, bf16[512,768]{1,0:T(8,128)(2,1)S(1)}) custom-call(bf16[528,512]{1,0:T(8,128)(2,1)S(1)} %copy-done.4, bf16[528,512]{1,0:T(8,128)(2,1)S(1)} %collective-permute-done.refs_1_, bf16[528,512]{1,0:T(8,128)(2,1)S(1)} %collective-permute-done.1.refs_2_, ...), custom_call_target="tpu_custom_call" | custom-call | flops 1811939328 | bytes 4718592 | tf_op jit(solution)/shard_map/project/pallas_call | solution.py:266
  113.3 0.1 collective-permute-start.8
  113.4 0.0 slice-start.2
  113.4 0.0 slice-start.3
  113.4 0.0 copy-start.3
  113.4 7.4 %collective-permute-start.9 = (bf16[32,1536]{1,0:T(8,128)(2,1)S(1)}, bf16[32,1536]{1,0:T(8,128)(2,1)S(1)}, u32[]{:S(2)}, u32[]{:S(2)}) collective-permute-start(bf16[32,1536]{1,0:T(8,128)(2,1)S(1)} %pad_maximum_fusion.1), channel_id=1, source_target_pairs={{1,0},{2,1},{3,2},{4,3},{5,4},{6,5},{7,6},{8,7},{9,8},{10,9},{11,1... | collective-permute-start | bytes 294920 | tf_op jit(solution)/shard_map/ppermute | solution.py:449
  120.9 0.3 hold.1.wdown
  121.2 1.6 %collective-permute-done.8.before_ref = bf16[32,1536]{1,0:T(8,128)(2,1)S(1)} collective-permute-done((bf16[32,1536]{1,0:T(8,128)(2,1)S(1)}, bf16[32,1536]{1,0:T(8,128)(2,1)S(1)}, u32[]{:S(2)}, u32[]{:S(2)}) %collective-permute-start.8) | collective-permute-done | bytes 98336 | tf_op jit(solution)/shard_map/ppermute | solution.py:448
  122.8 0.2 collective-permute-done.9.after_ref
  123.1 9.4 %attend.1 = bf16[512,768]{1,0:T(8,128)(2,1)} custom-call(f32[512,768]{1,0:T(8,128)S(1)} %get-tuple-element.29.stream_ref, bf16[512,768]{1,0:T(8,128)(2,1)S(1)} %get-tuple-element.30.q_ref, bf16[512,768]{1,0:T(8,128)(2,1)S(1)} %get-tuple-element.31.k_ref, bf16[512,768]{1,0:T(8,128)(2,1)S(1)} %get-tuple-element.32.v_ref, ...), custom_call_target="tpu_custom_call" | custom-call | tf_op jit(solution)/shard_map/attend/pallas_call | solution.py:333
  (25 shorter events, 0.2 us)
Async XLA Ops:
  11.0 42.0 %all-to-all-start = ((bf16[32,80,512]{2,1,0:T(8,128)(2,1)}), bf16[32,80,512]{2,1,0:T(8,128)(2,1)S(1)}, u32[]{:S(2)}, u32[]{:S(2)}) async-start(bf16[32,80,512]{2,1,0:T(8,128)(2,1)} %pack.2), calls=%async_computation | async-start | bytes 5242880 | tf_op jit(solution)/shard_map/all_to_all | solution.py:423
  53.0 21.4 %all-to-all-start.1 = ((bf16[32,64,256]{2,1,0:T(8,128)(2,1)}), bf16[32,64,256]{2,1,0:T(8,128)(2,1)}, u32[]{:S(2)}, u32[]{:S(2)}) async-start(bf16[32,64,256]{2,1,0:T(8,128)(2,1)} %pack.3), calls=%async_computation.1 | async-start | bytes 2097152 | tf_op jit(solution)/shard_map/all_to_all | solution.py:423
  62.3 0.8 copy-start.5
  63.1 34.1 %copy-start.7 = (bf16[264,512]{1,0:T(8,128)(2,1)S(1)}, bf16[264,512]{1,0:T(8,128)(2,1)}, u32[]{:S(2)}) copy-start(bf16[264,512]{1,0:T(8,128)(2,1)} %get-tuple-element.23) | copy-start | bytes 811012
  63.1 43.3 %copy-start.9 = (s32[1,1,3,512]{3,1,2,0:T(1,128)S(1)}, s32[1,1,3,512]{3,1,2,0:T(1,128)}, u32[]{:S(2)}) copy-start(s32[1,1,3,512]{3,1,2,0:T(1,128)} %param.16) | copy-start | bytes 18436
  63.1 28.1 %collective-permute-start = (bf16[528,512]{1,0:T(8,128)(2,1)}, bf16[528,512]{1,0:T(8,128)(2,1)S(1)}, u32[]{:S(2)}, u32[]{:S(2)}) collective-permute-start(bf16[528,512]{1,0:T(8,128)(2,1)} %get-tuple-element.20), channel_id=1, source_target_pairs={{0,32},{32,64},{64,96},{96,0},{1,33},{33,65},{65,97},{97,1},{2,34}... | collective-permute-start | bytes 1622024 | tf_op jit(solution)/shard_map/ppermute | solution.py:400
  74.5 7.5 %copy-start.6 = (bf16[528,512]{1,0:T(8,128)(2,1)S(1)}, bf16[528,512]{1,0:T(8,128)(2,1)}, u32[]{:S(2)}) copy-start(bf16[528,512]{1,0:T(8,128)(2,1)} %copy-done.5) | copy-start | bytes 1622020
  74.5 16.7 %copy-start.8 = (bf16[264,512]{1,0:T(8,128)(2,1)S(1)}, bf16[264,512]{1,0:T(8,128)(2,1)}, u32[]{:S(2)}) copy-start(bf16[264,512]{1,0:T(8,128)(2,1)} %get-tuple-element.22) | copy-start | bytes 811012
  74.5 36.3 %copy-start.4 = (bf16[528,512]{1,0:T(8,128)(2,1)S(1)}, bf16[528,512]{1,0:T(8,128)(2,1)}, u32[]{:S(2)}) copy-start(bf16[528,512]{1,0:T(8,128)(2,1)} %get-tuple-element.19.refs_0_) | copy-start | bytes 1622020
  80.0 30.7 %copy-start = (bf16[768,768]{1,0:T(8,128)(2,1)S(1)}, bf16[768,768]{1,0:T(8,128)(2,1)}, u32[]{:S(2)}) copy-start(bf16[768,768]{1,0:T(8,128)(2,1)} %refs_11_.1) | copy-start | bytes 3538948
  80.0 30.7 %copy-start.1 = (bf16[768,768]{1,0:T(8,128)(2,1)S(1)}, bf16[768,768]{1,0:T(8,128)(2,1)}, u32[]{:S(2)}) copy-start(bf16[768,768]{1,0:T(8,128)(2,1)} %refs_12_.1) | copy-start | bytes 3538948
  80.0 30.7 %copy-start.2 = (bf16[768,768]{1,0:T(8,128)(2,1)S(1)}, bf16[768,768]{1,0:T(8,128)(2,1)}, u32[]{:S(2)}) copy-start(bf16[768,768]{1,0:T(8,128)(2,1)} %refs_13_.1) | copy-start | bytes 3538948
  80.0 11.0 %collective-permute-start.4 = (bf16[512,256]{1,0:T(8,128)(2,1)S(1)}, bf16[512,256]{1,0:T(8,128)(2,1)S(1)}, u32[]{:S(2)}, u32[]{:S(2)}) collective-permute-start(bf16[512,256]{1,0:T(8,128)(2,1)S(1)} %get-tuple-element.25), channel_id=1, source_target_pairs={{0,32},{32,64},{64,96},{96,0},{1,33},{33,65},{65,97},{97,1},{2,34}... | collective-permute-start | bytes 786440 | tf_op jit(solution)/shard_map/ppermute | solution.py:400
  82.0 15.1 %collective-permute-start.1 = (bf16[528,512]{1,0:T(8,128)(2,1)S(1)}, bf16[528,512]{1,0:T(8,128)(2,1)S(1)}, u32[]{:S(2)}, u32[]{:S(2)}) collective-permute-start(bf16[528,512]{1,0:T(8,128)(2,1)S(1)} %copy-done.6), channel_id=1, source_target_pairs={{32,0},{64,32},{96,64},{0,96},{33,1},{65,33},{97,65},{1,97},{34,2}... | collective-permute-start | bytes 1622024 | tf_op jit(solution)/shard_map/ppermute | solution.py:400
  84.2 18.5 %collective-permute-start.5 = (bf16[512,256]{1,0:T(8,128)(2,1)S(1)}, bf16[512,256]{1,0:T(8,128)(2,1)S(1)}, u32[]{:S(2)}, u32[]{:S(2)}) collective-permute-start(bf16[512,256]{1,0:T(8,128)(2,1)S(1)} %get-tuple-element.26), channel_id=1, source_target_pairs={{32,0},{64,32},{96,64},{0,96},{33,1},{65,33},{97,65},{1,97},{34,2}... | collective-permute-start | bytes 786440 | tf_op jit(solution)/shard_map/ppermute | solution.py:400
  91.0 18.2 %collective-permute-start.6 = (bf16[256,256]{1,0:T(8,128)(2,1)S(1)}, bf16[256,256]{1,0:T(8,128)(2,1)S(1)}, u32[]{:S(2)}, u32[]{:S(2)}) collective-permute-start(bf16[256,256]{1,0:T(8,128)(2,1)S(1)} %add_convert_fusion.3), channel_id=1, source_target_pairs={{0,32},{32,64},{64,96},{96,0},{1,33},{33,65},{65,97},{97,1},{2,34}... | collective-permute-start | bytes 393224 | tf_op jit(solution)/shard_map/ppermute | solution.py:400
  91.3 19.5 %collective-permute-start.2 = (bf16[264,512]{1,0:T(8,128)(2,1)S(1)}, bf16[264,512]{1,0:T(8,128)(2,1)S(1)}, u32[]{:S(2)}, u32[]{:S(2)}) collective-permute-start(bf16[264,512]{1,0:T(8,128)(2,1)S(1)} %add_convert_fusion.1), channel_id=1, source_target_pairs={{0,32},{32,64},{64,96},{96,0},{1,33},{33,65},{65,97},{97,1},{2,34}... | collective-permute-start | bytes 811016 | tf_op jit(solution)/shard_map/ppermute | solution.py:400
  97.2 13.5 %collective-permute-start.3 = (bf16[264,512]{1,0:T(8,128)(2,1)S(1)}, bf16[264,512]{1,0:T(8,128)(2,1)S(1)}, u32[]{:S(2)}, u32[]{:S(2)}) collective-permute-start(bf16[264,512]{1,0:T(8,128)(2,1)S(1)} %add_convert_fusion), channel_id=1, source_target_pairs={{32,0},{64,32},{96,64},{0,96},{33,1},{65,33},{97,65},{1,97},{34,2}... | collective-permute-start | bytes 811016 | tf_op jit(solution)/shard_map/ppermute | solution.py:400
  102.8 7.9 %collective-permute-start.7 = (bf16[256,256]{1,0:T(8,128)(2,1)S(1)}, bf16[256,256]{1,0:T(8,128)(2,1)S(1)}, u32[]{:S(2)}, u32[]{:S(2)}) collective-permute-start(bf16[256,256]{1,0:T(8,128)(2,1)S(1)} %add_convert_fusion.2), channel_id=1, source_target_pairs={{32,0},{64,32},{96,64},{0,96},{33,1},{65,33},{97,65},{1,97},{34,2}... | collective-permute-start | bytes 393224 | tf_op jit(solution)/shard_map/ppermute | solution.py:400
  110.7 10.1 %slice-start = ((s8[4718592]{0:T(1024)(128)(4,1)}), s8[4194304]{0:T(1024)(128)(4,1)S(1)}, s32[]{:S(2)}) async-start(s8[4718592]{0:T(1024)(128)(4,1)} %bitcast.13), calls=%async_computation.2 | async-start | bytes 8388608
  110.8 10.1 %slice-start.1 = ((s8[4718592]{0:T(1024)(128)(4,1)}), s8[524288]{0:T(1024)(128)(4,1)S(1)}, s32[]{:S(2)}) async-start(s8[4718592]{0:T(1024)(128)(4,1)} %bitcast.13), calls=%async_computation.3 | async-start | bytes 1048576
  113.3 9.5 %collective-permute-start.8 = (bf16[32,1536]{1,0:T(8,128)(2,1)S(1)}, bf16[32,1536]{1,0:T(8,128)(2,1)S(1)}, u32[]{:S(2)}, u32[]{:S(2)}) collective-permute-start(bf16[32,1536]{1,0:T(8,128)(2,1)S(1)} %pad_maximum_fusion), channel_id=1, source_target_pairs={{0,1},{1,2},{2,3},{3,4},{4,5},{5,6},{6,7},{7,8},{8,9},{9,10},{10,1... | collective-permute-start | bytes 294920 | tf_op jit(solution)/shard_map/ppermute | solution.py:448
  113.4 9.7 %slice-start.2 = ((s8[4718592]{0:T(1024)(128)(4,1)}), s8[4194304]{0:T(1024)(128)(4,1)S(1)}, s32[]{:S(2)}) async-start(s8[4718592]{0:T(1024)(128)(4,1)} %bitcast.15), calls=%async_computation.4 | async-start | bytes 8388608
  113.4 9.7 %slice-start.3 = ((s8[4718592]{0:T(1024)(128)(4,1)}), s8[524288]{0:T(1024)(128)(4,1)S(1)}, s32[]{:S(2)}) async-start(s8[4718592]{0:T(1024)(128)(4,1)} %bitcast.15), calls=%async_computation.5 | async-start | bytes 1048576
  113.4 9.7 %copy-start.3 = (bf16[768,768]{1,0:T(8,128)(2,1)S(1)}, bf16[768,768]{1,0:T(8,128)(2,1)}, u32[]{:S(2)}) copy-start(bf16[768,768]{1,0:T(8,128)(2,1)} %wout_ref.1) | copy-start | bytes 3538948
  113.4 9.6 %collective-permute-start.9 = (bf16[32,1536]{1,0:T(8,128)(2,1)S(1)}, bf16[32,1536]{1,0:T(8,128)(2,1)S(1)}, u32[]{:S(2)}, u32[]{:S(2)}) collective-permute-start(bf16[32,1536]{1,0:T(8,128)(2,1)S(1)} %pad_maximum_fusion.1), channel_id=1, source_target_pairs={{1,0},{2,1},{3,2},{4,3},{5,4},{6,5},{7,6},{8,7},{9,8},{10,9},{11,1... | collective-permute-start | bytes 294920 | tf_op jit(solution)/shard_map/ppermute | solution.py:449
